TPU v7x, 32 devices: a whole 2x2x4 slice. The times are simulated.
32 devices in a mesh: seq: 8 (over z, x), grp: 4 (over y, core).
Axes of the slice: x: 2, y: 2, z: 4, core: 2. Of those that a mesh axis runs over, the one named last changes fastest.
Arguments:
- tokens: bfloat16 [16, 2048, 1024], P('seq', 'grp'), may hold values from -6 to 6
- segments: int32 [16, 2048], P('seq'), may hold values from 0 to 3, never falling along the last dimension, each value on 1 to 1024 neighbouring positions
- routed: int32 [16, 256], P('seq'), may hold values from 0 to 2047, as said below
- qkv_weight: bfloat16 [1024, 3072], P(('seq', 'grp')), may hold values from -0.1875 to 0.1875
- out_weight: bfloat16 [1024, 1024], P(('seq', 'grp')), may hold values from -0.75 to 0.75
- up_weight: bfloat16 [1024, 4096], P(('seq', 'grp')), may hold values from -0.1875 to 0.1875
- down_weight: bfloat16 [4096, 1024], P(('seq', 'grp')), may hold values from -0.09375 to 0.09375
- attn_gain: bfloat16 [1024], P(('seq', 'grp')), may hold values from 0.5 to 1.5
- mlp_gain: bfloat16 [1024], P(('seq', 'grp')), may hold values from 0.5 to 1.5
- router_weight: bfloat16 [1024], P(('seq', 'grp')), may hold values from -0.1875 to 0.1875
- cotangent: bfloat16 [16, 2048, 1024], P('seq', 'grp'), may hold values from -6 to 6
Outputs:
- mixed: bfloat16 [16, 2048, 1024], P('seq', 'grp')
- input_grad: bfloat16 [16, 2048, 1024], P('seq', 'grp')
- qkv_grad: float32 [1024, 3072], P(('seq', 'grp'))
- out_grad: float32 [1024, 1024], P(('seq', 'grp'))
- up_grad: float32 [1024, 4096], P(('seq', 'grp'))
- down_grad: float32 [4096, 1024], P(('seq', 'grp'))
- attn_gain_grad: float32 [1024], P(('seq', 'grp'))
- mlp_gain_grad: float32 [1024], P(('seq', 'grp'))
- router_grad: float32 [1024], P(('seq', 'grp'))
Inputs may be any that keep to these rules, and one draw needn't show every extreme that they name: Each sequence's 256 routed positions are distinct and ascending. In the aligned blocks of 512 positions (positions 0 to 511, and so on) at most 128 routed positions lie in one block, and in every sequence some block holds exactly 128.
All inputs are finite; a program needn't handle non-finite values.
Results may differ from a plain program's by a relative error of at most 0.01.
Values may be sent and summed in bfloat16 or wider, within the bound.
No kernel may reach another device: no remote copies, remote signals or barrier semaphores. Data moves between devices by JAX's collectives and lax.ppermute only.
A program may use at most 256 MiB of HBM per device.

v0:
```python
import jax
import jax.numpy as jnp
from jax import lax
from jax.experimental import pallas as pl
from jax.experimental.pallas import tpu as pltpu
from jax.sharding import PartitionSpec as P

HEAD_DIM = 64
SEG_COUNT = 4
BLOCKS = 8
epsilon = 1e-06
masked = -1e30
f32 = jnp.float32
bf16 = jnp.bfloat16
gelu_scale = 0.7978845608028654
gelu_cubic = 0.044715

NN = (((1,), (0,)), ((), ()))
NT = (((1,), (1,)), ((), ()))
TN = (((0,), (0,)), ((), ()))


def mm(a, b, dims=NN):
    return lax.dot_general(a, b, dims, preferred_element_type=f32)


VM = pl.BlockSpec(memory_space=pltpu.VMEM)
SM = pl.BlockSpec(memory_space=pltpu.SMEM)
MIB = 1024 * 1024


def call(
    body, args, outs, scratch=(), smem=0, flops=0, name=None, limit=8, keep=True, keep_out=True,
    cold=(),
):
    moved = sum(a.size * a.dtype.itemsize for a in args)
    moved += sum(o.size * o.dtype.itemsize for o in outs)
    if keep:
        args = tuple(
            a
            if n < smem
            else pltpu.with_memory_space_constraint(a, pltpu.HBM if n in cold else pltpu.VMEM)
            for n, a in enumerate(args)
        )
    if keep and keep_out:
        shapes = tuple(pltpu.VMEM(o.shape, o.dtype) for o in outs)
    else:
        shapes = tuple(outs)
    return pl.pallas_call(
        body,
        out_shape=shapes,
        in_specs=[SM] * smem + [VM] * (len(args) - smem),
        out_specs=tuple([VM] * len(outs)),
        scratch_shapes=list(scratch),
        cost_estimate=pl.CostEstimate(flops=flops, bytes_accessed=moved, transcendentals=0),
        compiler_params=pltpu.CompilerParams(vmem_limit_bytes=limit * MIB),
        name=name,
    )(*args)


def out(shape, dtype):
    return jax.ShapeDtypeStruct(shape, dtype)


def pick_body(meta, pos_ref, src_ref, own_ref, oth_ref):
    rows, span = pos_ref.shape[1], src_ref.shape[1]
    core, base = meta[0], meta[1]
    lane = lax.broadcasted_iota(jnp.int32, (rows, span), 1) + base
    for half, ref in ((0, own_ref), (1, oth_ref)):
        seq = core if half == 0 else 1 - core
        hot = jnp.where(pos_ref[half] == lane, 1.0, 0.0).astype(bf16)
        src = src_ref[seq]
        ref[...] = mm(hot, src).astype(bf16)


def place_body(meta, pos_ref, base_ref, own_ref, oth_ref, out_ref):
    rows, span = pos_ref.shape[2], base_ref.shape[1]
    core, base = meta[0], meta[1]
    row = lax.broadcasted_iota(jnp.int32, (span, rows), 0) + base
    for half, ref in ((0, own_ref), (1, oth_ref)):
        seq = core if half == 0 else 1 - core
        hot = jnp.where(pos_ref[half] == row, 1.0, 0.0).astype(bf16)
        added = mm(hot, ref[...])
        out_ref[seq] = (base_ref[seq].astype(f32) + added).astype(bf16)


def attn_fwd_body(
    idx, xo_ref, xt_ref, segc_ref, segr_ref, *refs
):
    packs = refs[:BLOCKS]
    a_ref, qkv_ref, p_ref, o_ref, bo_ref, bt_ref, wq_ref, wo_ref, gr_ref, r_ref, gcol = refs[BLOCKS:]
    rows, width = xo_ref.shape
    part = width // 4
    qcols = 3 * part
    blk = width // BLOCKS
    ob = part // BLOCKS
    for b, pk in enumerate(packs):
        s = idx[b]
        off = pl.multiple_of(s * blk, blk)
        wq_ref[pl.ds(off, blk), :] = pk[:, :qcols]
        gcol[pl.ds(off, blk), :] = pk[:, qcols : qcols + 128]
        off2 = pl.multiple_of(s * ob, ob)
        for j in range(4):
            wo_ref[pl.ds(off2, ob), j * part : (j + 1) * part] = pk[
                j * ob : (j + 1) * ob, qcols + 128 :
            ]
    eye = (
        lax.broadcasted_iota(jnp.int32, (8, 128), 0) == lax.broadcasted_iota(jnp.int32, (8, 128), 1)
    ).astype(f32).astype(bf16)
    gr = mm(eye, gcol[...], NT)
    gr_ref[...] = gr
    gain = gr[0:1]
    for half, x_ref in ((0, xo_ref), (1, xt_ref)):
        span = pl.ds(half * rows, rows)
        xb = x_ref[...]
        x = xb.astype(f32)
        scale = lax.rsqrt(jnp.mean(x * x, axis=-1, keepdims=True) + epsilon)
        a_ref[span, :] = (x * scale * gain).astype(bf16)
        r_ref[span, :] = mm(xb, gcol[...])

    def project(i, carry):
        cols = pl.ds(pl.multiple_of(i * part, part), part)
        qkv_ref[:, cols] = mm(a_ref[...], wq_ref[:, cols]).astype(bf16)
        return carry

    lax.fori_loop(0, 3, project, 0)
    ri = lax.broadcasted_iota(jnp.int32, (rows, rows), 0)
    ci = lax.broadcasted_iota(jnp.int32, (rows, rows), 1)
    causal = ci <= ri
    heads = part // HEAD_DIM
    score_scale = HEAD_DIM ** (-0.5)
    for half in range(2):
        allowed = causal & (segc_ref[half] == segr_ref[half])
        span = pl.ds(half * rows, rows)
        for h in range(heads):
            q = qkv_ref[span, h * HEAD_DIM : (h + 1) * HEAD_DIM]
            k = qkv_ref[span, part + h * HEAD_DIM : part + (h + 1) * HEAD_DIM]
            v = qkv_ref[span, 2 * part + h * HEAD_DIM : 2 * part + (h + 1) * HEAD_DIM]
            logits = jnp.where(allowed, mm(q, k, NT) * score_scale, masked)
            e = jnp.exp(logits - jnp.max(logits, axis=-1, keepdims=True))
            p = e / jnp.sum(e, axis=-1, keepdims=True)
            p_ref[half * heads + h] = p
            o_ref[span, h * HEAD_DIM : (h + 1) * HEAD_DIM] = mm(p.astype(bf16), v).astype(bf16)

    def project_out(i, carry):
        cols = pl.ds(pl.multiple_of(i * part, part), part)
        res = mm(o_ref[...], wo_ref[:, cols]).astype(bf16)
        bo_ref[:, cols] = res[:rows]
        bt_ref[:, cols] = res[rows:]
        return carry

    lax.fori_loop(0, 4, project_out, 0)


def norm_body(t_ref, u_ref, x_ref, gr_ref, m_ref):
    h = x_ref[...].astype(f32) + (t_ref[...].astype(f32) + u_ref[...].astype(f32))
    scale = lax.rsqrt(jnp.mean(h * h, axis=-1, keepdims=True) + epsilon)
    m_ref[...] = (h * scale * gr_ref[1:2]).astype(bf16)


def turn_body(a_ref, o_ref, at_ref, ot_ref):
    tile = 256

    def step(i, carry):
        cols = pl.ds(pl.multiple_of(i * tile, tile), tile)
        at_ref[cols, :] = a_ref[:, cols].T
        return carry

    lax.fori_loop(0, a_ref.shape[1] // tile, step, 0)
    ot_ref[...] = o_ref[...].T


def mlp_body(idx, mo_ref, mt_ref, co_ref, ct_ref, r_ref, *refs):
    packs, rest = refs[:BLOCKS], refs[BLOCKS:]
    g_ref, du_ref, db_ref, wu_ref, wd_ref, dmo_ref, dmt_ref = rest
    rows, width = mo_ref.shape
    units = wu_ref.shape[1]
    blk, sub = width // BLOCKS, units // BLOCKS
    for b in range(BLOCKS):
        wu_ref[pl.ds(pl.multiple_of(idx[b] * blk, blk), blk), :] = packs[b][:, :units]
        wd_ref[pl.ds(pl.multiple_of(idx[b] * sub, sub), sub), :] = packs[b][:, units:]
    r = r_ref[:, 2:3]
    db_ref[:rows, :] = (r[:rows] * co_ref[...].astype(f32)).astype(bf16)
    db_ref[rows:, :] = (r[rows:] * ct_ref[...].astype(f32)).astype(bf16)
    tile = 256

    def step(i, carry):
        cols = pl.ds(pl.multiple_of(i * tile, tile), tile)
        for half, m_ref in ((0, mo_ref), (1, mt_ref)):
            span = pl.ds(half * rows, rows)
            u = mm(m_ref[...], wu_ref[:, cols])
            u2 = u * u
            th = jnp.tanh(gelu_scale * (u + gelu_cubic * (u2 * u)))
            half_up = 0.5 * (1.0 + th)
            g_ref[span, cols] = (u * half_up).astype(bf16)
            slope = half_up + (0.5 * u) * (1.0 - th * th) * (
                gelu_scale * (1.0 + 3.0 * gelu_cubic * u2)
            )
            dg = mm(db_ref[span, :], wd_ref[cols, :], NT)
            du_ref[span, cols] = (dg * slope).astype(bf16)
        return carry

    lax.fori_loop(0, units // tile, step, 0)

    def step2(i, carry):
        cols = pl.ds(pl.multiple_of(i * tile, tile), tile)
        dm = mm(du_ref[...], wu_ref[cols, :], NT).astype(bf16)
        dmo_ref[:, cols] = dm[:rows]
        dmt_ref[:, cols] = dm[rows:]
        return carry

    lax.fori_loop(0, width // tile, step2, 0)


def up_grad_body(idx, du_ref, mo_ref, mt_ref, wu_ref, gcol, *refs):
    col_ref, ups, (flip,) = refs[0], refs[1 : 1 + BLOCKS], refs[1 + BLOCKS :]
    rows, width = mo_ref.shape
    blk = width // BLOCKS
    tile = 256

    def step(i, carry):
        cols = pl.ds(pl.multiple_of(i * tile, tile), tile)
        flip[cols, :rows] = mo_ref[:, cols].T
        flip[cols, rows:] = mt_ref[:, cols].T
        return carry

    lax.fori_loop(0, width // tile, step, 0)
    for b, ref in enumerate(ups):
        off = pl.ds(pl.multiple_of(idx[b] * blk, blk), blk)
        grad = mm(flip[off, :], du_ref[...])
        ref[...] = grad.astype(bf16)
        gain = jnp.sum(grad * wu_ref[off, :].astype(f32), axis=-1, keepdims=True)
        gain = gain / gcol[off, 1:2].astype(f32)
        col_ref[off, :] = jnp.broadcast_to(gain, (blk, 128))


def down_grad_body(
    idx, g_ref, db_ref, wd_ref, col_in, ao_ref, at_ref, co_ref, ct_ref, xo_ref, xt_ref, *refs
):
    bo_ref, bt_ref, col_ref = refs[:3]
    downs, (flip,) = refs[3 : 3 + BLOCKS], refs[3 + BLOCKS :]
    rows, width = bo_ref.shape
    units = wd_ref.shape[0]
    sub = units // BLOCKS
    tile = 256

    def step(i, carry):
        cols = pl.ds(pl.multiple_of(i * tile, tile), tile)
        res = mm(g_ref[...], wd_ref[:, cols])
        bo_ref[:, cols] = res[:rows].astype(bf16)
        bt_ref[:, cols] = res[rows:].astype(bf16)
        flip[cols, :] = g_ref[:, cols].T
        own, other = carry
        own += jnp.sum(
            (res[:rows] + ao_ref[:, cols].astype(f32)) * co_ref[:, cols].astype(f32),
            axis=-1, keepdims=True,
        )
        other += jnp.sum(
            (res[rows:] + at_ref[:, cols].astype(f32)) * ct_ref[:, cols].astype(f32),
            axis=-1, keepdims=True,
        )
        return own, other

    zero = jnp.zeros((rows, 1), f32)
    dots = lax.fori_loop(0, width // tile, step, (zero, zero))
    for b, ref in enumerate(downs):
        off = pl.multiple_of(idx[b] * sub, sub)
        ref[...] = mm(flip[pl.ds(off, sub), :], db_ref[...]).astype(bf16)
    lane = lax.broadcasted_iota(jnp.int32, (rows, 128), 1)
    route = jnp.zeros((width, 128), f32)
    for d, x_ref in zip(dots, (xo_ref, xt_ref)):
        high = d.astype(bf16).astype(f32)
        two = jnp.where(lane == 0, high, jnp.where(lane == 1, d - high, 0.0)).astype(bf16)
        route += mm(x_ref[...], two, TN)
    total = jnp.sum(route[:, :2], axis=-1, keepdims=True)
    wide = lax.broadcasted_iota(jnp.int32, (width, 128), 1)
    col_ref[...] = jnp.where(wide == 1, col_in[...], jnp.where(wide == 2, total, 0.0))


def hidden_grad_body(dt_ref, du_ref, bt_ref, bu_ref, x_ref, c_ref, r_ref, gr_ref, da_ref, dh_ref):
    dm = dt_ref[...].astype(f32) + du_ref[...].astype(f32)
    h = x_ref[...].astype(f32) + (bt_ref[...].astype(f32) + bu_ref[...].astype(f32))
    rows = h.shape[0]
    n = lax.rsqrt(jnp.mean(h * h, axis=-1, keepdims=True) + epsilon)
    t = dm * gr_ref[1:2]
    dh = n * t - h * (n * n * n) * jnp.mean(t * h, axis=-1, keepdims=True)
    dh_ref[...] = dh
    de = r_ref[:rows, 2:3] * c_ref[...].astype(f32)
    da_ref[...] = (de + dh).astype(bf16)


def result_body(at_ref, au_ref, mt_ref, mu_ref, c_ref, r_ref, e_ref, dr_ref):
    branch = (at_ref[...].astype(f32) + au_ref[...].astype(f32)) + (
        mt_ref[...].astype(f32) + mu_ref[...].astype(f32)
    )
    rows = branch.shape[0]
    e_ref[...] = (r_ref[:rows, 2:3] * branch).astype(bf16)
    dr = jnp.sum(c_ref[...].astype(f32) * branch, axis=-1, keepdims=True)
    dr_ref[...] = jnp.broadcast_to(dr, dr_ref.shape)


def attn_bwd_body(
    idx, at_ref, ot_ref, qkv_ref, p_ref, dao_ref, dat_ref, wq_ref, wo_ref, gcol, col_ref, *refs
):
    dqkv = refs[0]
    grads = refs[1 : 1 + BLOCKS]
    (da,) = refs[1 + BLOCKS :]
    rows, width = dao_ref.shape
    part = width // 4
    qcols = 3 * part
    heads = part // HEAD_DIM
    score_scale = HEAD_DIM ** (-0.5)
    da[:rows, :] = dao_ref[...]
    da[rows:, :] = dat_ref[...]
    for half in range(2):
        span = pl.ds(half * rows, rows)
        dmix = mm(da[span, :], wo_ref[...], NT).astype(bf16)
        for h in range(heads):
            lo, hi = h * HEAD_DIM, (h + 1) * HEAD_DIM
            q = qkv_ref[span, lo:hi]
            k = qkv_ref[span, part + lo : part + hi]
            v = qkv_ref[span, 2 * part + lo : 2 * part + hi]
            do = dmix[:, lo:hi]
            p = p_ref[half * heads + h]
            dp = mm(do, v, NT)
            ds = (p * (dp - jnp.sum(p * dp, axis=-1, keepdims=True))).astype(bf16)
            dqkv[span, lo:hi] = (mm(ds, k) * score_scale).astype(bf16)
            dqkv[span, part + lo : part + hi] = (mm(ds, q, TN) * score_scale).astype(bf16)
            dqkv[span, 2 * part + lo : 2 * part + hi] = mm(p.astype(bf16), do, TN).astype(bf16)
    blk = width // BLOCKS
    ob = part // BLOCKS
    lane = lax.broadcasted_iota(jnp.int32, (blk, 128), 1)
    for b, ref in enumerate(grads):
        s = idx[b]
        off = pl.ds(pl.multiple_of(s * blk, blk), blk)
        grad = mm(at_ref[off, :], dqkv[...])
        ref[:, :qcols] = grad.astype(bf16)
        gain = jnp.sum(grad * wq_ref[off, :].astype(f32), axis=-1, keepdims=True)
        gain = gain / gcol[off, 0:1].astype(f32)
        ref[:, qcols : qcols + 128] = jnp.where(lane == 0, gain, col_ref[off, :]).astype(bf16)
        og = mm(ot_ref[pl.ds(pl.multiple_of(s * ob, ob), ob), :], da[...]).astype(bf16)
        for j in range(4):
            ref[j * ob : (j + 1) * ob, qcols + 128 :] = og[:, j * part : (j + 1) * part]


def normed_grad_body(dqkv_ref, wq_ref, do_ref, dt_ref):
    rows, width = do_ref.shape
    tile = 256

    def step(i, carry):
        cols = pl.ds(pl.multiple_of(i * tile, tile), tile)
        d = mm(dqkv_ref[...], wq_ref[cols, :], NT).astype(bf16)
        do_ref[:, cols] = d[:rows]
        dt_ref[:, cols] = d[rows:]
        return carry

    lax.fori_loop(0, width // tile, step, 0)


def input_grad_body(t_ref, u_ref, x_ref, dh_ref, dr_ref, gr_ref, dx_ref):
    d = t_ref[...].astype(f32) + u_ref[...].astype(f32)
    x = x_ref[...].astype(f32)
    m = lax.rsqrt(jnp.mean(x * x, axis=-1, keepdims=True) + epsilon)
    s = d * gr_ref[0:1]
    dxn = m * s - x * (m * m * m) * jnp.mean(s * x, axis=-1, keepdims=True)
    dx_ref[...] = (dxn + dh_ref[...] + dr_ref[:, 0:1] * gr_ref[2:3]).astype(bf16)


HEAD_OF = (0, 2, 1, 3)


def pack_body(meta, qkv_ref, up_ref, gains_ref, *refs):
    outs, (tmp,) = refs[:4], refs[4:]
    width, units = qkv_ref.shape[1] // 3, up_ref.shape[1]
    part = width // 4
    sub = units // (4 * BLOCKS)
    for j in range(4):
        p = HEAD_OF[j]
        for t in range(3):
            for z in range(4):
                src = t * width + (4 * z + p) * HEAD_DIM
                dst = t * part + z * HEAD_DIM
                tmp[j, :, dst : dst + HEAD_DIM] = qkv_ref[:, src : src + HEAD_DIM]
        tmp[j, :, 3 * part : 3 * part + 128] = gains_ref[...]
        for s in range(BLOCKS):
            dst = 3 * part + 128 + s * sub
            src = (4 * s + j) * sub
            tmp[j, :, dst : dst + sub] = up_ref[:, src : src + sub]
    for k, ref in enumerate(outs):
        ref[...] = tmp[meta[3] ^ k]


def join_body(meta, c0, c1, c2, c3, own_ref, moved_ref, down_ref, attn_ref, mlp_ref):
    mine, width = own_ref.shape
    part = width // 4
    head = 3 * part + 128
    for k, ref in enumerate((c0, c1, c2, c3)):
        off = pl.ds(pl.multiple_of((meta[3] ^ k) * mine, mine), mine)
        attn_ref[off, :head] = ref[:, :head]
        mlp_ref[off, : mlp_ref.shape[1] - width] = ref[:, head:]
    mlp_ref[:, mlp_ref.shape[1] - width :] = down_ref[...]
    take = jnp.full(own_ref.shape, meta[4]) == 1
    rows = jnp.where(take, moved_ref[...].astype(f32), own_ref[...].astype(f32)).astype(bf16)
    for j in range(4):
        attn_ref[j * mine : (j + 1) * mine, head:] = rows[:, j * part : (j + 1) * part]


def split_attn_body(meta, a_ref, b_ref, c_ref, c0, c1, c2, c3, out_ref, tmp):
    mine, width = out_ref.shape
    part = width // 4
    head = 3 * part + 128
    tmp[...] = (a_ref[...].astype(f32) + b_ref[...].astype(f32)) + c_ref[...].astype(f32)
    for k, ref in enumerate((c0, c1, c2, c3)):
        off = pl.ds(pl.multiple_of((meta[3] ^ k) * mine, mine), mine)
        ref[...] = tmp[off, :head].astype(ref.dtype)
    for j in range(4):
        out_ref[:, j * part : (j + 1) * part] = tmp[j * mine : (j + 1) * mine, head:]


def split_up_body(meta, a_ref, b_ref, c_ref, c0, c1, c2, c3, tmp):
    mine = c0.shape[0]
    tmp[...] = (a_ref[...].astype(f32) + b_ref[...].astype(f32)) + c_ref[...].astype(f32)
    for k, ref in enumerate((c0, c1, c2, c3)):
        off = pl.ds(pl.multiple_of((meta[3] ^ k) * mine, mine), mine)
        ref[...] = tmp[off, :].astype(ref.dtype)


def final_attn_body(meta, c0, c1, c2, c3, out_ref, small_ref, tmp):
    mine = out_ref.shape[0]
    width = out_ref.shape[1] // 3
    part = width // 4
    for k, ref in enumerate((c0, c1, c2, c3)):
        tmp[meta[3] ^ k] = ref[...].astype(f32)
    for j in range(4):
        for t in range(3):
            for z in range(4):
                dst = t * width + (4 * z + HEAD_OF[j]) * HEAD_DIM
                src = t * part + z * HEAD_DIM
                out_ref[:, dst : dst + HEAD_DIM] = tmp[j, :, src : src + HEAD_DIM]
    head = slice(3 * part, 3 * part + 128)
    small = (tmp[0, :, head] + tmp[1, :, head]) + (tmp[2, :, head] + tmp[3, :, head])
    wide = jnp.concatenate([small, jnp.zeros((128 - mine, 128), f32)], axis=0)
    small_ref[...] = wide.T[:8]


def final_up_body(meta, c0, c1, c2, c3, out_ref, tmp):
    sub = out_ref.shape[1] // (4 * BLOCKS)
    for k, ref in enumerate((c0, c1, c2, c3)):
        tmp[meta[3] ^ k] = ref[...].astype(f32)
    for j in range(4):
        for s in range(BLOCKS):
            dst = (4 * s + j) * sub
            out_ref[:, dst : dst + sub] = tmp[j, :, s * sub : (s + 1) * sub]


def flip_bit(v, axis, size, mask):
    return lax.ppermute(v, axis, [(i, i ^ mask) for i in range(size)])


def swap_core(v):
    return flip_bit(v, "grp", 4, 1)


def swap_pair(v):
    return flip_bit(v, "grp", 4, 2)


def swap_side(v, seqs):
    return flip_bit(v, "seq", seqs, 1)


def ring(v, seqs):
    return lax.ppermute(v, "seq", [(i, (i + 2) % seqs) for i in range(seqs)])


def reorder(parts, member):
    low = (member & 1) == 1
    high = (member & 2) == 2
    res = []
    for j in range(4):
        straight = jnp.where(low, parts[j ^ 1], parts[j])
        crossed = jnp.where(low, parts[j ^ 3], parts[j ^ 2])
        res.append(jnp.where(high, crossed, straight))
    return res


def exchange(chunks, member):
    rel = reorder(chunks, member)
    got = [rel[0]] + [flip_bit(rel[k], "grp", 4, k) for k in range(1, 4)]
    return reorder(got, member)


def native_gather(pack):
    full = lax.all_gather(pack, "seq", axis=0, tiled=True)
    return list(full.reshape((BLOCKS, -1) + full.shape[1:]))


def native_scatter(blocks):
    full = jnp.concatenate(blocks, axis=0)
    return lax.psum_scatter(full.astype(f32), "seq", scatter_dimension=0, tiled=True)


def add(*parts):
    total = parts[0].astype(f32)
    for p in parts[1:]:
        total = total + p.astype(f32)
    return total.astype(bf16)


class Flow:
    def __init__(self):
        self.v = {}

    def __getitem__(self, name):
        return self.v[name]

    def __setitem__(self, name, value):
        self.v[name] = value

    def order(self, value, name):
        token = lax.create_token()
        token, self.v[name] = lax.optimization_barrier((token, self.v[name]))
        return lax.optimization_barrier((token, value))[1]

    def sync(self, *names):
        held = [n for n in names if n in self.v]
        done = lax.optimization_barrier(tuple(self.v[n] for n in held))
        for n, value in zip(held, done):
            self.v[n] = value


def on_device(
    tokens,
    segments,
    routed,
    qkv_weight,
    out_weight,
    up_weight,
    down_weight,
    attn_gain,
    mlp_gain,
    router_weight,
    cotangent,
):
    groups, seqs = lax.axis_size("grp"), lax.axis_size("seq")
    member, place = lax.axis_index("grp"), lax.axis_index("seq")
    seq_dev, span, width = tokens.shape
    rows = routed.shape[1]
    units = down_weight.shape[0] * groups * seqs
    if groups != 4 or seq_dev != 2:
        raise ValueError("mesh")
    native = seqs != BLOCKS
    part, ff = width // 4, units // 4
    core, pair = member & 1, member >> 1
    mine = qkv_weight.shape[0]
    head = 3 * part + 128
    both = 2 * rows
    odd = (place ^ member) & 1
    meta = jnp.stack([core, member * span, pair, member, odd]).astype(jnp.int32)
    half = out((rows, width), bf16)
    v = Flow()

    queue = []

    def side(name, t, lag=3):
        if len(queue) >= lag:
            t = v.order(t, queue[-lag])
        queue.append(name)
        v[name] = swap_side(t, seqs)

    def turn(t):
        return ring(t, seqs)

    flip = core == 1
    pos = jnp.where(flip, routed[::-1], routed)
    starts = jnp.stack(
        [jnp.sum((segments < n).astype(jnp.int32), axis=1) for n in range(1, SEG_COUNT)], axis=0
    )
    seg = jnp.sum((routed[None] >= starts[:, :, None]).astype(jnp.int32), axis=0)
    seg = jnp.where(flip, seg[::-1], seg)
    pos_col, pos_row = pos[:, :, None], pos[:, None, :]
    seg_col, seg_row = seg[:, :, None], seg[:, None, :]

    def pick(source, name):
        return call(
            pick_body, (meta, pos_col, source), (half, half), smem=1,
            flops=4 * rows * span * width, name=name, keep=False, limit=24,
        )

    gains = jnp.stack([attn_gain, mlp_gain, router_weight], axis=1)
    gains = jnp.pad(gains, ((0, 0), (0, 125)))
    x_mine, x_send = pick(tokens, "pick_tokens")
    if native:
        qkv_view = qkv_weight.reshape(mine, 3, 4, 4, HEAD_DIM)
        chunks = [
            jnp.concatenate([qkv_view[:, :, :, p].reshape(mine, 3 * part), gains], axis=1)
            for p in HEAD_OF
        ]
        qkv_blocks = native_gather(jnp.concatenate(exchange(chunks, member), axis=0))
        out_full = lax.all_gather(out_weight, ("seq", "grp"), axis=0, tiled=True)
        out_view = out_full.reshape(4, 4, HEAD_DIM, width)
        head_set = 2 * core + pair
        out_rows = lax.dynamic_index_in_dim(out_view, head_set, 1, keepdims=False)
        out_rows = out_rows.reshape(BLOCKS, part // BLOCKS, width)
        attn_packs = [
            jnp.concatenate(
                [q, jnp.concatenate([o[:, j * part : (j + 1) * part] for j in range(4)], axis=0)],
                axis=1,
            )
            for q, o in zip(qkv_blocks, out_rows)
        ]
        up_view = up_weight.reshape(mine, seqs, 4, ff // seqs)
        chunks = [up_view[:, :, j].reshape(mine, ff) for j in range(4)]
        up_rows = jnp.concatenate(exchange(chunks, member), axis=0)
        mlp_packs = native_gather(jnp.concatenate([up_rows, down_weight], axis=1))
        order = jnp.arange(BLOCKS, dtype=jnp.int32)
        v["tx"] = add(x_mine, swap_core(x_send))
        v["yx"] = swap_pair(v["tx"])
        v["x"] = v["tx"] + v["yx"]
        v["xo"] = swap_core(v["x"])
        c_mine, c_send = pick(cotangent, "pick_cotangent")
        v["tc"] = add(c_mine, swap_core(c_send))
    else:
        order = jnp.stack(
            [((place ^ r) - 2 * k) % seqs for k in range(BLOCKS // 2) for r in range(2)]
        ).astype(jnp.int32)
        swaps = [
            (s * 4 + g, (s ^ 1) * 4 + (g ^ 1)) for s in range(seqs) for g in range(4) if (s ^ g) & 1
        ]
        chunk = out((mine, head + ff), bf16)
        chunks = call(
            pack_body, (meta, qkv_weight, up_weight, gains), (chunk,) * 4,
            scratch=[pltpu.VMEM((4, mine, head + ff), bf16)], smem=1, name="pack", cold=(1, 2, 3),
        )
        got = [chunks[0]] + [flip_bit(chunks[k], "grp", 4, k) for k in range(1, 4)]
        moved = lax.ppermute(out_weight, ("seq", "grp"), swaps)
        v["a0"], v["m0"] = call(
            join_body, (meta, *got, out_weight, moved, down_weight),
            (out((mine * 4, width + 128), bf16), out((mine * 4, ff + width), bf16)), smem=1,
            name="join", cold=(2, 3, 4, 5, 6, 7),
        )
        v["tx"] = add(x_mine, swap_core(x_send))
        v.sync("a0", "m0", "tx")
        v["a1"] = turn(v["a0"])
        v["m1"] = turn(v["m0"])
        side("xa0", v["a0"], 2)
        side("xm0", v["m0"], 2)
        v["yx"] = swap_pair(v["tx"])
        v["a2"] = turn(v["a1"])
        side("xa1", v["a1"], 2)
        v["a3"] = turn(v["a2"])
        side("xa2", v["a2"], 2)
        v["x"] = v["tx"] + v["yx"]
        v["xo"] = swap_core(v["x"])
        side("xa3", v["a3"], 2)
        v["m2"] = turn(v["m1"])
        v["m3"] = turn(v["m2"])
        side("xm1", v["m1"], 2)
        side("xm2", v["m2"], 2)
        side("xm3", v["m3"], 2)
        c_mine, c_send = pick(cotangent, "pick_cotangent")
        v["tc"] = add(c_mine, swap_core(c_send))
        v["yc"] = swap_pair(v["tc"])
        attn_names = [n + str(k) for k in range(4) for n in ("a", "xa")]
        attn_packs = [v[n] for n in attn_names]

    a, qkv, probs, mix, ba_o, ba_t, w_qkv, w_out, gain_rows, r, gain_cols = call(
        attn_fwd_body,
        (order, v["x"], v["xo"], seg_col, seg_row, *attn_packs),
        (
            out((both, width), bf16),
            out((both, 3 * part), bf16),
            out((2 * part // HEAD_DIM, rows, rows), f32),
            out((both, part), bf16),
            half,
            half,
            out((width, 3 * part), bf16),
            out((part, width), bf16),
            out((8, width), f32),
            out((both, 128), f32),
            out((width, 128), bf16),
        ),
        smem=1,
        flops=2 * both * width * width,
        name="attn_fwd",
        cold=range(1, 13),
    )
    v["a"], v["mix"] = a, mix
    v["tb"] = add(ba_o, swap_core(ba_t))
    v.sync("tb", "a", "mix")
    v["yb"] = swap_pair(v["tb"])
    if native:
        v["yc"] = swap_pair(v["tc"])
    a_turned, mix_turned = call(
        turn_body, (v["a"], v["mix"]), (out((width, both), bf16), out((part, both), bf16)),
        name="turn",
    )
    v["c"] = v["tc"] + v["yc"]
    v["co"] = swap_core(v["c"])
    v.sync("yb", "tb", "co", "c")
    (v["h"],) = call(
        norm_body, (v["tb"], v["yb"], v["x"], gain_rows), (half,), name="norm_two", cold=(0, 1, 2)
    )
    v["ho"] = swap_core(v["h"])
    if not native:
        mlp_packs = [v[n + str(k)] for k in range(4) for n in ("m", "xm")]
    g, du, db, w_up, w_down, dm_o, dm_t = call(
        mlp_body,
        (order, v["h"], v["ho"], v["c"], v["co"], r, *mlp_packs),
        (
            out((both, ff), bf16),
            out((both, ff), bf16),
            out((both, width), bf16),
            out((width, ff), bf16),
            out((ff, width), bf16),
            half,
            half,
        ),
        smem=1,
        flops=6 * both * width * ff,
        name="mlp",
        cold=(2, 3, 4, *range(6, 14)),
    )

    v["du"] = du
    v["td"] = add(dm_o, swap_core(dm_t))
    v.sync("td", "du")
    v["yd"] = swap_pair(v["td"])
    col, *up_grads = call(
        up_grad_body,
        (order, v["du"], v["h"], v["ho"], w_up, gain_cols),
        (out((width, 128), f32), *([out((width // BLOCKS, ff), bf16)] * BLOCKS)),
        scratch=[pltpu.VMEM((width, both), bf16)],
        smem=1,
        flops=2 * both * width * ff,
        name="up_grad",
        cold=(3,),
    )
    v["g"] = g
    if not native:
        for k in (1, 2, 3):
            side("xu%d" % k, up_grads[2 * k + 1])
    bm_o, bm_t, cols, *down_grads = call(
        down_grad_body,
        (
            order, v["g"], db, w_down, col, ba_o, ba_t, v["c"], v["co"], v["x"], v["xo"],
        ),
        (half, half, out((width, 128), f32), *([out((ff // BLOCKS, width), bf16)] * BLOCKS)),
        scratch=[pltpu.VMEM((ff, both), bf16)],
        smem=1,
        flops=4 * both * width * ff,
        name="down_grad",
        cold=(7, 8, 9, 10),
    )
    v["bm"], v["bn"], v["col"] = bm_o, bm_t, col
    v.sync("yd", "td", "bm")
    v["tm"] = add(v["bm"], swap_core(v["bn"]))
    da_own, dh = call(
        hidden_grad_body,
        (v["td"], v["yd"], v["tb"], v["yb"], v["x"], v["c"], r, gain_rows),
        (half, out((rows, width), f32)),
        name="hidden_grad",
        cold=range(6),
    )
    v["da"] = da_own
    v["dao"] = swap_core(da_own)

    def attention_back(v):
        dqkv, *attn_grads = call(
            attn_bwd_body,
            (
                order, a_turned, mix_turned, qkv, probs, v["da"], v["dao"], w_qkv, w_out,
                gain_cols, cols,
            ),
            (
                out((both, 3 * part), bf16),
                *([out((width // BLOCKS, width + 128), bf16)] * BLOCKS),
            ),
            scratch=[pltpu.VMEM((both, width), bf16)],
            smem=1,
            flops=3 * both * width * width,
            name="attn_bwd",
            cold=(6,),
        )
        v["dqkv"] = dqkv
        return attn_grads

    def normed_back(dqkv):
        return call(
            normed_grad_body, (dqkv, w_qkv), (half, half), flops=2 * both * width * 3 * part,
            name="normed_grad",
        )

    def give():
        return call(
            result_body,
            (v["tb"], v["yb"], v["tm"], v["ym"], v["c"], r),
            (half, out((rows, 128), f32)),
            name="result",
            cold=range(5),
        )

    def take(dr):
        return call(
            input_grad_body, (v["tx2"], v["yx2"], v["x"], dh, dr, gain_rows), (half,),
            name="input_grad", cold=range(3),
        )[0]

    def place_rows(base, own, other, name):
        return call(
            place_body, (meta, pos_row, base, own, other), (out(base.shape, bf16),), smem=1,
            flops=4 * rows * span * width, name=name, keep=False, limit=24,
        )[0]

    if native:
        attn_grads = attention_back(v)
        dx_o, dx_t = normed_back(v["dqkv"])
        v["ym"] = swap_pair(v["tm"])
        v["tx2"] = add(dx_o, swap_core(dx_t))
        v["yx2"] = swap_pair(v["tx2"])
        v["e"], dr = give()
        v["eo"] = swap_core(v["e"])
        v["dx"] = take(dr)
        v["dxo"] = swap_core(v["dx"])
    else:
        attn_grads = attention_back(v)
        v["ym"] = swap_pair(v.order(v["tm"], "dqkv"))
        v["dxm"], v["dxs"] = normed_back(v["dqkv"])
        down_grads[3] = v.order(down_grads[3], "dqkv")
        parts = {"u": up_grads, "a": attn_grads, "w": down_grads}
        up_grads[2] = v.order(up_grads[2], "dqkv")
        for n, k in (("u", 0), ("w", 1), ("a", 1), ("a", 2), ("a", 3), ("w", 2), ("w", 3), ("a", 0), ("w", 0)):
            side("x%s%d" % (n, k), parts[n][2 * k + 1])
        for n, blocks in parts.items():
            z = turn(add(blocks[2], v["x%s1" % n]))
            z = turn(add(blocks[4], v["x%s2" % n], z))
            v["z%s3" % n] = turn(add(blocks[6], v["x%s3" % n], z))
            v[n + "0"] = blocks[0]
        v["tx2"] = add(v["dxm"], swap_core(v["dxs"]))
        v["yx2"] = swap_pair(v["tx2"])
        v["e"], dr = give()
        v["eo"] = swap_core(v["e"])
        v["dx"] = take(dr)
        v["dxo"] = swap_core(v["dx"])
        piece = [out((mine, ff), f32)] + [out((mine, ff), bf16)] * 3
        cut = call(
            split_up_body, (meta, v["u0"], v["xu0"], v["zu3"]), piece,
            scratch=[pltpu.VMEM((4 * mine, ff), f32)], smem=1, name="split_up", cold=(2, 3),
        )
        cut = [cut[0]] + [flip_bit(cut[k], "grp", 4, k) for k in range(1, 4)]
        (up_grad,) = call(
            final_up_body, (meta, *cut), (out((mine, units), f32),),
            scratch=[pltpu.VMEM((4, mine, ff), f32)], smem=1, name="final_up", keep_out=False,
            cold=(2, 3, 4),
        )
        piece = [out((mine, head), f32)] + [out((mine, head), bf16)] * 3
        *cut, og = call(
            split_attn_body, (meta, v["a0"], v["xa0"], v["za3"]),
            (*piece, out((mine, width), f32)),
            scratch=[pltpu.VMEM((4 * mine, width + 128), f32)], smem=1, name="split_attn",
            cold=(2, 3),
        )
        cut = [cut[0]] + [flip_bit(cut[k], "grp", 4, k) for k in range(1, 4)]
        out_moved = lax.ppermute(og, ("seq", "grp"), swaps)
        out_grad = jnp.where(odd == 1, out_moved, og)
        down_grad = v["w0"].astype(f32) + v["xw0"].astype(f32) + v["zw3"].astype(f32)
        qkv_grad, small = call(
            final_attn_body, (meta, *cut),
            (out((mine, 3 * width), f32), out((8, 128), f32)),
            scratch=[pltpu.VMEM((4, mine, head), f32)], smem=1, name="final_attn", keep_out=False,
            cold=(2, 3, 4),
        )
        small = small[:3, :mine]

    mixed = place_rows(tokens, v["e"], v["eo"], "place_mixed")
    input_grad = place_rows(cotangent, v["dx"], v["dxo"], "place_input_grad")

    if native:
        up_sum = native_scatter(up_grads)
        down_grad = native_scatter(down_grads)
        back = exchange([up_sum[j * mine : (j + 1) * mine] for j in range(4)], member)
        up_grad = jnp.stack([b.reshape(mine, seqs, ff // seqs) for b in back], axis=2)
        up_grad = up_grad.reshape(mine, units)
        step = part // BLOCKS
        out_mine = jnp.concatenate(
            [
                jnp.concatenate([b[j * step : (j + 1) * step, head:] for j in range(4)], axis=1)
                for b in attn_grads
            ],
            axis=0,
        )
        out_mine = out_mine.astype(f32).reshape(4, 1, HEAD_DIM, width)
        slots = (jnp.arange(4) == head_set).astype(f32)[None, :, None, None]
        out_all = (out_mine * slots).reshape(width, width)
        out_grad = lax.psum_scatter(out_all, ("seq", "grp"), scatter_dimension=0, tiled=True)
        attn_sum = native_scatter([b[:, :head] for b in attn_grads])
        back = exchange([attn_sum[j * mine : (j + 1) * mine] for j in range(4)], member)
        by_head = [b[:, : 3 * part].reshape(mine, 3, 4, HEAD_DIM) for b in back]
        qkv_grad = jnp.stack([by_head[HEAD_OF.index(p)] for p in range(4)], axis=3)
        qkv_grad = qkv_grad.reshape(mine, 3 * width)
        small = sum(b[:, 3 * part : 3 * part + 3] for b in back).T
    return (
        mixed,
        input_grad,
        qkv_grad,
        out_grad,
        up_grad,
        down_grad,
        small[0],
        small[1],
        small[2],
    )


def solution(mesh):
    placed = (
        P("seq", "grp", None),
        P("seq", None),
        P("seq", None),
        P(("seq", "grp"), None),
        P(("seq", "grp"), None),
        P(("seq", "grp"), None),
        P(("seq", "grp"), None),
        P(("seq", "grp")),
        P(("seq", "grp")),
        P(("seq", "grp")),
        P("seq", "grp", None),
    )
    return jax.shard_map(
        on_device,
        mesh=mesh,
        in_specs=placed,
        out_specs=(
            P("seq", "grp", None),
            P("seq", "grp", None),
            P(("seq", "grp"), None),
            P(("seq", "grp"), None),
            P(("seq", "grp"), None),
            P(("seq", "grp"), None),
            P(("seq", "grp")),
            P(("seq", "grp")),
            P(("seq", "grp")),
        ),
        check_vma=False,
    )
```

profile of v0, /device:TPU:0, one launch (start us, length us, event | category | flops | bytes accessed | tf_op | source)
XLA Modules:
  0.0 237.1 jit_solution(8014239741224445496)
XLA Ops:
  4.0 2.1 pick_tokens.1
  8.6 3.0 %collective-permute-start.1 = (bf16[32,1920]{1,0:T(8,128)(2,1)S(1)}, bf16[32,1920]{1,0:T(8,128)(2,1)S(1)}, u32[]{:S(2)}, u32[]{:S(2)}) collective-permute-start(bf16[32,1920]{1,0:T(8,128)(2,1)S(1)} %get-tuple-element.159), channel_id=1, source_target_pairs={{0,2},{1,3},{2,0},{3,1},{4,6},{5,7},{6,4},{7,5},{8,10},{9,11},{10,... | collective-permute-start | bytes 368648 | tf_op jit(solution)/shard_map/ppermute | solution.py:457
  12.3 3.4 %collective-permute-done.1.c2 = bf16[32,1920]{1,0:T(8,128)(2,1)S(1)} collective-permute-done((bf16[32,1920]{1,0:T(8,128)(2,1)S(1)}, bf16[32,1920]{1,0:T(8,128)(2,1)S(1)}, u32[]{:S(2)}, u32[]{:S(2)}) %collective-permute-start.1) | collective-permute-done | bytes 122912 | tf_op jit(solution)/shard_map/ppermute | solution.py:457
  25.8 6.5 %collective-permute-done.8.refs_2_ = bf16[128,1152]{1,0:T(8,128)(2,1)} collective-permute-done((bf16[128,1152]{1,0:T(8,128)(2,1)S(1)}, bf16[128,1152]{1,0:T(8,128)(2,1)}, u32[]{:S(2)}, u32[]{:S(2)}) %collective-permute-start.8) | collective-permute-done | bytes 294944 | tf_op jit(solution)/shard_map/ppermute | solution.py:473
  32.4 2.1 pick_cotangent.1
  34.5 9.7 %collective-permute-done.7.refs_1_ = bf16[128,1152]{1,0:T(8,128)(2,1)S(1)} collective-permute-done((bf16[128,1152]{1,0:T(8,128)(2,1)S(1)}, bf16[128,1152]{1,0:T(8,128)(2,1)S(1)}, u32[]{:S(2)}, u32[]{:S(2)}) %collective-permute-start.7) | collective-permute-done | bytes 294944 | tf_op jit(solution)/shard_map/ppermute | solution.py:457
  50.2 2.5 %collective-permute-done.9.refs_3_ = bf16[128,1152]{1,0:T(8,128)(2,1)} collective-permute-done((bf16[128,1152]{1,0:T(8,128)(2,1)}, bf16[128,1152]{1,0:T(8,128)(2,1)}, u32[]{:S(2)}, u32[]{:S(2)}) %collective-permute-start.9) | collective-permute-done | bytes 294944 | tf_op jit(solution)/shard_map/ppermute | solution.py:457
  54.0 3.6 %collective-permute-done.13.refs_6_ = bf16[128,1152]{1,0:T(8,128)(2,1)} collective-permute-done((bf16[128,1152]{1,0:T(8,128)(2,1)}, bf16[128,1152]{1,0:T(8,128)(2,1)}, u32[]{:S(2)}, u32[]{:S(2)}) %collective-permute-start.13) | collective-permute-done | bytes 294944 | tf_op jit(solution)/shard_map/ppermute | solution.py:473
  60.6 6.1 %collective-permute-done.21.refs_2_ = bf16[128,2048]{1,0:T(8,128)(2,1)S(1)} collective-permute-done((bf16[128,2048]{1,0:T(8,128)(2,1)S(1)}, bf16[128,2048]{1,0:T(8,128)(2,1)S(1)}, u32[]{:S(2)}, u32[]{:S(2)}) %collective-permute-start.21) | collective-permute-done | bytes 524320 | tf_op jit(solution)/shard_map/ppermute | solution.py:473
  67.6 8.2 %attn_fwd.1 = (bf16[512,1024]{1,0:T(8,128)(2,1)S(1)}, bf16[512,768]{1,0:T(8,128)(2,1)S(1)}, f32[8,256,256]{2,1,0:T(8,128)S(1)}, bf16[512,256]{1,0:T(8,128)(2,1)S...) custom-call(s32[8]{0:T(128)S(1)} %stack.83.idx, ...), custom_call_target="tpu_custom_call" | custom-call | flops 1073741824 | bytes 11309088 | tf_op jit(solution)/shard_map/attn_fwd/pallas_call | solution.py:49
  77.8 2.5 %collective-permute-done.23.refs_4_ = bf16[128,2048]{1,0:T(8,128)(2,1)S(1)} collective-permute-done((bf16[128,2048]{1,0:T(8,128)(2,1)S(1)}, bf16[128,2048]{1,0:T(8,128)(2,1)S(1)}, u32[]{:S(2)}, u32[]{:S(2)}) %collective-permute-start.23) | collective-permute-done | bytes 524320 | tf_op jit(solution)/shard_map/ppermute | solution.py:473
  82.2 9.3 %collective-permute-done.22.refs_3_ = bf16[128,2048]{1,0:T(8,128)(2,1)S(1)} collective-permute-done((bf16[128,2048]{1,0:T(8,128)(2,1)S(1)}, bf16[128,2048]{1,0:T(8,128)(2,1)S(1)}, u32[]{:S(2)}, u32[]{:S(2)}) %collective-permute-start.22) | collective-permute-done | bytes 524320 | tf_op jit(solution)/shard_map/ppermute | solution.py:457
  97.0 5.8 %collective-permute-done.24.refs_5_ = bf16[128,2048]{1,0:T(8,128)(2,1)S(1)} collective-permute-done((bf16[128,2048]{1,0:T(8,128)(2,1)S(1)}, bf16[128,2048]{1,0:T(8,128)(2,1)S(1)}, u32[]{:S(2)}, u32[]{:S(2)}) %collective-permute-start.24) | collective-permute-done | bytes 524320 | tf_op jit(solution)/shard_map/ppermute | solution.py:457
  102.7 10.4 %collective-permute-done.26.refs_7_ = bf16[128,2048]{1,0:T(8,128)(2,1)S(1)} collective-permute-done((bf16[128,2048]{1,0:T(8,128)(2,1)S(1)}, bf16[128,2048]{1,0:T(8,128)(2,1)S(1)}, u32[]{:S(2)}, u32[]{:S(2)}) %collective-permute-start.26) | collective-permute-done | bytes 524320 | tf_op jit(solution)/shard_map/ppermute | solution.py:457
  114.1 8.8 %mlp.1 = (bf16[512,1024]{1,0:T(8,128)(2,1)S(1)}, bf16[512,1024]{1,0:T(8,128)(2,1)S(1)}, bf16[512,1024]{1,0:T(8,128)(2,1)S(1)}, bf16[1024,1024]{1,0:T(8,128)(2,1)...) custom-call(s32[8]{0:T(128)S(1)} %stack.83.idx, ...), custom_call_target="tpu_custom_call" | custom-call | flops 3221225472 | bytes 14942240 | tf_op jit(solution)/shard_map/mlp/pallas_call | solution.py:49
  125.7 3.2 %up_grad.1 = (f32[1024,128]{1,0:T(8,128)S(1)}, bf16[128,1024]{1,0:T(8,128)(2,1)S(1)}, bf16[128,1024]{1,0:T(8,128)(2,1)S(1)}, bf16[128,1024]{1,0:T(8,128)(2,1)S(1...) custom-call(s32[8]{0:T(128)S(1)} %stack.83.idx, ...), custom_call_target="tpu_custom_call" | custom-call | flops 1073741824 | bytes 7077920 | tf_op jit(solution)/shard_map/up_grad/pallas_call | solution.py:49
  132.0 5.5 %down_grad.1 = (bf16[256,1024]{1,0:T(8,128)(2,1)S(1)}, bf16[256,1024]{1,0:T(8,128)(2,1)S(1)}, f32[1024,128]{1,0:T(8,128)S(1)}, bf16[128,1024]{1,0:T(8,128)(2,1)S...) custom-call(s32[8]{0:T(128)S(1)} %stack.83.idx, ...), custom_call_target="tpu_custom_call" | custom-call | flops 2147483648 | bytes 11534368 | tf_op jit(solution)/shard_map/down_grad/pallas_call | solution.py:49
  139.9 2.6 %hidden_grad.1 = (bf16[256,1024]{1,0:T(8,128)(2,1)S(1)}, f32[256,1024]{1,0:T(8,128)S(1)}) custom-call(bf16[256,1024]{1,0:T(8,128)(2,1)} %copy-done.18, bf16[256,1024]{1,0:T(8,128)(2,1)} %copy-done.23, bf16[256,1024]{1,0:T(8,128)(2,1)} %copy-done.13, bf16[256,1024]{1,0:T(8,128)(2,1)} %copy-done.15, bf16[256,1024]{1,0:T(8,128)(2,1)} %copy-done.12, ...), custom_call_target="tpu_custom_call" | custom-call | bytes 5013504 | tf_op jit(solution)/shard_map/hidden_grad/pallas_call | solution.py:49
  146.2 2.2 collective-permute-done.36
  148.4 5.0 %collective-permute-done.52 = bf16[128,1024]{1,0:T(8,128)(2,1)S(1)} collective-permute-done((bf16[128,1024]{1,0:T(8,128)(2,1)S(1)}, bf16[128,1024]{1,0:T(8,128)(2,1)S(1)}, u32[]{:S(2)}, u32[]{:S(2)}) %collective-permute-start.52) | collective-permute-done | bytes 262176 | tf_op jit(solution)/shard_map/ppermute | solution.py:473
  154.6 8.2 %attn_bwd.1 = (bf16[512,768]{1,0:T(8,128)(2,1)S(1)}, bf16[128,1152]{1,0:T(8,128)(2,1)S(1)}, bf16[128,1152]{1,0:T(8,128)(2,1)}, bf16[128,1152]{1,0:T(8,128)(2,1)S...) custom-call(s32[8]{0:T(128)S(1)} %stack.83.idx, ...), custom_call_target="tpu_custom_call" | custom-call | flops 1610612736 | bytes 11272224 | tf_op jit(solution)/shard_map/attn_bwd/pallas_call | solution.py:49
  168.0 4.7 %collective-permute-done.44 = bf16[128,1152]{1,0:T(8,128)(2,1)S(1)} collective-permute-done((bf16[128,1152]{1,0:T(8,128)(2,1)S(1)}, bf16[128,1152]{1,0:T(8,128)(2,1)S(1)}, u32[]{:S(2)}, u32[]{:S(2)}) %collective-permute-start.44) | collective-permute-done | bytes 294944 | tf_op jit(solution)/shard_map/ppermute | solution.py:457
  179.6 3.8 %collective-permute-done.42 = bf16[128,1152]{1,0:T(8,128)(2,1)S(1)} collective-permute-done((bf16[128,1152]{1,0:T(8,128)(2,1)S(1)}, bf16[128,1152]{1,0:T(8,128)(2,1)S(1)}, u32[]{:S(2)}, u32[]{:S(2)}) %collective-permute-start.42) | collective-permute-done | bytes 294944 | tf_op jit(solution)/shard_map/ppermute | solution.py:457
  187.5 2.9 %result.1 = (bf16[256,1024]{1,0:T(8,128)(2,1)}, f32[256,128]{1,0:T(8,128)S(1)}) custom-call(bf16[256,1024]{1,0:T(8,128)(2,1)} %copy-done.13, bf16[256,1024]{1,0:T(8,128)(2,1)} %copy-done.15, bf16[256,1024]{1,0:T(8,128)(2,1)} %copy-done.17, bf16[256,1024]{1,0:T(8,128)(2,1)} %copy-done.22, bf16[256,1024]{1,0:T(8,128)(2,1)} %copy-done.14, ...), custom_call_target="tpu_custom_call" | custom-call | bytes 3538944 | tf_op jit(solution)/shard_map/result/pallas_call | solution.py:49
  191.0 5.9 %collective-permute-done.58 = bf16[128,1024]{1,0:T(8,128)(2,1)S(1)} collective-permute-done((bf16[128,1024]{1,0:T(8,128)(2,1)S(1)}, bf16[128,1024]{1,0:T(8,128)(2,1)S(1)}, u32[]{:S(2)}, u32[]{:S(2)}) %collective-permute-start.58) | collective-permute-done | bytes 262176 | tf_op jit(solution)/shard_map/ppermute | solution.py:457
  199.7 2.2 collective-permute-done.56.c2
  204.2 2.1 collective-permute-done.60
  207.1 3.0 %collective-permute-done.62 = bf16[128,1024]{1,0:T(8,128)(2,1)S(1)} collective-permute-done((bf16[128,1024]{1,0:T(8,128)(2,1)S(1)}, bf16[128,1024]{1,0:T(8,128)(2,1)S(1)}, u32[]{:S(2)}, u32[]{:S(2)}) %collective-permute-start.62) | collective-permute-done | bytes 262176 | tf_op jit(solution)/shard_map/ppermute | solution.py:473
  210.9 2.8 %collective-permute-done.34.u_ref = bf16[256,1024]{1,0:T(8,128)(2,1)S(1)} collective-permute-done((bf16[256,1024]{1,0:T(8,128)(2,1)S(1)}, bf16[256,1024]{1,0:T(8,128)(2,1)S(1)}, u32[]{:S(2)}, u32[]{:S(2)}) %collective-permute-start.34) | collective-permute-done | bytes 524320 | tf_op jit(solution)/shard_map/ppermute | solution.py:457
  218.7 2.0 input_grad.1.own_ref
  220.8 3.2 %place_mixed.1 = bf16[2,512,1024]{2,1,0:T(8,128)(2,1)} custom-call(s32[5]{0:T(128)S(1)} %stack.74.meta, s32[2,1,256]{2,1,0:T(1,128)S(1)} %broadcast_in_dim.14.pos_ref, bf16[2,512,1024]{2,1,0:T(8,128)(2,1)S(1)} %copy-done.1, bf16[256,1024]{1,0:T(8,128)(2,1)} %get-tuple-element.228.own_ref, bf16[256,1024]{1,0:T(8,128)(2,1)} %collective-permute-done.32.oth_ref), custom_call_target="tpu_custom_call" | custom-call | flops 536870912 | bytes 5244948 | tf_op jit(solution)/shard_map/place_mixed/pallas_call | solution.py:49
  234.5 2.6 %place_input_grad.1 = bf16[2,512,1024]{2,1,0:T(8,128)(2,1)} custom-call(s32[5]{0:T(128)S(1)} %stack.74.meta, s32[2,1,256]{2,1,0:T(1,128)S(1)} %broadcast_in_dim.14.pos_ref, bf16[2,512,1024]{2,1,0:T(8,128)(2,1)S(1)} %copy-done.3, bf16[256,1024]{1,0:T(8,128)(2,1)S(1)} %input_grad.1.own_ref, bf16[256,1024]{1,0:T(8,128)(2,1)S(1)} %collective-permute-done.35.oth_ref), custom_call_target="tpu_custom_call" | custom-call | flops 536870912 | bytes 5244948 | tf_op jit(solution)/shard_map/place_input_grad/pallas_call | solution.py:49
  (257 shorter events, 89.6 us)
Async XLA Ops:
  6.1 13.1 %collective-permute-start.4 = (bf16[256,1024]{1,0:T(8,128)(2,1)}, bf16[256,1024]{1,0:T(8,128)(2,1)}, u32[]{:S(2)}, u32[]{:S(2)}) collective-permute-start(bf16[256,1024]{1,0:T(8,128)(2,1)} %get-tuple-element.164), channel_id=1, source_target_pairs={{0,1},{1,0},{2,3},{3,2},{4,5},{5,4},{6,7},{7,6},{8,9},{9,8},{10,11... | collective-permute-start | bytes 1572872 | tf_op jit(solution)/shard_map/ppermute | solution.py:457
  22.4 25.0 %collective-permute-start.5 = (bf16[256,1024]{1,0:T(8,128)(2,1)S(1)}, bf16[256,1024]{1,0:T(8,128)(2,1)S(1)}, u32[]{:S(2)}, u32[]{:S(2)}) collective-permute-start(bf16[256,1024]{1,0:T(8,128)(2,1)S(1)} %add_convert_fusion.5), channel_id=1, source_target_pairs={{0,2},{1,3},{2,0},{3,1},{4,6},{5,7},{6,4},{7,5},{8,10},{9,11},{10,... | collective-permute-start | bytes 1572872 | tf_op jit(solution)/shard_map/ppermute | solution.py:457
  23.8 25.4 %collective-permute-start.11 = (bf16[128,2048]{1,0:T(8,128)(2,1)S(1)}, bf16[128,2048]{1,0:T(8,128)(2,1)S(1)}, u32[]{:S(2)}, u32[]{:S(2)}) collective-permute-start(bf16[128,2048]{1,0:T(8,128)(2,1)S(1)} %get-tuple-element.171.refs_0_), channel_id=1, source_target_pairs={{0,4},{4,0},{8,12},{12,8},{16,20},{20,16},{24,28},{28,24},{1,5},{5... | collective-permute-start | bytes 1572872 | tf_op jit(solution)/shard_map/ppermute | solution.py:457
  25.4 18.8 %collective-permute-start.7 = (bf16[128,1152]{1,0:T(8,128)(2,1)S(1)}, bf16[128,1152]{1,0:T(8,128)(2,1)S(1)}, u32[]{:S(2)}, u32[]{:S(2)}) collective-permute-start(bf16[128,1152]{1,0:T(8,128)(2,1)S(1)} %get-tuple-element.166.refs_0_), channel_id=1, source_target_pairs={{0,4},{4,0},{8,12},{12,8},{16,20},{20,16},{24,28},{28,24},{1,5},{5... | collective-permute-start | bytes 884744 | tf_op jit(solution)/shard_map/ppermute | solution.py:457
  32.4 13.2 %collective-permute-start.10 = (bf16[128,1152]{1,0:T(8,128)(2,1)}, bf16[128,1152]{1,0:T(8,128)(2,1)}, u32[]{:S(2)}, u32[]{:S(2)}) collective-permute-start(bf16[128,1152]{1,0:T(8,128)(2,1)} %collective-permute-done.8.refs_2_), channel_id=1, source_target_pairs={{0,8},{4,12},{8,16},{12,20},{16,24},{20,28},{24,0},{28,4},{1,9},{5... | collective-permute-start | bytes 884744 | tf_op jit(solution)/shard_map/ppermute | solution.py:473
  34.5 25.3 %collective-permute-start.17 = (bf16[256,1024]{1,0:T(8,128)(2,1)}, bf16[256,1024]{1,0:T(8,128)(2,1)S(1)}, u32[]{:S(2)}, u32[]{:S(2)}) collective-permute-start(bf16[256,1024]{1,0:T(8,128)(2,1)} %get-tuple-element.184), channel_id=1, source_target_pairs={{0,1},{1,0},{2,3},{3,2},{4,5},{5,4},{6,7},{7,6},{8,9},{9,8},{10,11... | collective-permute-start | bytes 1572872 | tf_op jit(solution)/shard_map/ppermute | solution.py:457
  47.4 19.3 %collective-permute-start.21 = (bf16[128,2048]{1,0:T(8,128)(2,1)S(1)}, bf16[128,2048]{1,0:T(8,128)(2,1)S(1)}, u32[]{:S(2)}, u32[]{:S(2)}) collective-permute-start(bf16[128,2048]{1,0:T(8,128)(2,1)S(1)} %get-tuple-element.171.refs_0_), channel_id=1, source_target_pairs={{0,8},{4,12},{8,16},{12,20},{16,24},{20,28},{24,0},{28,4},{1,9},{5... | collective-permute-start | bytes 1572872 | tf_op jit(solution)/shard_map/ppermute | solution.py:473
  49.2 17.5 %collective-permute-start.6 = (bf16[256,1024]{1,0:T(8,128)(2,1)S(1)}, bf16[256,1024]{1,0:T(8,128)(2,1)S(1)}, u32[]{:S(2)}, u32[]{:S(2)}) collective-permute-start(bf16[256,1024]{1,0:T(8,128)(2,1)S(1)} %add.117.xo_ref.x_ref), channel_id=1, source_target_pairs={{0,1},{1,0},{2,3},{3,2},{4,5},{5,4},{6,7},{7,6},{8,9},{9,8},{10,11... | collective-permute-start | bytes 1572872 | tf_op jit(solution)/shard_map/ppermute | solution.py:457
  52.8 13.9 %collective-permute-start.12 = (bf16[128,1152]{1,0:T(8,128)(2,1)}, bf16[128,1152]{1,0:T(8,128)(2,1)}, u32[]{:S(2)}, u32[]{:S(2)}) collective-permute-start(bf16[128,1152]{1,0:T(8,128)(2,1)} %collective-permute-done.10.refs_4_), channel_id=1, source_target_pairs={{0,4},{4,0},{8,12},{12,8},{16,20},{20,16},{24,28},{28,24},{1,5},{5... | collective-permute-start | bytes 884744 | tf_op jit(solution)/shard_map/ppermute | solution.py:457
  60.0 16.0 %collective-permute-start.18 = (bf16[256,1024]{1,0:T(8,128)(2,1)S(1)}, bf16[256,1024]{1,0:T(8,128)(2,1)S(1)}, u32[]{:S(2)}, u32[]{:S(2)}) collective-permute-start(bf16[256,1024]{1,0:T(8,128)(2,1)S(1)} %add_convert_fusion.3), channel_id=1, source_target_pairs={{0,2},{1,3},{2,0},{3,1},{4,6},{5,7},{6,4},{7,5},{8,10},{9,11},{10,... | collective-permute-start | bytes 1572872 | tf_op jit(solution)/shard_map/ppermute | solution.py:457
  66.7 13.6 %collective-permute-start.23 = (bf16[128,2048]{1,0:T(8,128)(2,1)S(1)}, bf16[128,2048]{1,0:T(8,128)(2,1)S(1)}, u32[]{:S(2)}, u32[]{:S(2)}) collective-permute-start(bf16[128,2048]{1,0:T(8,128)(2,1)S(1)} %collective-permute-done.21.refs_2_), channel_id=1, source_target_pairs={{0,8},{4,12},{8,16},{12,20},{16,24},{20,28},{24,0},{28,4},{1,9},{5... | collective-permute-start | bytes 1572872 | tf_op jit(solution)/shard_map/ppermute | solution.py:473
  76.2 18.2 %collective-permute-start.19 = (bf16[256,1024]{1,0:T(8,128)(2,1)S(1)}, bf16[256,1024]{1,0:T(8,128)(2,1)S(1)}, u32[]{:S(2)}, u32[]{:S(2)}) collective-permute-start(bf16[256,1024]{1,0:T(8,128)(2,1)S(1)} %add.120.co_ref.c_ref), channel_id=1, source_target_pairs={{0,1},{1,0},{2,3},{3,2},{4,5},{5,4},{6,7},{7,6},{8,9},{9,8},{10,11... | collective-permute-start | bytes 1572872 | tf_op jit(solution)/shard_map/ppermute | solution.py:457
  76.7 14.8 %collective-permute-start.22 = (bf16[128,2048]{1,0:T(8,128)(2,1)S(1)}, bf16[128,2048]{1,0:T(8,128)(2,1)S(1)}, u32[]{:S(2)}, u32[]{:S(2)}) collective-permute-start(bf16[128,2048]{1,0:T(8,128)(2,1)S(1)} %collective-permute-done.21.refs_2_), channel_id=1, source_target_pairs={{0,4},{4,0},{8,12},{12,8},{16,20},{20,16},{24,28},{28,24},{1,5},{5... | collective-permute-start | bytes 1572872 | tf_op jit(solution)/shard_map/ppermute | solution.py:457
  80.5 13.8 %collective-permute-start.16 = (bf16[256,1024]{1,0:T(8,128)(2,1)S(1)}, bf16[256,1024]{1,0:T(8,128)(2,1)S(1)}, u32[]{:S(2)}, u32[]{:S(2)}) collective-permute-start(bf16[256,1024]{1,0:T(8,128)(2,1)S(1)} %add_convert_fusion.4.t_ref.bt_ref.at_ref), channel_id=1, source_target_pairs={{0,2},{1,3},{2,0},{3,1},{4,6},{5,7},{6,4},{7,5},{8,10},{9,11},{10,... | collective-permute-start | bytes 1572872 | tf_op jit(solution)/shard_map/ppermute | solution.py:457
  81.2 21.6 %collective-permute-start.24 = (bf16[128,2048]{1,0:T(8,128)(2,1)S(1)}, bf16[128,2048]{1,0:T(8,128)(2,1)S(1)}, u32[]{:S(2)}, u32[]{:S(2)}) collective-permute-start(bf16[128,2048]{1,0:T(8,128)(2,1)S(1)} %collective-permute-done.23.refs_4_), channel_id=1, source_target_pairs={{0,4},{4,0},{8,12},{12,8},{16,20},{20,16},{24,28},{28,24},{1,5},{5... | collective-permute-start | bytes 1572872 | tf_op jit(solution)/shard_map/ppermute | solution.py:457
  93.2 19.9 %collective-permute-start.26 = (bf16[128,2048]{1,0:T(8,128)(2,1)S(1)}, bf16[128,2048]{1,0:T(8,128)(2,1)S(1)}, u32[]{:S(2)}, u32[]{:S(2)}) collective-permute-start(bf16[128,2048]{1,0:T(8,128)(2,1)S(1)} %collective-permute-done.25.refs_6_), channel_id=1, source_target_pairs={{0,4},{4,0},{8,12},{12,8},{16,20},{20,16},{24,28},{28,24},{1,5},{5... | collective-permute-start | bytes 1572872 | tf_op jit(solution)/shard_map/ppermute | solution.py:457
  96.9 16.2 %collective-permute-start.20 = (bf16[256,1024]{1,0:T(8,128)(2,1)S(1)}, bf16[256,1024]{1,0:T(8,128)(2,1)S(1)}, u32[]{:S(2)}, u32[]{:S(2)}) collective-permute-start(bf16[256,1024]{1,0:T(8,128)(2,1)S(1)} %norm_two.1.mo_ref), channel_id=1, source_target_pairs={{0,1},{1,0},{2,3},{3,2},{4,5},{5,4},{6,7},{7,6},{8,9},{9,8},{10,11... | collective-permute-start | bytes 1572872 | tf_op jit(solution)/shard_map/ppermute | solution.py:457
  125.0 14.0 %collective-permute-start.28 = (bf16[256,1024]{1,0:T(8,128)(2,1)S(1)}, bf16[256,1024]{1,0:T(8,128)(2,1)S(1)}, u32[]{:S(2)}, u32[]{:S(2)}) collective-permute-start(bf16[256,1024]{1,0:T(8,128)(2,1)S(1)} %add_convert_fusion.2.dt_ref), channel_id=1, source_target_pairs={{0,2},{1,3},{2,0},{3,1},{4,6},{5,7},{6,4},{7,5},{8,10},{9,11},{10,... | collective-permute-start | bytes 1572872 | tf_op jit(solution)/shard_map/ppermute | solution.py:457
  130.0 15.0 %collective-permute-start.43 = (bf16[128,1024]{1,0:T(8,128)(2,1)S(1)}, bf16[128,1024]{1,0:T(8,128)(2,1)S(1)}, u32[]{:S(2)}, u32[]{:S(2)}) collective-permute-start(bf16[128,1024]{1,0:T(8,128)(2,1)S(1)} %get-tuple-element.265), channel_id=1, source_target_pairs={{0,4},{4,0},{8,12},{12,8},{16,20},{20,16},{24,28},{28,24},{1,5},{5... | collective-permute-start | bytes 786440 | tf_op jit(solution)/shard_map/ppermute | solution.py:457
  131.0 17.4 %collective-permute-start.36 = (bf16[128,1024]{1,0:T(8,128)(2,1)S(1)}, bf16[128,1024]{1,0:T(8,128)(2,1)S(1)}, u32[]{:S(2)}, u32[]{:S(2)}) collective-permute-start(bf16[128,1024]{1,0:T(8,128)(2,1)S(1)} %get-tuple-element.237), channel_id=1, source_target_pairs={{0,4},{4,0},{8,12},{12,8},{16,20},{20,16},{24,28},{28,24},{1,5},{5... | collective-permute-start | bytes 786440 | tf_op jit(solution)/shard_map/ppermute | solution.py:457
  144.2 19.5 %collective-permute-start.29 = (bf16[256,1024]{1,0:T(8,128)(2,1)S(1)}, bf16[256,1024]{1,0:T(8,128)(2,1)S(1)}, u32[]{:S(2)}, u32[]{:S(2)}) collective-permute-start(bf16[256,1024]{1,0:T(8,128)(2,1)S(1)} %get-tuple-element.212), channel_id=1, source_target_pairs={{0,1},{1,0},{2,3},{3,2},{4,5},{5,4},{6,7},{7,6},{8,9},{9,8},{10,11... | collective-permute-start | bytes 1572872 | tf_op jit(solution)/shard_map/ppermute | solution.py:457
  145.0 18.9 %collective-permute-start.41 = (bf16[128,1024]{1,0:T(8,128)(2,1)S(1)}, bf16[128,1024]{1,0:T(8,128)(2,1)S(1)}, u32[]{:S(2)}, u32[]{:S(2)}) collective-permute-start(bf16[128,1024]{1,0:T(8,128)(2,1)S(1)} %get-tuple-element.257), channel_id=1, source_target_pairs={{0,4},{4,0},{8,12},{12,8},{16,20},{20,16},{24,28},{28,24},{1,5},{5... | collective-permute-start | bytes 786440 | tf_op jit(solution)/shard_map/ppermute | solution.py:457
  166.4 17.0 %collective-permute-start.42 = (bf16[128,1152]{1,0:T(8,128)(2,1)S(1)}, bf16[128,1152]{1,0:T(8,128)(2,1)S(1)}, u32[]{:S(2)}, u32[]{:S(2)}) collective-permute-start(bf16[128,1152]{1,0:T(8,128)(2,1)S(1)} %get-tuple-element.260), channel_id=1, source_target_pairs={{0,4},{4,0},{8,12},{12,8},{16,20},{20,16},{24,28},{28,24},{1,5},{5... | collective-permute-start | bytes 884744 | tf_op jit(solution)/shard_map/ppermute | solution.py:457
  167.5 19.2 %collective-permute-start.31 = (bf16[256,1024]{1,0:T(8,128)(2,1)S(1)}, bf16[256,1024]{1,0:T(8,128)(2,1)S(1)}, u32[]{:S(2)}, u32[]{:S(2)}) collective-permute-start(bf16[256,1024]{1,0:T(8,128)(2,1)S(1)} %add_convert_fusion.1.mt_ref), channel_id=1, source_target_pairs={{0,2},{1,3},{2,0},{3,1},{4,6},{5,7},{6,4},{7,5},{8,10},{9,11},{10,... | collective-permute-start | bytes 1572872 | tf_op jit(solution)/shard_map/ppermute | solution.py:457
  178.4 19.0 %collective-permute-start.61 = (bf16[128,1024]{1,0:T(8,128)(2,1)S(1)}, bf16[128,1024]{1,0:T(8,128)(2,1)S(1)}, u32[]{:S(2)}, u32[]{:S(2)}) collective-permute-start(bf16[128,1024]{1,0:T(8,128)(2,1)S(1)} %add_convert_fusion.11), channel_id=1, source_target_pairs={{0,8},{4,12},{8,16},{12,20},{16,24},{20,28},{24,0},{28,4},{1,9},{5... | collective-permute-start | bytes 786440 | tf_op jit(solution)/shard_map/ppermute | solution.py:473
  183.5 14.1 %collective-permute-start.38 = (bf16[128,1152]{1,0:T(8,128)(2,1)S(1)}, bf16[128,1152]{1,0:T(8,128)(2,1)S(1)}, u32[]{:S(2)}, u32[]{:S(2)}) collective-permute-start(bf16[128,1152]{1,0:T(8,128)(2,1)S(1)} %get-tuple-element.245), channel_id=1, source_target_pairs={{0,4},{4,0},{8,12},{12,8},{16,20},{20,16},{24,28},{28,24},{1,5},{5... | collective-permute-start | bytes 884744 | tf_op jit(solution)/shard_map/ppermute | solution.py:457
  185.6 16.2 %collective-permute-start.46 = (bf16[128,1152]{1,0:T(8,128)(2,1)S(1)}, bf16[128,1152]{1,0:T(8,128)(2,1)S(1)}, u32[]{:S(2)}, u32[]{:S(2)}) collective-permute-start(bf16[128,1152]{1,0:T(8,128)(2,1)S(1)} %add_convert_fusion.7), channel_id=1, source_target_pairs={{0,8},{4,12},{8,16},{12,20},{16,24},{20,28},{24,0},{28,4},{1,9},{5... | collective-permute-start | bytes 884744 | tf_op jit(solution)/shard_map/ppermute | solution.py:473
  198.4 22.3 %collective-permute-start.32 = (bf16[256,1024]{1,0:T(8,128)(2,1)}, bf16[256,1024]{1,0:T(8,128)(2,1)}, u32[]{:S(2)}, u32[]{:S(2)}) collective-permute-start(bf16[256,1024]{1,0:T(8,128)(2,1)} %get-tuple-element.228.own_ref), channel_id=1, source_target_pairs={{0,1},{1,0},{2,3},{3,2},{4,5},{5,4},{6,7},{7,6},{8,9},{9,8},{10,11... | collective-permute-start | bytes 1572872 | tf_op jit(solution)/shard_map/ppermute | solution.py:457
  203.1 21.0 %collective-permute-start.39 = (bf16[128,1152]{1,0:T(8,128)(2,1)}, bf16[128,1152]{1,0:T(8,128)(2,1)}, u32[]{:S(2)}, u32[]{:S(2)}) collective-permute-start(bf16[128,1152]{1,0:T(8,128)(2,1)} %get-tuple-element.248), channel_id=1, source_target_pairs={{0,4},{4,0},{8,12},{12,8},{16,20},{20,16},{24,28},{28,24},{1,5},{5... | collective-permute-start | bytes 884744 | tf_op jit(solution)/shard_map/ppermute | solution.py:457
  206.3 20.4 %collective-permute-start.59 = (bf16[128,1024]{1,0:T(8,128)(2,1)}, bf16[128,1024]{1,0:T(8,128)(2,1)}, u32[]{:S(2)}, u32[]{:S(2)}) collective-permute-start(bf16[128,1024]{1,0:T(8,128)(2,1)} %get-tuple-element.295), channel_id=1, source_target_pairs={{0,4},{4,0},{8,12},{12,8},{16,20},{20,16},{24,28},{28,24},{1,5},{5... | collective-permute-start | bytes 786440 | tf_op jit(solution)/shard_map/ppermute | solution.py:457
  210.1 14.0 %collective-permute-start.47 = (bf16[128,1152]{1,0:T(8,128)(2,1)}, bf16[128,1152]{1,0:T(8,128)(2,1)}, u32[]{:S(2)}, u32[]{:S(2)}) collective-permute-start(bf16[128,1152]{1,0:T(8,128)(2,1)} %add_convert_fusion.6), channel_id=1, source_target_pairs={{0,8},{4,12},{8,16},{12,20},{16,24},{20,28},{24,0},{28,4},{1,9},{5... | collective-permute-start | bytes 884744 | tf_op jit(solution)/shard_map/ppermute | solution.py:473
  220.8 13.8 %collective-permute-start.35 = (bf16[256,1024]{1,0:T(8,128)(2,1)S(1)}, bf16[256,1024]{1,0:T(8,128)(2,1)S(1)}, u32[]{:S(2)}, u32[]{:S(2)}) collective-permute-start(bf16[256,1024]{1,0:T(8,128)(2,1)S(1)} %input_grad.1.own_ref), channel_id=1, source_target_pairs={{0,1},{1,0},{2,3},{3,2},{4,5},{5,4},{6,7},{7,6},{8,9},{9,8},{10,11... | collective-permute-start | bytes 1572872 | tf_op jit(solution)/shard_map/ppermute | solution.py:457
  (84 other events, 817.9 us)
where the time goes:
time: 240 us; the launch traced here: 237 us
  waiting for transfers between devices  99.9 us (42%)
  Pallas kernels  64.1 us (27%)
  starting transfers between devices  46.5 us (19%)
  local copies, waits for them, and re-layouts  16.3 us (7%)
  other arithmetic  8.8 us (4%)
    ppermute x47, waiting for transfers between devices, flip_bit(): return lax.ppermute(v, axis, [(i, i ^ mask) for i in range(size)])  71.4 us
    pallas_call x21, Pallas kernels, call(): pl.pallas_call(body, out_shape=shapes, in_specs=[SM] * smem + [VM] * (len...  64.1 us
    ppermute x47, starting transfers between devices, flip_bit(): return lax.ppermute(v, axis, [(i, i ^ mask) for i in range(size)])  33 us
    ppermute x15, waiting for transfers between devices, ring(): return lax.ppermute(v, 'seq', [(i, (i + 2) % seqs) for i in range(seqs)])  28.5 us
    unnamed x104, local copies, waits for them, and re-layouts  12.5 us
    ppermute x15, starting transfers between devices, ring(): return lax.ppermute(v, 'seq', [(i, (i + 2) % seqs) for i in range(seqs)])  12.2 us
    convert_element_type x15, other arithmetic, add(): return total.astype(bf16)  4.84 us
  transfers between devices with their start and end apart: 64, of which 27 were waited for; matrix products, arithmetic and copies ran while one was open for 4% of the time, Pallas kernels for 21%

commit v1 on v0

--- a/solution.py
+++ b/solution.py
@@ -31,14 +31,14 @@
 
 def call(
     body, args, outs, scratch=(), smem=0, flops=0, name=None, limit=8, keep=True, keep_out=True,
-    cold=(),
+    cold=(), free=(),
 ):
     moved = sum(a.size * a.dtype.itemsize for a in args)
     moved += sum(o.size * o.dtype.itemsize for o in outs)
     if keep:
         args = tuple(
             a
-            if n < smem
+            if n < smem or n in free
             else pltpu.with_memory_space_constraint(a, pltpu.HBM if n in cold else pltpu.VMEM)
             for n, a in enumerate(args)
         )
@@ -138,7 +138,7 @@
             v = qkv_ref[span, 2 * part + h * HEAD_DIM : 2 * part + (h + 1) * HEAD_DIM]
             logits = jnp.where(allowed, mm(q, k, NT) * score_scale, masked)
             e = jnp.exp(logits - jnp.max(logits, axis=-1, keepdims=True))
-            p = e / jnp.sum(e, axis=-1, keepdims=True)
+            p = e * (1.0 / jnp.sum(e, axis=-1, keepdims=True))
             p_ref[half * heads + h] = p
             o_ref[span, h * HEAD_DIM : (h + 1) * HEAD_DIM] = mm(p.astype(bf16), v).astype(bf16)
 
@@ -212,37 +212,31 @@
     lax.fori_loop(0, width // tile, step2, 0)
 
 
-def up_grad_body(idx, du_ref, mo_ref, mt_ref, wu_ref, gcol, *refs):
-    col_ref, ups, (flip,) = refs[0], refs[1 : 1 + BLOCKS], refs[1 + BLOCKS :]
+def mlp_grad_body(
+    idx, g_ref, du_ref, db_ref, mo_ref, mt_ref, wu_ref, wd_ref, gcol, ao_ref, at_ref, co_ref,
+    ct_ref, xo_ref, xt_ref, *refs
+):
+    bo_ref, bt_ref, col_ref = refs[:3]
+    grads, (flip,) = refs[3 : 3 + BLOCKS], refs[3 + BLOCKS :]
     rows, width = mo_ref.shape
-    blk = width // BLOCKS
+    units = wu_ref.shape[1]
+    blk, sub = width // BLOCKS, units // BLOCKS
     tile = 256
 
-    def step(i, carry):
+    def turn_rows(i, carry):
         cols = pl.ds(pl.multiple_of(i * tile, tile), tile)
         flip[cols, :rows] = mo_ref[:, cols].T
         flip[cols, rows:] = mt_ref[:, cols].T
         return carry
 
-    lax.fori_loop(0, width // tile, step, 0)
-    for b, ref in enumerate(ups):
+    lax.fori_loop(0, width // tile, turn_rows, 0)
+    for b, ref in enumerate(grads):
         off = pl.ds(pl.multiple_of(idx[b] * blk, blk), blk)
         grad = mm(flip[off, :], du_ref[...])
-        ref[...] = grad.astype(bf16)
+        ref[:, :units] = grad.astype(bf16)
         gain = jnp.sum(grad * wu_ref[off, :].astype(f32), axis=-1, keepdims=True)
         gain = gain / gcol[off, 1:2].astype(f32)
         col_ref[off, :] = jnp.broadcast_to(gain, (blk, 128))
-
-
-def down_grad_body(
-    idx, g_ref, db_ref, wd_ref, col_in, ao_ref, at_ref, co_ref, ct_ref, xo_ref, xt_ref, *refs
-):
-    bo_ref, bt_ref, col_ref = refs[:3]
-    downs, (flip,) = refs[3 : 3 + BLOCKS], refs[3 + BLOCKS :]
-    rows, width = bo_ref.shape
-    units = wd_ref.shape[0]
-    sub = units // BLOCKS
-    tile = 256
 
     def step(i, carry):
         cols = pl.ds(pl.multiple_of(i * tile, tile), tile)
@@ -263,9 +257,9 @@
 
     zero = jnp.zeros((rows, 1), f32)
     dots = lax.fori_loop(0, width // tile, step, (zero, zero))
-    for b, ref in enumerate(downs):
+    for b, ref in enumerate(grads):
         off = pl.multiple_of(idx[b] * sub, sub)
-        ref[...] = mm(flip[pl.ds(off, sub), :], db_ref[...]).astype(bf16)
+        ref[:, units:] = mm(flip[pl.ds(off, sub), :], db_ref[...]).astype(bf16)
     lane = lax.broadcasted_iota(jnp.int32, (rows, 128), 1)
     route = jnp.zeros((width, 128), f32)
     for d, x_ref in zip(dots, (xo_ref, xt_ref)):
@@ -274,7 +268,7 @@
         route += mm(x_ref[...], two, TN)
     total = jnp.sum(route[:, :2], axis=-1, keepdims=True)
     wide = lax.broadcasted_iota(jnp.int32, (width, 128), 1)
-    col_ref[...] = jnp.where(wide == 1, col_in[...], jnp.where(wide == 2, total, 0.0))
+    col_ref[...] = jnp.where(wide == 1, col_ref[...], jnp.where(wide == 2, total, 0.0))
 
 
 def hidden_grad_body(dt_ref, du_ref, bt_ref, bu_ref, x_ref, c_ref, r_ref, gr_ref, da_ref, dh_ref):
@@ -302,9 +296,7 @@
 def attn_bwd_body(
     idx, at_ref, ot_ref, qkv_ref, p_ref, dao_ref, dat_ref, wq_ref, wo_ref, gcol, col_ref, *refs
 ):
-    dqkv = refs[0]
-    grads = refs[1 : 1 + BLOCKS]
-    (da,) = refs[1 + BLOCKS :]
+    dqkv, near, far, (da,) = refs[0], refs[1:5], refs[5:7], refs[7:]
     rows, width = dao_ref.shape
     part = width // 4
     qcols = 3 * part
@@ -330,17 +322,20 @@
     blk = width // BLOCKS
     ob = part // BLOCKS
     lane = lax.broadcasted_iota(jnp.int32, (blk, 128), 1)
-    for b, ref in enumerate(grads):
+    for b in range(BLOCKS):
         s = idx[b]
+        k = b // 2
+        ref, row = (near[k], 0) if b % 2 == 0 else (far[(k + 3) % 4 // 2], (k + 3) % 2 * blk)
+        rows_of = slice(row, row + blk)
         off = pl.ds(pl.multiple_of(s * blk, blk), blk)
         grad = mm(at_ref[off, :], dqkv[...])
-        ref[:, :qcols] = grad.astype(bf16)
+        ref[rows_of, :qcols] = grad.astype(bf16)
         gain = jnp.sum(grad * wq_ref[off, :].astype(f32), axis=-1, keepdims=True)
         gain = gain / gcol[off, 0:1].astype(f32)
-        ref[:, qcols : qcols + 128] = jnp.where(lane == 0, gain, col_ref[off, :]).astype(bf16)
+        ref[rows_of, qcols : qcols + 128] = jnp.where(lane == 0, gain, col_ref[off, :]).astype(bf16)
         og = mm(ot_ref[pl.ds(pl.multiple_of(s * ob, ob), ob), :], da[...]).astype(bf16)
         for j in range(4):
-            ref[j * ob : (j + 1) * ob, qcols + 128 :] = og[:, j * part : (j + 1) * part]
+            ref[row + j * ob : row + (j + 1) * ob, qcols + 128 :] = og[:, j * part : (j + 1) * part]
 
 
 def normed_grad_body(dqkv_ref, wq_ref, do_ref, dt_ref):
@@ -405,30 +400,34 @@
         attn_ref[j * mine : (j + 1) * mine, head:] = rows[:, j * part : (j + 1) * part]
 
 
-def split_attn_body(meta, a_ref, b_ref, c_ref, c0, c1, c2, c3, out_ref, tmp):
+def split_body(
+    meta, m0, m1, m2, a0, a1, a2, c0, c1, c2, c3, down_ref, out_ref, tm, ta
+):
     mine, width = out_ref.shape
+    units = m0.shape[1] - width
     part = width // 4
     head = 3 * part + 128
-    tmp[...] = (a_ref[...].astype(f32) + b_ref[...].astype(f32)) + c_ref[...].astype(f32)
+    for n in range(4):
+        span = pl.ds(n * mine, mine)
+        total = (m0[span, :].astype(f32) + m1[span, :].astype(f32)) + m2[span, :].astype(f32)
+        down_ref[span, :] = total[:, units:]
+        tm[span, :] = total[:, :units]
+        late = pl.ds((4 + n) * mine, mine)
+        total = (a0[span, :].astype(f32) + a1[late, :].astype(f32)) + a2[span, :].astype(f32)
+        ta[span, :] = total[:, :head]
+        out_ref[:, n * part : (n + 1) * part] = total[:, head:]
     for k, ref in enumerate((c0, c1, c2, c3)):
         off = pl.ds(pl.multiple_of((meta[3] ^ k) * mine, mine), mine)
-        ref[...] = tmp[off, :head].astype(ref.dtype)
-    for j in range(4):
-        out_ref[:, j * part : (j + 1) * part] = tmp[j * mine : (j + 1) * mine, head:]
-
-
-def split_up_body(meta, a_ref, b_ref, c_ref, c0, c1, c2, c3, tmp):
-    mine = c0.shape[0]
-    tmp[...] = (a_ref[...].astype(f32) + b_ref[...].astype(f32)) + c_ref[...].astype(f32)
-    for k, ref in enumerate((c0, c1, c2, c3)):
-        off = pl.ds(pl.multiple_of((meta[3] ^ k) * mine, mine), mine)
-        ref[...] = tmp[off, :].astype(ref.dtype)
-
-
-def final_attn_body(meta, c0, c1, c2, c3, out_ref, small_ref, tmp):
-    mine = out_ref.shape[0]
-    width = out_ref.shape[1] // 3
+        ref[:, :head] = ta[off, :].astype(ref.dtype)
+        ref[:, head:] = tm[off, :].astype(ref.dtype)
+
+
+def final_body(meta, c0, c1, c2, c3, qkv_ref, up_ref, small_ref, tmp):
+    mine = qkv_ref.shape[0]
+    width = qkv_ref.shape[1] // 3
     part = width // 4
+    head = 3 * part + 128
+    sub = up_ref.shape[1] // (4 * BLOCKS)
     for k, ref in enumerate((c0, c1, c2, c3)):
         tmp[meta[3] ^ k] = ref[...].astype(f32)
     for j in range(4):
@@ -436,23 +435,16 @@
             for z in range(4):
                 dst = t * width + (4 * z + HEAD_OF[j]) * HEAD_DIM
                 src = t * part + z * HEAD_DIM
-                out_ref[:, dst : dst + HEAD_DIM] = tmp[j, :, src : src + HEAD_DIM]
-    head = slice(3 * part, 3 * part + 128)
-    small = (tmp[0, :, head] + tmp[1, :, head]) + (tmp[2, :, head] + tmp[3, :, head])
+                qkv_ref[:, dst : dst + HEAD_DIM] = tmp[j, :, src : src + HEAD_DIM]
+        for s in range(BLOCKS):
+            dst = (4 * s + j) * sub
+            up_ref[:, dst : dst + sub] = tmp[j, :, head + s * sub : head + (s + 1) * sub]
+    last = slice(3 * part, head)
+    small = (tmp[0, :, last] + tmp[1, :, last]) + (tmp[2, :, last] + tmp[3, :, last])
     wide = jnp.concatenate([small, jnp.zeros((128 - mine, 128), f32)], axis=0)
     small_ref[...] = wide.T[:8]
 
 
-def final_up_body(meta, c0, c1, c2, c3, out_ref, tmp):
-    sub = out_ref.shape[1] // (4 * BLOCKS)
-    for k, ref in enumerate((c0, c1, c2, c3)):
-        tmp[meta[3] ^ k] = ref[...].astype(f32)
-    for j in range(4):
-        for s in range(BLOCKS):
-            dst = (4 * s + j) * sub
-            out_ref[:, dst : dst + sub] = tmp[j, :, s * sub : (s + 1) * sub]
-
-
 def flip_bit(v, axis, size, mask):
     return lax.ppermute(v, axis, [(i, i ^ mask) for i in range(size)])
 
@@ -469,7 +461,7 @@
     return flip_bit(v, "seq", seqs, 1)
 
 
-def ring(v, seqs):
+def shift_one(v, seqs):
     return lax.ppermute(v, "seq", [(i, (i + 2) % seqs) for i in range(seqs)])
 
 
@@ -508,25 +500,22 @@
 
 
 class Flow:
-    def __init__(self):
-        self.v = {}
-
     def __getitem__(self, name):
-        return self.v[name]
+        return self.__dict__[name]
 
     def __setitem__(self, name, value):
-        self.v[name] = value
+        self.__dict__[name] = value
 
     def order(self, value, name):
         token = lax.create_token()
-        token, self.v[name] = lax.optimization_barrier((token, self.v[name]))
+        token, self[name] = lax.optimization_barrier((token, self[name]))
         return lax.optimization_barrier((token, value))[1]
 
     def sync(self, *names):
-        held = [n for n in names if n in self.v]
-        done = lax.optimization_barrier(tuple(self.v[n] for n in held))
+        held = [n for n in names if n in self.__dict__]
+        done = lax.optimization_barrier(tuple(self[n] for n in held))
         for n, value in zip(held, done):
-            self.v[n] = value
+            self[n] = value
 
 
 def on_device(
@@ -562,14 +551,20 @@
 
     queue = []
 
-    def side(name, t, lag=3):
+    chain = []
+
+    def hop(name, t, lag):
+        if len(chain) >= lag:
+            t = v.order(t, chain[-lag])
+        chain.append(name)
+        v[name] = shift_one(t, seqs)
+
+    def side(name, t, lag):
         if len(queue) >= lag:
             t = v.order(t, queue[-lag])
         queue.append(name)
         v[name] = swap_side(t, seqs)
 
-    def turn(t):
-        return ring(t, seqs)
 
     flip = core == 1
     pos = jnp.where(flip, routed[::-1], routed)
@@ -589,7 +584,6 @@
 
     gains = jnp.stack([attn_gain, mlp_gain, router_weight], axis=1)
     gains = jnp.pad(gains, ((0, 0), (0, 125)))
-    x_mine, x_send = pick(tokens, "pick_tokens")
     if native:
         qkv_view = qkv_weight.reshape(mine, 3, 4, 4, HEAD_DIM)
         chunks = [
@@ -614,12 +608,13 @@
         up_rows = jnp.concatenate(exchange(chunks, member), axis=0)
         mlp_packs = native_gather(jnp.concatenate([up_rows, down_weight], axis=1))
         order = jnp.arange(BLOCKS, dtype=jnp.int32)
-        v["tx"] = add(x_mine, swap_core(x_send))
-        v["yx"] = swap_pair(v["tx"])
-        v["x"] = v["tx"] + v["yx"]
-        v["xo"] = swap_core(v["x"])
+        x_mine, x_send = pick(tokens, "pick_tokens")
+        v.tx = add(x_mine, swap_core(x_send))
+        v.yx = swap_pair(v.tx)
+        v.x = v.tx + v.yx
+        v.xo = swap_core(v.x)
         c_mine, c_send = pick(cotangent, "pick_cotangent")
-        v["tc"] = add(c_mine, swap_core(c_send))
+        v.tc = add(c_mine, swap_core(c_send))
     else:
         order = jnp.stack(
             [((place ^ r) - 2 * k) % seqs for k in range(BLOCKS // 2) for r in range(2)]
@@ -632,41 +627,37 @@
             pack_body, (meta, qkv_weight, up_weight, gains), (chunk,) * 4,
             scratch=[pltpu.VMEM((4, mine, head + ff), bf16)], smem=1, name="pack", cold=(1, 2, 3),
         )
-        got = [chunks[0]] + [flip_bit(chunks[k], "grp", 4, k) for k in range(1, 4)]
+        v.k0, v.k1, v.k2, v.k3 = chunks
+        v.tokens = tokens
+        v.sync("k1", "k2", "k3", "tokens")
+        got = [v.k0] + [flip_bit(v["k%d" % k], "grp", 4, k) for k in range(1, 4)]
+        x_mine, x_send = pick(v.tokens, "pick_tokens")
         moved = lax.ppermute(out_weight, ("seq", "grp"), swaps)
-        v["a0"], v["m0"] = call(
+        v.a0, v.m0 = call(
             join_body, (meta, *got, out_weight, moved, down_weight),
             (out((mine * 4, width + 128), bf16), out((mine * 4, ff + width), bf16)), smem=1,
             name="join", cold=(2, 3, 4, 5, 6, 7),
         )
-        v["tx"] = add(x_mine, swap_core(x_send))
+        v.tx = add(x_mine, swap_core(x_send))
         v.sync("a0", "m0", "tx")
-        v["a1"] = turn(v["a0"])
-        v["m1"] = turn(v["m0"])
-        side("xa0", v["a0"], 2)
-        side("xm0", v["m0"], 2)
-        v["yx"] = swap_pair(v["tx"])
-        v["a2"] = turn(v["a1"])
-        side("xa1", v["a1"], 2)
-        v["a3"] = turn(v["a2"])
-        side("xa2", v["a2"], 2)
-        v["x"] = v["tx"] + v["yx"]
-        v["xo"] = swap_core(v["x"])
-        side("xa3", v["a3"], 2)
-        v["m2"] = turn(v["m1"])
-        v["m3"] = turn(v["m2"])
-        side("xm1", v["m1"], 2)
-        side("xm2", v["m2"], 2)
-        side("xm3", v["m3"], 2)
+        for n, k in (('a', 1), ('m', 1), ('a', 2), ('a', 3), ('m', 2), ('m', 3)):
+            hop("%s%d" % (n, k), v["%s%d" % (n, k - 1)], 3)
+        v.yx = swap_pair(v.tx)
+        v.x = v.tx + v.yx
+        v.xo = swap_core(v.x)
+        for n, k in (('m', 0), ('a', 0), ('a', 1), ('a', 2), ('a', 3), ('m', 1), ('m', 2), ('m', 3)):
+            side("x%s%d" % (n, k), v["%s%d" % (n, k)], 2)
         c_mine, c_send = pick(cotangent, "pick_cotangent")
-        v["tc"] = add(c_mine, swap_core(c_send))
-        v["yc"] = swap_pair(v["tc"])
+        v.tc = add(c_mine, swap_core(c_send))
+        v.yc = swap_pair(v.tc)
+        v.sync("x", "xo", "m1")
+        v.sync("tc", "xo")
         attn_names = [n + str(k) for k in range(4) for n in ("a", "xa")]
         attn_packs = [v[n] for n in attn_names]
 
     a, qkv, probs, mix, ba_o, ba_t, w_qkv, w_out, gain_rows, r, gain_cols = call(
         attn_fwd_body,
-        (order, v["x"], v["xo"], seg_col, seg_row, *attn_packs),
+        (order, v.x, v.xo, seg_col, seg_row, *attn_packs),
         (
             out((both, width), bf16),
             out((both, 3 * part), bf16),
@@ -685,28 +676,28 @@
         name="attn_fwd",
         cold=range(1, 13),
     )
-    v["a"], v["mix"] = a, mix
-    v["tb"] = add(ba_o, swap_core(ba_t))
-    v.sync("tb", "a", "mix")
-    v["yb"] = swap_pair(v["tb"])
+    v.a, v.mix = a, mix
+    v.tb = add(ba_o, swap_core(ba_t))
+    v.sync("tb", "a", "mix", "xm1")
+    v.yb = swap_pair(v.tb)
     if native:
-        v["yc"] = swap_pair(v["tc"])
+        v.yc = swap_pair(v.tc)
     a_turned, mix_turned = call(
-        turn_body, (v["a"], v["mix"]), (out((width, both), bf16), out((part, both), bf16)),
+        turn_body, (v.a, v.mix), (out((width, both), bf16), out((part, both), bf16)),
         name="turn",
     )
-    v["c"] = v["tc"] + v["yc"]
-    v["co"] = swap_core(v["c"])
-    v.sync("yb", "tb", "co", "c")
-    (v["h"],) = call(
-        norm_body, (v["tb"], v["yb"], v["x"], gain_rows), (half,), name="norm_two", cold=(0, 1, 2)
-    )
-    v["ho"] = swap_core(v["h"])
+    v.c = v.tc + v.yc
+    v.co = swap_core(v.c)
+    v.sync("yb", "tb", "co", "c", "xm2")
+    (v.h,) = call(
+        norm_body, (v.tb, v.yb, v.x, gain_rows), (half,), name="norm_two", free=(0, 1, 2)
+    )
+    v.ho = swap_core(v.h)
     if not native:
         mlp_packs = [v[n + str(k)] for k in range(4) for n in ("m", "xm")]
     g, du, db, w_up, w_down, dm_o, dm_t = call(
         mlp_body,
-        (order, v["h"], v["ho"], v["c"], v["co"], r, *mlp_packs),
+        (order, v.h, v.ho, v.c, v.co, r, *mlp_packs),
         (
             out((both, ff), bf16),
             out((both, ff), bf16),
@@ -722,67 +713,64 @@
         cold=(2, 3, 4, *range(6, 14)),
     )
 
-    v["du"] = du
-    v["td"] = add(dm_o, swap_core(dm_t))
+    v.du = du
+    v.td = add(dm_o, swap_core(dm_t))
     v.sync("td", "du")
-    v["yd"] = swap_pair(v["td"])
-    col, *up_grads = call(
-        up_grad_body,
-        (order, v["du"], v["h"], v["ho"], w_up, gain_cols),
-        (out((width, 128), f32), *([out((width // BLOCKS, ff), bf16)] * BLOCKS)),
+    v.yd = swap_pair(v.td)
+    bm_o, bm_t, cols, *mlp_grads = call(
+        mlp_grad_body,
+        (
+            order, g, v.du, db, v.h, v.ho, w_up, w_down, gain_cols, ba_o, ba_t, v.c,
+            v.co, v.x, v.xo,
+        ),
+        (
+            half, half, out((width, 128), f32),
+            *([out((width // BLOCKS, ff + width), bf16)] * BLOCKS),
+        ),
         scratch=[pltpu.VMEM((width, both), bf16)],
         smem=1,
-        flops=2 * both * width * ff,
-        name="up_grad",
-        cold=(3,),
-    )
-    v["g"] = g
+        flops=6 * both * width * ff,
+        name="mlp_grad",
+        cold=(5, 11, 12, 13, 14),
+    )
+    v.bm, v.bn = bm_o, bm_t
+    v.tm = add(v.bm, swap_core(v.bn))
+    parts = {"m": mlp_grads}
+    queue.clear()
+    chain.clear()
+    v.__dict__.update({n + str(k): None for n in ("xm", "xa") for k in range(4)})
     if not native:
-        for k in (1, 2, 3):
-            side("xu%d" % k, up_grads[2 * k + 1])
-    bm_o, bm_t, cols, *down_grads = call(
-        down_grad_body,
-        (
-            order, v["g"], db, w_down, col, ba_o, ba_t, v["c"], v["co"], v["x"], v["xo"],
-        ),
-        (half, half, out((width, 128), f32), *([out((ff // BLOCKS, width), bf16)] * BLOCKS)),
-        scratch=[pltpu.VMEM((ff, both), bf16)],
-        smem=1,
-        flops=4 * both * width * ff,
-        name="down_grad",
-        cold=(7, 8, 9, 10),
-    )
-    v["bm"], v["bn"], v["col"] = bm_o, bm_t, col
+        for n, k in (('m', 1), ('m', 2)):
+            side("x%s%d" % (n, k), parts[n][2 * k + 1], 3)
     v.sync("yd", "td", "bm")
-    v["tm"] = add(v["bm"], swap_core(v["bn"]))
     da_own, dh = call(
         hidden_grad_body,
-        (v["td"], v["yd"], v["tb"], v["yb"], v["x"], v["c"], r, gain_rows),
+        (v.td, v.yd, v.tb, v.yb, v.x, v.c, r, gain_rows),
         (half, out((rows, width), f32)),
         name="hidden_grad",
-        cold=range(6),
-    )
-    v["da"] = da_own
-    v["dao"] = swap_core(da_own)
-
+        free=range(6),
+    )
+    v.da = da_own
+    v.dao = swap_core(da_own)
     def attention_back(v):
         dqkv, *attn_grads = call(
             attn_bwd_body,
             (
-                order, a_turned, mix_turned, qkv, probs, v["da"], v["dao"], w_qkv, w_out,
+                order, a_turned, mix_turned, qkv, probs, v.da, v.dao, w_qkv, w_out,
                 gain_cols, cols,
             ),
             (
                 out((both, 3 * part), bf16),
-                *([out((width // BLOCKS, width + 128), bf16)] * BLOCKS),
+                *([out((width // BLOCKS, width + 128), bf16)] * 4),
+                *([out((2 * width // BLOCKS, width + 128), bf16)] * 2),
             ),
             scratch=[pltpu.VMEM((both, width), bf16)],
             smem=1,
             flops=3 * both * width * width,
             name="attn_bwd",
-            cold=(6,),
-        )
-        v["dqkv"] = dqkv
+            free=(6,),
+        )
+        v.dqkv = dqkv
         return attn_grads
 
     def normed_back(dqkv):
@@ -794,16 +782,16 @@
     def give():
         return call(
             result_body,
-            (v["tb"], v["yb"], v["tm"], v["ym"], v["c"], r),
+            (v.tb, v.yb, v.tm, v.ym, v.c, r),
             (half, out((rows, 128), f32)),
             name="result",
-            cold=range(5),
+            free=range(5),
         )
 
     def take(dr):
         return call(
-            input_grad_body, (v["tx2"], v["yx2"], v["x"], dh, dr, gain_rows), (half,),
-            name="input_grad", cold=range(3),
+            input_grad_body, (v.tx2, v.yx2, v.x, dh, dr, gain_rows), (half,),
+            name="input_grad", free=range(3),
         )[0]
 
     def place_rows(base, own, other, name):
@@ -814,70 +802,87 @@
 
     if native:
         attn_grads = attention_back(v)
-        dx_o, dx_t = normed_back(v["dqkv"])
-        v["ym"] = swap_pair(v["tm"])
-        v["tx2"] = add(dx_o, swap_core(dx_t))
-        v["yx2"] = swap_pair(v["tx2"])
-        v["e"], dr = give()
-        v["eo"] = swap_core(v["e"])
-        v["dx"] = take(dr)
-        v["dxo"] = swap_core(v["dx"])
+        blk = width // BLOCKS
+        far = {(k + 3) % 4: attn_grads[4 + (k + 3) % 4 // 2] for k in range(4)}
+        attn_grads = [
+            attn_grads[k] if r == 0 else far[(k + 3) % 4][(k + 3) % 2 * blk :][:blk]
+            for k in range(4)
+            for r in range(2)
+        ]
+        dx_o, dx_t = normed_back(v.dqkv)
+        v.ym = swap_pair(v.tm)
+        v.tx2 = add(dx_o, swap_core(dx_t))
+        v.yx2 = swap_pair(v.tx2)
+        v.e, dr = give()
+        v.eo = swap_core(v.e)
+        v.dx = take(dr)
+        v.dxo = swap_core(v.dx)
     else:
         attn_grads = attention_back(v)
-        v["ym"] = swap_pair(v.order(v["tm"], "dqkv"))
-        v["dxm"], v["dxs"] = normed_back(v["dqkv"])
-        down_grads[3] = v.order(down_grads[3], "dqkv")
-        parts = {"u": up_grads, "a": attn_grads, "w": down_grads}
-        up_grads[2] = v.order(up_grads[2], "dqkv")
-        for n, k in (("u", 0), ("w", 1), ("a", 1), ("a", 2), ("a", 3), ("w", 2), ("w", 3), ("a", 0), ("w", 0)):
-            side("x%s%d" % (n, k), parts[n][2 * k + 1])
-        for n, blocks in parts.items():
-            z = turn(add(blocks[2], v["x%s1" % n]))
-            z = turn(add(blocks[4], v["x%s2" % n], z))
-            v["z%s3" % n] = turn(add(blocks[6], v["x%s3" % n], z))
-            v[n + "0"] = blocks[0]
-        v["tx2"] = add(v["dxm"], swap_core(v["dxs"]))
-        v["yx2"] = swap_pair(v["tx2"])
-        v["e"], dr = give()
-        v["eo"] = swap_core(v["e"])
-        v["dx"] = take(dr)
-        v["dxo"] = swap_core(v["dx"])
-        piece = [out((mine, ff), f32)] + [out((mine, ff), bf16)] * 3
-        cut = call(
-            split_up_body, (meta, v["u0"], v["xu0"], v["zu3"]), piece,
-            scratch=[pltpu.VMEM((4 * mine, ff), f32)], smem=1, name="split_up", cold=(2, 3),
-        )
-        cut = [cut[0]] + [flip_bit(cut[k], "grp", 4, k) for k in range(1, 4)]
-        (up_grad,) = call(
-            final_up_body, (meta, *cut), (out((mine, units), f32),),
-            scratch=[pltpu.VMEM((4, mine, ff), f32)], smem=1, name="final_up", keep_out=False,
-            cold=(2, 3, 4),
-        )
-        piece = [out((mine, head), f32)] + [out((mine, head), bf16)] * 3
-        *cut, og = call(
-            split_attn_body, (meta, v["a0"], v["xa0"], v["za3"]),
-            (*piece, out((mine, width), f32)),
-            scratch=[pltpu.VMEM((4 * mine, width + 128), f32)], smem=1, name="split_attn",
-            cold=(2, 3),
+        v.dxm, v.dxs = normed_back(v.dqkv)
+        parts["a"] = attn_grads
+        for k in range(4):
+            v["m%d" % k], v["a%d" % k] = mlp_grads[2 * k], attn_grads[k]
+        v.ym = swap_pair(v.tm)
+        for n, k in (('a', 4), ('a', 5), ('m', 3), ('m', 0)):
+            side("x%s%d" % (n, k), parts[n][2 * k + 1 if n == "m" else k], 3)
+        blk = width // BLOCKS
+        v.tx2 = add(v.dxm, swap_core(v.dxs))
+
+        def step(n, k):
+            across = v["xm%d" % k] if n == "m" else v["xa%d" % (4 + k // 3)]
+            if n == "a":
+                across = across[blk:] if k == 2 else across[:blk]
+            terms = [v["%s%d" % (n, k)], across]
+            if k > 1:
+                terms.append(v["z%s%d" % (n, k - 1)])
+            hop("z%s%d" % (n, k), add(*terms), 2)
+
+        for n, k in (('m', 1), ('a', 1), ('m', 2), ('a', 2), ('a', 3), ('m', 3)):
+            if (n, k) == ("a", 1):
+                v.sync("tx2", "a1")
+                v.yx2 = swap_pair(v.tx2)
+            if (n, k) == ("a", 2):
+                v.sync("ym", "tm", "a2")
+                v.e, dr = give()
+                v.eo = swap_core(v.e)
+            if (n, k) == ("a", 3):
+                v.sync("yx2", "tx2", "eo", "e", "a3")
+            if (n, k) == ("m", 3):
+                v.dx = take(dr)
+                v.dxo = swap_core(v.dx)
+                v.mixed = place_rows(tokens, v.e, v.eo, "place_mixed")
+                v.sync("mixed", "dxo", "dx", "m3")
+            step(n, k)
+        v.input_grad = place_rows(cotangent, v.dx, v.dxo, "place_input_grad")
+        v.sync("input_grad", "m0")
+        piece = [out((mine, head + ff), f32)] + [out((mine, head + ff), bf16)] * 3
+        *cut, down_grad, og = call(
+            split_body,
+            (meta, v.m0, v.xm0, v.zm3, v.a0, v.xa5, v.za3),
+            (*piece, out((4 * mine, width), f32), out((mine, width), f32)),
+            scratch=[pltpu.VMEM((4 * mine, ff), f32), pltpu.VMEM((4 * mine, head), f32)], smem=1,
+            name="split", cold=(2, 3, 5, 6),
         )
         cut = [cut[0]] + [flip_bit(cut[k], "grp", 4, k) for k in range(1, 4)]
         out_moved = lax.ppermute(og, ("seq", "grp"), swaps)
         out_grad = jnp.where(odd == 1, out_moved, og)
-        down_grad = v["w0"].astype(f32) + v["xw0"].astype(f32) + v["zw3"].astype(f32)
-        qkv_grad, small = call(
-            final_attn_body, (meta, *cut),
-            (out((mine, 3 * width), f32), out((8, 128), f32)),
-            scratch=[pltpu.VMEM((4, mine, head), f32)], smem=1, name="final_attn", keep_out=False,
+        qkv_grad, up_grad, small = call(
+            final_body, (meta, *cut),
+            (out((mine, 3 * width), f32), out((mine, units), f32), out((8, 128), f32)),
+            scratch=[pltpu.VMEM((4, mine, head + ff), f32)], smem=1, name="final", keep_out=False,
             cold=(2, 3, 4),
         )
         small = small[:3, :mine]
 
-    mixed = place_rows(tokens, v["e"], v["eo"], "place_mixed")
-    input_grad = place_rows(cotangent, v["dx"], v["dxo"], "place_input_grad")
-
     if native:
-        up_sum = native_scatter(up_grads)
-        down_grad = native_scatter(down_grads)
+        v.mixed = place_rows(tokens, v.e, v.eo, "place_mixed")
+        v.input_grad = place_rows(cotangent, v.dx, v.dxo, "place_input_grad")
+    mixed, input_grad = v.mixed, v.input_grad
+
+    if native:
+        mlp_sum = native_scatter(mlp_grads)
+        up_sum, down_grad = mlp_sum[:, :ff], mlp_sum[:, ff:]
         back = exchange([up_sum[j * mine : (j + 1) * mine] for j in range(4)], member)
         up_grad = jnp.stack([b.reshape(mine, seqs, ff // seqs) for b in back], axis=2)
         up_grad = up_grad.reshape(mine, units)

time: 240 us -> 230 us (0.958)
  waiting for transfers between devices: 99.9 us -> 114 us
  Pallas kernels: 64.1 us -> 52.6 us
  local copies, waits for them, and re-layouts: 16.3 us -> 10.1 us
  other arithmetic: 8.8 us -> 5.81 us
    ppermute x15 -> x12, waiting for transfers between devices: 28.5 us -> 65.1 us  [shift_one(): return lax.ppermute(v, 'seq', [(i, (i + 2) % seqs) for i in range(seqs)])]
    ppermute x47 -> x38, waiting for transfers between devices: 71.4 us -> 49.3 us  [flip_bit(): return lax.ppermute(v, axis, [(i, i ^ mask) for i in range(size)])]
    pallas_call x21 -> x18, Pallas kernels: 64.1 us -> 52.6 us  [call(): pl.pallas_call(body, out_shape=shapes, in_specs=[SM] * smem + [VM] * (len...]
    unnamed x104 -> x67, local copies, waits for them, and re-layouts: 12.5 us -> 6.23 us
    convert_element_type x15 -> x12, other arithmetic: 4.84 us -> 3.1 us  [add(): return total.astype(bf16)]
    ppermute x15 -> x12, starting transfers between devices: 12.2 us -> 10.6 us  [shift_one(): return lax.ppermute(v, 'seq', [(i, (i + 2) % seqs) for i in range(seqs)])]
    ppermute x47 -> x38, starting transfers between devices: 33 us -> 33.2 us  [flip_bit(): return lax.ppermute(v, axis, [(i, i ^ mask) for i in range(size)])]
  transfers between devices with their start and end apart: 64 -> 52, of which waited for: 27 -> 26; matrix products, arithmetic and copies ran while one was open for 4% -> 3% of each run, Pallas kernels for 21% -> 17%
where the time goes in v1:
time: 230 us; the launch traced here: 229 us
  waiting for transfers between devices  114 us (50%)
  Pallas kernels  52.6 us (23%)
  starting transfers between devices  45.1 us (20%)
  local copies, waits for them, and re-layouts  10.1 us (4%)
  other arithmetic  5.81 us (3%)
    ppermute x12, waiting for transfers between devices, shift_one(): return lax.ppermute(v, 'seq', [(i, (i + 2) % seqs) for i in range(seqs)])  65.1 us
    pallas_call x18, Pallas kernels, call(): pl.pallas_call(body, out_shape=shapes, in_specs=[SM] * smem + [VM] * (len...  52.6 us
    ppermute x38, waiting for transfers between devices, flip_bit(): return lax.ppermute(v, axis, [(i, i ^ mask) for i in range(size)])  49.3 us
    ppermute x38, starting transfers between devices, flip_bit(): return lax.ppermute(v, axis, [(i, i ^ mask) for i in range(size)])  33.2 us
    ppermute x12, starting transfers between devices, shift_one(): return lax.ppermute(v, 'seq', [(i, (i + 2) % seqs) for i in range(seqs)])  10.6 us
    unnamed x67, local copies, waits for them, and re-layouts  6.23 us
  transfers between devices with their start and end apart: 52, of which 26 were waited for; matrix products, arithmetic and copies ran while one was open for 3% of the time, Pallas kernels for 17%

profile of v1, /device:TPU:0, one launch (start us, length us, event | category | flops | bytes accessed | tf_op | source)
XLA Modules:
  0.0 229.2 jit_solution(14897472740891502659)
XLA Ops:
  8.5 3.0 %collective-permute-start.1 = (bf16[32,1920]{1,0:T(8,128)(2,1)S(1)}, bf16[32,1920]{1,0:T(8,128)(2,1)S(1)}, u32[]{:S(2)}, u32[]{:S(2)}) collective-permute-start(bf16[32,1920]{1,0:T(8,128)(2,1)S(1)} %get-tuple-element.163), channel_id=1, source_target_pairs={{0,2},{1,3},{2,0},{3,1},{4,6},{5,7},{6,4},{7,5},{8,10},{9,11},{10,... | collective-permute-start | bytes 368648 | tf_op jit(solution)/shard_map/ppermute | solution.py:449
  12.2 3.4 %collective-permute-done.1.c2 = bf16[32,1920]{1,0:T(8,128)(2,1)S(1)} collective-permute-done((bf16[32,1920]{1,0:T(8,128)(2,1)S(1)}, bf16[32,1920]{1,0:T(8,128)(2,1)S(1)}, u32[]{:S(2)}, u32[]{:S(2)}) %collective-permute-start.1) | collective-permute-done | bytes 122912 | tf_op jit(solution)/shard_map/ppermute | solution.py:449
  17.7 2.1 join.1
  24.6 7.0 %collective-permute-done.10.refs_2_ = bf16[128,1152]{1,0:T(8,128)(2,1)} collective-permute-done((bf16[128,1152]{1,0:T(8,128)(2,1)S(1)}, bf16[128,1152]{1,0:T(8,128)(2,1)}, u32[]{:S(2)}, u32[]{:S(2)}) %collective-permute-start.10) | collective-permute-done | bytes 294944 | tf_op jit(solution)/shard_map/ppermute | solution.py:465
  33.0 2.1 pick_cotangent.1
  38.1 4.3 %collective-permute-done.13.refs_4_ = bf16[128,1152]{1,0:T(8,128)(2,1)} collective-permute-done((bf16[128,1152]{1,0:T(8,128)(2,1)}, bf16[128,1152]{1,0:T(8,128)(2,1)}, u32[]{:S(2)}, u32[]{:S(2)}) %collective-permute-start.13) | collective-permute-done | bytes 294944 | tf_op jit(solution)/shard_map/ppermute | solution.py:465
  43.9 4.9 %collective-permute-done.12.refs_3_ = bf16[128,1152]{1,0:T(8,128)(2,1)} collective-permute-done((bf16[128,1152]{1,0:T(8,128)(2,1)}, bf16[128,1152]{1,0:T(8,128)(2,1)}, u32[]{:S(2)}, u32[]{:S(2)}) %collective-permute-start.12) | collective-permute-done | bytes 294944 | tf_op jit(solution)/shard_map/ppermute | solution.py:449
  50.2 4.3 %collective-permute-done.15.refs_6_ = bf16[128,1152]{1,0:T(8,128)(2,1)} collective-permute-done((bf16[128,1152]{1,0:T(8,128)(2,1)}, bf16[128,1152]{1,0:T(8,128)(2,1)}, u32[]{:S(2)}, u32[]{:S(2)}) %collective-permute-start.15) | collective-permute-done | bytes 294944 | tf_op jit(solution)/shard_map/ppermute | solution.py:465
  60.4 3.4 %collective-permute-done.7.refs_2_ = bf16[128,2048]{1,0:T(8,128)(2,1)} collective-permute-done((bf16[128,2048]{1,0:T(8,128)(2,1)}, bf16[128,2048]{1,0:T(8,128)(2,1)}, u32[]{:S(2)}, u32[]{:S(2)}) %collective-permute-start.7) | collective-permute-done | bytes 524320 | tf_op jit(solution)/shard_map/ppermute | solution.py:465
  65.3 8.3 %attn_fwd.1 = (bf16[512,1024]{1,0:T(8,128)(2,1)S(1)}, bf16[512,768]{1,0:T(8,128)(2,1)S(1)}, f32[8,256,256]{2,1,0:T(8,128)S(1)}, bf16[512,256]{1,0:T(8,128)(2,1)S...) custom-call(s32[8]{0:T(128)S(1)} %stack.83.idx, ...), custom_call_target="tpu_custom_call" | custom-call | flops 1073741824 | bytes 11309088 | tf_op jit(solution)/shard_map/attn_fwd/pallas_call | solution.py:49
  73.6 4.0 %collective-permute-done.22.refs_4_ = bf16[128,2048]{1,0:T(8,128)(2,1)S(1)} collective-permute-done((bf16[128,2048]{1,0:T(8,128)(2,1)}, bf16[128,2048]{1,0:T(8,128)(2,1)S(1)}, u32[]{:S(2)}, u32[]{:S(2)}) %collective-permute-start.22) | collective-permute-done | bytes 524320 | tf_op jit(solution)/shard_map/ppermute | solution.py:465
  81.3 9.1 %collective-permute-done.25.refs_6_ = bf16[128,2048]{1,0:T(8,128)(2,1)S(1)} collective-permute-done((bf16[128,2048]{1,0:T(8,128)(2,1)S(1)}, bf16[128,2048]{1,0:T(8,128)(2,1)S(1)}, u32[]{:S(2)}, u32[]{:S(2)}) %collective-permute-start.25) | collective-permute-done | bytes 524320 | tf_op jit(solution)/shard_map/ppermute | solution.py:465
  94.2 9.3 %collective-permute-done.26.refs_7_ = bf16[128,2048]{1,0:T(8,128)(2,1)S(1)} collective-permute-done((bf16[128,2048]{1,0:T(8,128)(2,1)S(1)}, bf16[128,2048]{1,0:T(8,128)(2,1)S(1)}, u32[]{:S(2)}, u32[]{:S(2)}) %collective-permute-start.26) | collective-permute-done | bytes 524320 | tf_op jit(solution)/shard_map/ppermute | solution.py:449
  104.5 8.9 %mlp.1 = (bf16[512,1024]{1,0:T(8,128)(2,1)S(1)}, bf16[512,1024]{1,0:T(8,128)(2,1)S(1)}, bf16[512,1024]{1,0:T(8,128)(2,1)S(1)}, bf16[1024,1024]{1,0:T(8,128)(2,1)...) custom-call(s32[8]{0:T(128)S(1)} %stack.83.idx, ...), custom_call_target="tpu_custom_call" | custom-call | flops 3221225472 | bytes 14942240 | tf_op jit(solution)/shard_map/mlp/pallas_call | solution.py:49
  113.4 1.9 collective-permute-done.27
  115.5 2.0 collective-permute-start.28
  117.5 7.9 %mlp_grad.1 = (bf16[256,1024]{1,0:T(8,128)(2,1)S(1)}, bf16[256,1024]{1,0:T(8,128)(2,1)S(1)}, f32[1024,128]{1,0:T(8,128)S(1)}, bf16[128,2048]{1,0:T(8,128)(2,1)S(...) custom-call(s32[8]{0:T(128)S(1)} %stack.83.idx, ...), custom_call_target="tpu_custom_call" | custom-call | flops 3221225472 | bytes 17563680 | tf_op jit(solution)/shard_map/mlp_grad/pallas_call | solution.py:49
  132.7 7.6 %collective-permute-done.42 = bf16[128,2048]{1,0:T(8,128)(2,1)S(1)} collective-permute-done((bf16[128,2048]{1,0:T(8,128)(2,1)S(1)}, bf16[128,2048]{1,0:T(8,128)(2,1)S(1)}, u32[]{:S(2)}, u32[]{:S(2)}) %collective-permute-start.42) | collective-permute-done | bytes 524320 | tf_op jit(solution)/shard_map/ppermute | solution.py:449
  140.7 7.2 %attn_bwd.1 = (bf16[512,768]{1,0:T(8,128)(2,1)S(1)}, bf16[128,1152]{1,0:T(8,128)(2,1)S(1)}, bf16[128,1152]{1,0:T(8,128)(2,1)S(1)}, bf16[128,1152]{1,0:T(8,128)(2...) custom-call(s32[8]{0:T(128)S(1)} %stack.83.idx, ...), custom_call_target="tpu_custom_call" | custom-call | flops 1610612736 | bytes 11272224 | tf_op jit(solution)/shard_map/attn_bwd/pallas_call | solution.py:49
  152.1 3.7 %collective-permute-done.43 = bf16[128,2048]{1,0:T(8,128)(2,1)S(1)} collective-permute-done((bf16[128,2048]{1,0:T(8,128)(2,1)S(1)}, bf16[128,2048]{1,0:T(8,128)(2,1)S(1)}, u32[]{:S(2)}, u32[]{:S(2)}) %collective-permute-start.43) | collective-permute-done | bytes 524320 | tf_op jit(solution)/shard_map/ppermute | solution.py:465
  156.7 9.1 %collective-permute-done.36 = bf16[256,1152]{1,0:T(8,128)(2,1)S(1)} collective-permute-done((bf16[256,1152]{1,0:T(8,128)(2,1)S(1)}, bf16[256,1152]{1,0:T(8,128)(2,1)S(1)}, u32[]{:S(2)}, u32[]{:S(2)}) %collective-permute-start.36) | collective-permute-done | bytes 589856 | tf_op jit(solution)/shard_map/ppermute | solution.py:449
  166.9 4.2 %collective-permute-start.44 = (bf16[128,2048]{1,0:T(8,128)(2,1)S(1)}, bf16[128,2048]{1,0:T(8,128)(2,1)S(1)}, u32[]{:S(2)}, u32[]{:S(2)}) collective-permute-start(bf16[128,2048]{1,0:T(8,128)(2,1)S(1)} %add_convert_fusion.1), channel_id=1, source_target_pairs={{0,8},{4,12},{8,16},{12,20},{16,24},{20,28},{24,0},{28,4},{1,9},{5... | collective-permute-start | bytes 1572872 | tf_op jit(solution)/shard_map/ppermute | solution.py:465
  171.9 5.7 %collective-permute-done.38 = bf16[128,1152]{1,0:T(8,128)(2,1)S(1)} collective-permute-done((bf16[128,1152]{1,0:T(8,128)(2,1)S(1)}, bf16[128,1152]{1,0:T(8,128)(2,1)S(1)}, u32[]{:S(2)}, u32[]{:S(2)}) %collective-permute-start.38) | collective-permute-done | bytes 294944 | tf_op jit(solution)/shard_map/ppermute | solution.py:465
  179.5 9.4 %collective-permute-done.44 = bf16[128,2048]{1,0:T(8,128)(2,1)S(1)} collective-permute-done((bf16[128,2048]{1,0:T(8,128)(2,1)S(1)}, bf16[128,2048]{1,0:T(8,128)(2,1)S(1)}, u32[]{:S(2)}, u32[]{:S(2)}) %collective-permute-start.44) | collective-permute-done | bytes 524320 | tf_op jit(solution)/shard_map/ppermute | solution.py:465
  189.9 2.6 %place_mixed.1 = bf16[2,512,1024]{2,1,0:T(8,128)(2,1)} custom-call(s32[5]{0:T(128)S(1)} %stack.74.meta, s32[2,1,256]{2,1,0:T(1,128)S(1)} %broadcast_in_dim.14.pos_ref, bf16[2,512,1024]{2,1,0:T(8,128)(2,1)S(1)} %copy-done.1, bf16[256,1024]{1,0:T(8,128)(2,1)S(1)} %get-tuple-element.254.own_ref, bf16[256,1024]{1,0:T(8,128)(2,1)S(1)} %collective-permute-done.34.oth_ref), custom_call_target="tpu_custom_call" | custom-call | flops 536870912 | bytes 5244948 | tf_op jit(solution)/shard_map/place_mixed/pallas_call | solution.py:49
  194.4 2.5 %collective-permute-start.47 = (bf16[128,1152]{1,0:T(8,128)(2,1)S(1)}, bf16[128,1152]{1,0:T(8,128)(2,1)S(1)}, u32[]{:S(2)}, u32[]{:S(2)}) collective-permute-start(bf16[128,1152]{1,0:T(8,128)(2,1)S(1)} %add_convert_fusion.9), channel_id=1, source_target_pairs={{0,8},{4,12},{8,16},{12,20},{16,24},{20,28},{24,0},{28,4},{1,9},{5... | collective-permute-start | bytes 884744 | tf_op jit(solution)/shard_map/ppermute | solution.py:465
  197.0 2.6 %place_input_grad.1 = bf16[2,512,1024]{2,1,0:T(8,128)(2,1)} custom-call(s32[5]{0:T(128)S(1)} %stack.74.meta, s32[2,1,256]{2,1,0:T(1,128)S(1)} %broadcast_in_dim.14.pos_ref, bf16[2,512,1024]{2,1,0:T(8,128)(2,1)S(1)} %copy-done.2, bf16[256,1024]{1,0:T(8,128)(2,1)S(1)} %input_grad.1.own_ref, bf16[256,1024]{1,0:T(8,128)(2,1)S(1)} %collective-permute-done.35.oth_ref), custom_call_target="tpu_custom_call" | custom-call | flops 536870912 | bytes 5244948 | tf_op jit(solution)/shard_map/place_input_grad/pallas_call | solution.py:49
  199.5 1.8 collective-permute-done.37.m1
  201.4 13.1 %collective-permute-done.47.a2 = bf16[128,1152]{1,0:T(8,128)(2,1)S(1)} collective-permute-done((bf16[128,1152]{1,0:T(8,128)(2,1)S(1)}, bf16[128,1152]{1,0:T(8,128)(2,1)S(1)}, u32[]{:S(2)}, u32[]{:S(2)}) %collective-permute-start.47) | collective-permute-done | bytes 294944 | tf_op jit(solution)/shard_map/ppermute | solution.py:465
  215.3 1.9 split.1
  220.6 2.9 %collective-permute-done.49.c2 = bf16[32,1920]{1,0:T(8,128)(2,1)S(1)} collective-permute-done((bf16[32,1920]{1,0:T(8,128)(2,1)S(1)}, bf16[32,1920]{1,0:T(8,128)(2,1)S(1)}, u32[]{:S(2)}, u32[]{:S(2)}) %collective-permute-start.49) | collective-permute-done | bytes 122912 | tf_op jit(solution)/shard_map/ppermute | solution.py:449
  225.8 2.2 final.1
  (189 shorter events, 65.8 us)
Async XLA Ops:
  21.6 14.9 %collective-permute-start.11 = (bf16[128,2048]{1,0:T(8,128)(2,1)}, bf16[128,2048]{1,0:T(8,128)(2,1)S(1)}, u32[]{:S(2)}, u32[]{:S(2)}) collective-permute-start(bf16[128,2048]{1,0:T(8,128)(2,1)} %get-tuple-element.171.refs_0_), channel_id=1, source_target_pairs={{0,4},{4,0},{8,12},{12,8},{16,20},{20,16},{24,28},{28,24},{1,5},{5... | collective-permute-start | bytes 1572872 | tf_op jit(solution)/shard_map/ppermute | solution.py:449
  23.2 19.5 %collective-permute-start.5 = (bf16[256,1024]{1,0:T(8,128)(2,1)S(1)}, bf16[256,1024]{1,0:T(8,128)(2,1)S(1)}, u32[]{:S(2)}, u32[]{:S(2)}) collective-permute-start(bf16[256,1024]{1,0:T(8,128)(2,1)S(1)} %add_convert_fusion.8), channel_id=1, source_target_pairs={{0,2},{1,3},{2,0},{3,1},{4,6},{5,7},{6,4},{7,5},{8,10},{9,11},{10,... | collective-permute-start | bytes 1572872 | tf_op jit(solution)/shard_map/ppermute | solution.py:449
  35.2 22.4 %collective-permute-start.8 = (bf16[256,1024]{1,0:T(8,128)(2,1)}, bf16[256,1024]{1,0:T(8,128)(2,1)}, u32[]{:S(2)}, u32[]{:S(2)}) collective-permute-start(bf16[256,1024]{1,0:T(8,128)(2,1)} %get-tuple-element.175), channel_id=1, source_target_pairs={{0,1},{1,0},{2,3},{3,2},{4,5},{5,4},{6,7},{7,6},{8,9},{9,8},{10,11... | collective-permute-start | bytes 1572872 | tf_op jit(solution)/shard_map/ppermute | solution.py:449
  36.6 12.3 %collective-permute-start.12 = (bf16[128,1152]{1,0:T(8,128)(2,1)}, bf16[128,1152]{1,0:T(8,128)(2,1)}, u32[]{:S(2)}, u32[]{:S(2)}) collective-permute-start(bf16[128,1152]{1,0:T(8,128)(2,1)} %collective-permute-done.10.refs_2_), channel_id=1, source_target_pairs={{0,4},{4,0},{8,12},{12,8},{16,20},{20,16},{24,28},{28,24},{1,5},{5... | collective-permute-start | bytes 884744 | tf_op jit(solution)/shard_map/ppermute | solution.py:449
  42.5 12.1 %collective-permute-start.15 = (bf16[128,1152]{1,0:T(8,128)(2,1)}, bf16[128,1152]{1,0:T(8,128)(2,1)}, u32[]{:S(2)}, u32[]{:S(2)}) collective-permute-start(bf16[128,1152]{1,0:T(8,128)(2,1)} %collective-permute-done.13.refs_4_), channel_id=1, source_target_pairs={{0,8},{4,12},{8,16},{12,20},{16,24},{20,28},{24,0},{28,4},{1,9},{5... | collective-permute-start | bytes 884744 | tf_op jit(solution)/shard_map/ppermute | solution.py:465
  42.7 21.0 %collective-permute-start.7 = (bf16[128,2048]{1,0:T(8,128)(2,1)}, bf16[128,2048]{1,0:T(8,128)(2,1)}, u32[]{:S(2)}, u32[]{:S(2)}) collective-permute-start(bf16[128,2048]{1,0:T(8,128)(2,1)} %get-tuple-element.171.refs_0_), channel_id=1, source_target_pairs={{0,8},{4,12},{8,16},{12,20},{16,24},{20,28},{24,0},{28,4},{1,9},{5... | collective-permute-start | bytes 1572872 | tf_op jit(solution)/shard_map/ppermute | solution.py:465
  43.0 22.3 %collective-permute-start.6 = (bf16[256,1024]{1,0:T(8,128)(2,1)S(1)}, bf16[256,1024]{1,0:T(8,128)(2,1)}, u32[]{:S(2)}, u32[]{:S(2)}) collective-permute-start(bf16[256,1024]{1,0:T(8,128)(2,1)S(1)} %add.96.xo_ref.x_ref), channel_id=1, source_target_pairs={{0,1},{1,0},{2,3},{3,2},{4,5},{5,4},{6,7},{7,6},{8,9},{9,8},{10,11... | collective-permute-start | bytes 1572872 | tf_op jit(solution)/shard_map/ppermute | solution.py:449
  48.8 14.9 %collective-permute-start.14 = (bf16[128,1152]{1,0:T(8,128)(2,1)}, bf16[128,1152]{1,0:T(8,128)(2,1)S(1)}, u32[]{:S(2)}, u32[]{:S(2)}) collective-permute-start(bf16[128,1152]{1,0:T(8,128)(2,1)} %collective-permute-done.13.refs_4_), channel_id=1, source_target_pairs={{0,4},{4,0},{8,12},{12,8},{16,20},{20,16},{24,28},{28,24},{1,5},{5... | collective-permute-start | bytes 884744 | tf_op jit(solution)/shard_map/ppermute | solution.py:449
  58.8 18.8 %collective-permute-start.20 = (bf16[256,1024]{1,0:T(8,128)(2,1)S(1)}, bf16[256,1024]{1,0:T(8,128)(2,1)S(1)}, u32[]{:S(2)}, u32[]{:S(2)}) collective-permute-start(bf16[256,1024]{1,0:T(8,128)(2,1)S(1)} %add_convert_fusion.7), channel_id=1, source_target_pairs={{0,2},{1,3},{2,0},{3,1},{4,6},{5,7},{6,4},{7,5},{8,10},{9,11},{10,... | collective-permute-start | bytes 1572872 | tf_op jit(solution)/shard_map/ppermute | solution.py:449
  63.7 13.9 %collective-permute-start.22 = (bf16[128,2048]{1,0:T(8,128)(2,1)}, bf16[128,2048]{1,0:T(8,128)(2,1)S(1)}, u32[]{:S(2)}, u32[]{:S(2)}) collective-permute-start(bf16[128,2048]{1,0:T(8,128)(2,1)} %collective-permute-done.7.refs_2_), channel_id=1, source_target_pairs={{0,8},{4,12},{8,16},{12,20},{16,24},{20,28},{24,0},{28,4},{1,9},{5... | collective-permute-start | bytes 1572872 | tf_op jit(solution)/shard_map/ppermute | solution.py:465
  63.7 15.7 %collective-permute-start.18 = (bf16[128,2048]{1,0:T(8,128)(2,1)}, bf16[128,2048]{1,0:T(8,128)(2,1)S(1)}, u32[]{:S(2)}, u32[]{:S(2)}) collective-permute-start(bf16[128,2048]{1,0:T(8,128)(2,1)} %collective-permute-done.7.refs_2_), channel_id=1, source_target_pairs={{0,4},{4,0},{8,12},{12,8},{16,20},{20,16},{24,28},{28,24},{1,5},{5... | collective-permute-start | bytes 1572872 | tf_op jit(solution)/shard_map/ppermute | solution.py:449
  77.6 12.8 %collective-permute-start.25 = (bf16[128,2048]{1,0:T(8,128)(2,1)S(1)}, bf16[128,2048]{1,0:T(8,128)(2,1)S(1)}, u32[]{:S(2)}, u32[]{:S(2)}) collective-permute-start(bf16[128,2048]{1,0:T(8,128)(2,1)S(1)} %collective-permute-done.22.refs_4_), channel_id=1, source_target_pairs={{0,8},{4,12},{8,16},{12,20},{16,24},{20,28},{24,0},{28,4},{1,9},{5... | collective-permute-start | bytes 1572872 | tf_op jit(solution)/shard_map/ppermute | solution.py:465
  77.9 14.0 %collective-permute-start.21 = (bf16[256,1024]{1,0:T(8,128)(2,1)S(1)}, bf16[256,1024]{1,0:T(8,128)(2,1)S(1)}, u32[]{:S(2)}, u32[]{:S(2)}) collective-permute-start(bf16[256,1024]{1,0:T(8,128)(2,1)S(1)} %add.99.co_ref.c_ref), channel_id=1, source_target_pairs={{0,1},{1,0},{2,3},{3,2},{4,5},{5,4},{6,7},{7,6},{8,9},{9,8},{10,11... | collective-permute-start | bytes 1572872 | tf_op jit(solution)/shard_map/ppermute | solution.py:449
  77.9 14.8 %collective-permute-start.23 = (bf16[128,2048]{1,0:T(8,128)(2,1)S(1)}, bf16[128,2048]{1,0:T(8,128)(2,1)S(1)}, u32[]{:S(2)}, u32[]{:S(2)}) collective-permute-start(bf16[128,2048]{1,0:T(8,128)(2,1)S(1)} %collective-permute-done.22.refs_4_), channel_id=1, source_target_pairs={{0,4},{4,0},{8,12},{12,8},{16,20},{20,16},{24,28},{28,24},{1,5},{5... | collective-permute-start | bytes 1572872 | tf_op jit(solution)/shard_map/ppermute | solution.py:449
  79.7 14.1 %collective-permute-start.19 = (bf16[256,1024]{1,0:T(8,128)(2,1)S(1)}, bf16[256,1024]{1,0:T(8,128)(2,1)S(1)}, u32[]{:S(2)}, u32[]{:S(2)}) collective-permute-start(bf16[256,1024]{1,0:T(8,128)(2,1)S(1)} %add_convert_fusion.6.t_ref.bt_ref.at_ref), channel_id=1, source_target_pairs={{0,2},{1,3},{2,0},{3,1},{4,6},{5,7},{6,4},{7,5},{8,10},{9,11},{10,... | collective-permute-start | bytes 1572872 | tf_op jit(solution)/shard_map/ppermute | solution.py:449
  90.4 13.1 %collective-permute-start.26 = (bf16[128,2048]{1,0:T(8,128)(2,1)S(1)}, bf16[128,2048]{1,0:T(8,128)(2,1)S(1)}, u32[]{:S(2)}, u32[]{:S(2)}) collective-permute-start(bf16[128,2048]{1,0:T(8,128)(2,1)S(1)} %collective-permute-done.25.refs_6_), channel_id=1, source_target_pairs={{0,4},{4,0},{8,12},{12,8},{16,20},{20,16},{24,28},{28,24},{1,5},{5... | collective-permute-start | bytes 1572872 | tf_op jit(solution)/shard_map/ppermute | solution.py:449
  115.5 14.2 %collective-permute-start.28 = (bf16[256,1024]{1,0:T(8,128)(2,1)S(1)}, bf16[256,1024]{1,0:T(8,128)(2,1)S(1)}, u32[]{:S(2)}, u32[]{:S(2)}) collective-permute-start(bf16[256,1024]{1,0:T(8,128)(2,1)S(1)} %add_convert_fusion.5.dt_ref), channel_id=1, source_target_pairs={{0,2},{1,3},{2,0},{3,1},{4,6},{5,7},{6,4},{7,5},{8,10},{9,11},{10,... | collective-permute-start | bytes 1572872 | tf_op jit(solution)/shard_map/ppermute | solution.py:449
  125.5 14.8 %collective-permute-start.42 = (bf16[128,2048]{1,0:T(8,128)(2,1)S(1)}, bf16[128,2048]{1,0:T(8,128)(2,1)S(1)}, u32[]{:S(2)}, u32[]{:S(2)}) collective-permute-start(bf16[128,2048]{1,0:T(8,128)(2,1)S(1)} %get-tuple-element.283), channel_id=1, source_target_pairs={{0,4},{4,0},{8,12},{12,8},{16,20},{20,16},{24,28},{28,24},{1,5},{5... | collective-permute-start | bytes 1572872 | tf_op jit(solution)/shard_map/ppermute | solution.py:449
  127.2 23.8 %collective-permute-start.40 = (bf16[128,2048]{1,0:T(8,128)(2,1)S(1)}, bf16[128,2048]{1,0:T(8,128)(2,1)S(1)}, u32[]{:S(2)}, u32[]{:S(2)}) collective-permute-start(bf16[128,2048]{1,0:T(8,128)(2,1)S(1)} %get-tuple-element.278), channel_id=1, source_target_pairs={{0,4},{4,0},{8,12},{12,8},{16,20},{20,16},{24,28},{28,24},{1,5},{5... | collective-permute-start | bytes 1572872 | tf_op jit(solution)/shard_map/ppermute | solution.py:449
  130.9 24.9 %collective-permute-start.33 = (bf16[256,1024]{1,0:T(8,128)(2,1)S(1)}, bf16[256,1024]{1,0:T(8,128)(2,1)S(1)}, u32[]{:S(2)}, u32[]{:S(2)}) collective-permute-start(bf16[256,1024]{1,0:T(8,128)(2,1)S(1)} %add_convert_fusion.3.mt_ref), channel_id=1, source_target_pairs={{0,2},{1,3},{2,0},{3,1},{4,6},{5,7},{6,4},{7,5},{8,10},{9,11},{10,... | collective-permute-start | bytes 1572872 | tf_op jit(solution)/shard_map/ppermute | solution.py:449
  140.4 15.4 %collective-permute-start.43 = (bf16[128,2048]{1,0:T(8,128)(2,1)S(1)}, bf16[128,2048]{1,0:T(8,128)(2,1)S(1)}, u32[]{:S(2)}, u32[]{:S(2)}) collective-permute-start(bf16[128,2048]{1,0:T(8,128)(2,1)S(1)} %add_convert_fusion.2), channel_id=1, source_target_pairs={{0,8},{4,12},{8,16},{12,20},{16,24},{20,28},{24,0},{28,4},{1,9},{5... | collective-permute-start | bytes 1572872 | tf_op jit(solution)/shard_map/ppermute | solution.py:465
  149.6 16.2 %collective-permute-start.36 = (bf16[256,1152]{1,0:T(8,128)(2,1)S(1)}, bf16[256,1152]{1,0:T(8,128)(2,1)S(1)}, u32[]{:S(2)}, u32[]{:S(2)}) collective-permute-start(bf16[256,1152]{1,0:T(8,128)(2,1)S(1)} %get-tuple-element.267), channel_id=1, source_target_pairs={{0,4},{4,0},{8,12},{12,8},{16,20},{20,16},{24,28},{28,24},{1,5},{5... | collective-permute-start | bytes 1769480 | tf_op jit(solution)/shard_map/ppermute | solution.py:449
  151.0 42.6 %collective-permute-start.41 = (bf16[128,2048]{1,0:T(8,128)(2,1)S(1)}, bf16[128,2048]{1,0:T(8,128)(2,1)S(1)}, u32[]{:S(2)}, u32[]{:S(2)}) collective-permute-start(bf16[128,2048]{1,0:T(8,128)(2,1)S(1)} %get-tuple-element.281), channel_id=1, source_target_pairs={{0,4},{4,0},{8,12},{12,8},{16,20},{20,16},{24,28},{28,24},{1,5},{5... | collective-permute-start | bytes 1572872 | tf_op jit(solution)/shard_map/ppermute | solution.py:449
  156.2 14.9 %collective-permute-start.34 = (bf16[256,1024]{1,0:T(8,128)(2,1)S(1)}, bf16[256,1024]{1,0:T(8,128)(2,1)S(1)}, u32[]{:S(2)}, u32[]{:S(2)}) collective-permute-start(bf16[256,1024]{1,0:T(8,128)(2,1)S(1)} %get-tuple-element.254.own_ref), channel_id=1, source_target_pairs={{0,1},{1,0},{2,3},{3,2},{4,5},{5,4},{6,7},{7,6},{8,9},{9,8},{10,11... | collective-permute-start | bytes 1572872 | tf_op jit(solution)/shard_map/ppermute | solution.py:449
  156.5 14.6 %collective-permute-start.31 = (bf16[256,1024]{1,0:T(8,128)(2,1)S(1)}, bf16[256,1024]{1,0:T(8,128)(2,1)S(1)}, u32[]{:S(2)}, u32[]{:S(2)}) collective-permute-start(bf16[256,1024]{1,0:T(8,128)(2,1)S(1)} %add_convert_fusion.4.t_ref), channel_id=1, source_target_pairs={{0,2},{1,3},{2,0},{3,1},{4,6},{5,7},{6,4},{7,5},{8,10},{9,11},{10,... | collective-permute-start | bytes 1572872 | tf_op jit(solution)/shard_map/ppermute | solution.py:449
  166.9 22.0 %collective-permute-start.44 = (bf16[128,2048]{1,0:T(8,128)(2,1)S(1)}, bf16[128,2048]{1,0:T(8,128)(2,1)S(1)}, u32[]{:S(2)}, u32[]{:S(2)}) collective-permute-start(bf16[128,2048]{1,0:T(8,128)(2,1)S(1)} %add_convert_fusion.1), channel_id=1, source_target_pairs={{0,8},{4,12},{8,16},{12,20},{16,24},{20,28},{24,0},{28,4},{1,9},{5... | collective-permute-start | bytes 1572872 | tf_op jit(solution)/shard_map/ppermute | solution.py:465
  171.8 21.8 %collective-permute-start.35 = (bf16[256,1024]{1,0:T(8,128)(2,1)S(1)}, bf16[256,1024]{1,0:T(8,128)(2,1)S(1)}, u32[]{:S(2)}, u32[]{:S(2)}) collective-permute-start(bf16[256,1024]{1,0:T(8,128)(2,1)S(1)} %input_grad.1.own_ref), channel_id=1, source_target_pairs={{0,1},{1,0},{2,3},{3,2},{4,5},{5,4},{6,7},{7,6},{8,9},{9,8},{10,11... | collective-permute-start | bytes 1572872 | tf_op jit(solution)/shard_map/ppermute | solution.py:449
  177.7 15.9 %collective-permute-start.39 = (bf16[128,1152]{1,0:T(8,128)(2,1)S(1)}, bf16[128,1152]{1,0:T(8,128)(2,1)S(1)}, u32[]{:S(2)}, u32[]{:S(2)}) collective-permute-start(bf16[128,1152]{1,0:T(8,128)(2,1)S(1)} %add_convert_fusion.10), channel_id=1, source_target_pairs={{0,8},{4,12},{8,16},{12,20},{16,24},{20,28},{24,0},{28,4},{1,9},{5... | collective-permute-start | bytes 884744 | tf_op jit(solution)/shard_map/ppermute | solution.py:465
  178.4 15.9 %collective-permute-start.46 = (bf16[256,1152]{1,0:T(8,128)(2,1)S(1)}, bf16[256,1152]{1,0:T(8,128)(2,1)S(1)}, u32[]{:S(2)}, u32[]{:S(2)}) collective-permute-start(bf16[256,1152]{1,0:T(8,128)(2,1)S(1)} %get-tuple-element.294), channel_id=1, source_target_pairs={{0,4},{4,0},{8,12},{12,8},{16,20},{20,16},{24,28},{28,24},{1,5},{5... | collective-permute-start | bytes 1769480 | tf_op jit(solution)/shard_map/ppermute | solution.py:449
  188.9 12.5 %collective-permute-start.37 = (bf16[128,2048]{1,0:T(8,128)(2,1)S(1)}, bf16[128,2048]{1,0:T(8,128)(2,1)S(1)}, u32[]{:S(2)}, u32[]{:S(2)}) collective-permute-start(bf16[128,2048]{1,0:T(8,128)(2,1)S(1)} %get-tuple-element.270), channel_id=1, source_target_pairs={{0,4},{4,0},{8,12},{12,8},{16,20},{20,16},{24,28},{28,24},{1,5},{5... | collective-permute-start | bytes 1572872 | tf_op jit(solution)/shard_map/ppermute | solution.py:449
  193.9 20.6 %collective-permute-start.45 = (bf16[128,2048]{1,0:T(8,128)(2,1)S(1)}, bf16[128,2048]{1,0:T(8,128)(2,1)S(1)}, u32[]{:S(2)}, u32[]{:S(2)}) collective-permute-start(bf16[128,2048]{1,0:T(8,128)(2,1)S(1)} %add_convert_fusion), channel_id=1, source_target_pairs={{0,8},{4,12},{8,16},{12,20},{16,24},{20,28},{24,0},{28,4},{1,9},{5... | collective-permute-start | bytes 1572872 | tf_op jit(solution)/shard_map/ppermute | solution.py:465
  194.4 20.0 %collective-permute-start.47 = (bf16[128,1152]{1,0:T(8,128)(2,1)S(1)}, bf16[128,1152]{1,0:T(8,128)(2,1)S(1)}, u32[]{:S(2)}, u32[]{:S(2)}) collective-permute-start(bf16[128,1152]{1,0:T(8,128)(2,1)S(1)} %add_convert_fusion.9), channel_id=1, source_target_pairs={{0,8},{4,12},{8,16},{12,20},{16,24},{20,28},{24,0},{28,4},{1,9},{5... | collective-permute-start | bytes 884744 | tf_op jit(solution)/shard_map/ppermute | solution.py:465
  (53 other events, 497.6 us)

commit v2 on v1

--- a/solution.py
+++ b/solution.py
@@ -212,38 +212,55 @@
     lax.fori_loop(0, width // tile, step2, 0)
 
 
-def mlp_grad_body(
-    idx, g_ref, du_ref, db_ref, mo_ref, mt_ref, wu_ref, wd_ref, gcol, ao_ref, at_ref, co_ref,
-    ct_ref, xo_ref, xt_ref, *refs
+EARLY, LATE = (2, 3, 4, 5), (0, 1, 6, 7)
+
+
+def grad_block(idx, b, ref, fm_ref, fg_ref, du_ref, db_ref, wu_ref, gcol, col_ref):
+    width, units = fm_ref.shape[0], fg_ref.shape[0]
+    blk, sub = width // BLOCKS, units // BLOCKS
+    off = pl.ds(pl.multiple_of(idx[b] * blk, blk), blk)
+    grad = mm(fm_ref[off, :], du_ref[...])
+    ref[:, :units] = grad.astype(bf16)
+    gain = jnp.sum(grad * wu_ref[off, :].astype(f32), axis=-1, keepdims=True)
+    gain = gain / gcol[off, 1:2].astype(f32)
+    col_ref[off, :] = jnp.broadcast_to(gain, (blk, 128))
+    off = pl.ds(pl.multiple_of(idx[b] * sub, sub), sub)
+    ref[:, units:] = mm(fg_ref[off, :], db_ref[...]).astype(bf16)
+
+
+def early_grad_body(
+    idx, g_ref, du_ref, db_ref, mo_ref, mt_ref, wu_ref, gcol, col_ref, fm_ref, fg_ref, *grads
 ):
-    bo_ref, bt_ref, col_ref = refs[:3]
-    grads, (flip,) = refs[3 : 3 + BLOCKS], refs[3 + BLOCKS :]
     rows, width = mo_ref.shape
-    units = wu_ref.shape[1]
-    blk, sub = width // BLOCKS, units // BLOCKS
     tile = 256
 
     def turn_rows(i, carry):
         cols = pl.ds(pl.multiple_of(i * tile, tile), tile)
-        flip[cols, :rows] = mo_ref[:, cols].T
-        flip[cols, rows:] = mt_ref[:, cols].T
+        fm_ref[cols, :rows] = mo_ref[:, cols].T
+        fm_ref[cols, rows:] = mt_ref[:, cols].T
+        fg_ref[cols, :] = g_ref[:, cols].T
         return carry
 
     lax.fori_loop(0, width // tile, turn_rows, 0)
-    for b, ref in enumerate(grads):
-        off = pl.ds(pl.multiple_of(idx[b] * blk, blk), blk)
-        grad = mm(flip[off, :], du_ref[...])
-        ref[:, :units] = grad.astype(bf16)
-        gain = jnp.sum(grad * wu_ref[off, :].astype(f32), axis=-1, keepdims=True)
-        gain = gain / gcol[off, 1:2].astype(f32)
-        col_ref[off, :] = jnp.broadcast_to(gain, (blk, 128))
+    for b, ref in zip(EARLY, grads):
+        grad_block(idx, b, ref, fm_ref, fg_ref, du_ref, db_ref, wu_ref, gcol, col_ref)
+
+
+def late_grad_body(
+    idx, g_ref, du_ref, db_ref, wu_ref, wd_ref, gcol, col_in, fm_ref, fg_ref, ao_ref, at_ref,
+    co_ref, ct_ref, xo_ref, xt_ref, bo_ref, bt_ref, col_ref, *grads
+):
+    rows, width = bo_ref.shape
+    tile = 256
+    col_ref[...] = col_in[...]
+    for b, ref in zip(LATE, grads):
+        grad_block(idx, b, ref, fm_ref, fg_ref, du_ref, db_ref, wu_ref, gcol, col_ref)
 
     def step(i, carry):
         cols = pl.ds(pl.multiple_of(i * tile, tile), tile)
         res = mm(g_ref[...], wd_ref[:, cols])
         bo_ref[:, cols] = res[:rows].astype(bf16)
         bt_ref[:, cols] = res[rows:].astype(bf16)
-        flip[cols, :] = g_ref[:, cols].T
         own, other = carry
         own += jnp.sum(
             (res[:rows] + ao_ref[:, cols].astype(f32)) * co_ref[:, cols].astype(f32),
@@ -257,9 +274,6 @@
 
     zero = jnp.zeros((rows, 1), f32)
     dots = lax.fori_loop(0, width // tile, step, (zero, zero))
-    for b, ref in enumerate(grads):
-        off = pl.multiple_of(idx[b] * sub, sub)
-        ref[:, units:] = mm(flip[pl.ds(off, sub), :], db_ref[...]).astype(bf16)
     lane = lax.broadcasted_iota(jnp.int32, (rows, 128), 1)
     route = jnp.zeros((width, 128), f32)
     for d, x_ref in zip(dots, (xo_ref, xt_ref)):
@@ -717,22 +731,36 @@
     v.td = add(dm_o, swap_core(dm_t))
     v.sync("td", "du")
     v.yd = swap_pair(v.td)
-    bm_o, bm_t, cols, *mlp_grads = call(
-        mlp_grad_body,
+    packet = out((width // BLOCKS, ff + width), bf16)
+    col, turned_m, turned_g, *first = call(
+        early_grad_body,
+        (order, g, v.du, db, v.h, v.ho, w_up, gain_cols),
         (
-            order, g, v.du, db, v.h, v.ho, w_up, w_down, gain_cols, ba_o, ba_t, v.c,
-            v.co, v.x, v.xo,
+            out((width, 128), f32), out((width, both), bf16), out((ff, both), bf16),
+            *([packet] * 4),
         ),
+        smem=1,
+        flops=2 * both * width * ff,
+        name="early_grad",
+        cold=(5,),
+    )
+    v.g = g
+    v.f0, v.f1 = first[1], first[3]
+    v.sync("f0", "f1", "g")
+    first[1], first[3] = v.f0, v.f1
+    bm_o, bm_t, cols, *last = call(
+        late_grad_body,
         (
-            half, half, out((width, 128), f32),
-            *([out((width // BLOCKS, ff + width), bf16)] * BLOCKS),
+            order, v.g, v.du, db, w_up, w_down, gain_cols, col, turned_m, turned_g, ba_o, ba_t,
+            v.c, v.co, v.x, v.xo,
         ),
-        scratch=[pltpu.VMEM((width, both), bf16)],
+        (half, half, out((width, 128), f32), *([packet] * 4)),
         smem=1,
-        flops=6 * both * width * ff,
-        name="mlp_grad",
-        cold=(5, 11, 12, 13, 14),
-    )
+        flops=4 * both * width * ff,
+        name="late_grad",
+        cold=(12, 13, 14, 15),
+    )
+    mlp_grads = [*last[:2], *first, *last[2:]]
     v.bm, v.bn = bm_o, bm_t
     v.tm = add(v.bm, swap_core(v.bn))
     parts = {"m": mlp_grads}
@@ -741,7 +769,7 @@
     v.__dict__.update({n + str(k): None for n in ("xm", "xa") for k in range(4)})
     if not native:
         for n, k in (('m', 1), ('m', 2)):
-            side("x%s%d" % (n, k), parts[n][2 * k + 1], 3)
+            side("x%s%d" % (n, k), parts[n][2 * k + 1], 2)
     v.sync("yd", "td", "bm")
     da_own, dh = call(
         hidden_grad_body,
@@ -824,8 +852,8 @@
         for k in range(4):
             v["m%d" % k], v["a%d" % k] = mlp_grads[2 * k], attn_grads[k]
         v.ym = swap_pair(v.tm)
-        for n, k in (('a', 4), ('a', 5), ('m', 3), ('m', 0)):
-            side("x%s%d" % (n, k), parts[n][2 * k + 1 if n == "m" else k], 3)
+        for n, k in (('m', 3), ('a', 4), ('m', 0), ('a', 5)):
+            side("x%s%d" % (n, k), parts[n][2 * k + 1 if n == "m" else k], 2)
         blk = width // BLOCKS
         v.tx2 = add(v.dxm, swap_core(v.dxs))
 
@@ -838,7 +866,7 @@
                 terms.append(v["z%s%d" % (n, k - 1)])
             hop("z%s%d" % (n, k), add(*terms), 2)
 
-        for n, k in (('m', 1), ('a', 1), ('m', 2), ('a', 2), ('a', 3), ('m', 3)):
+        for n, k in (('m', 1), ('m', 2), ('a', 1), ('a', 2), ('a', 3), ('m', 3)):
             if (n, k) == ("a", 1):
                 v.sync("tx2", "a1")
                 v.yx2 = swap_pair(v.tx2)
@@ -846,8 +874,6 @@
                 v.sync("ym", "tm", "a2")
                 v.e, dr = give()
                 v.eo = swap_core(v.e)
-            if (n, k) == ("a", 3):
-                v.sync("yx2", "tx2", "eo", "e", "a3")
             if (n, k) == ("m", 3):
                 v.dx = take(dr)
                 v.dxo = swap_core(v.dx)

time: 230 us -> 221 us (0.961)
  waiting for transfers between devices: 114 us -> 107 us
  starting transfers between devices: 45.1 us -> 42.4 us
    ppermute x12, waiting for transfers between devices: 65.1 us -> 45.2 us  [shift_one(): return lax.ppermute(v, 'seq', [(i, (i + 2) % seqs) for i in range(seqs)])]
    ppermute x38, waiting for transfers between devices: 49.3 us -> 61.8 us  [flip_bit(): return lax.ppermute(v, axis, [(i, i ^ mask) for i in range(size)])]
    ppermute x12, starting transfers between devices: 10.6 us -> 7.75 us  [shift_one(): return lax.ppermute(v, 'seq', [(i, (i + 2) % seqs) for i in range(seqs)])]
    pallas_call x18 -> x19, Pallas kernels: 52.6 us -> 53.6 us  [call(): pl.pallas_call(body, out_shape=shapes, in_specs=[SM] * smem + [VM] * (len...]
  transfers between devices with their start and end apart: 52 -> 52, of which waited for: 26 -> 27; matrix products, arithmetic and copies ran while one was open for 3% -> 3% of each run, Pallas kernels for 17% -> 18%
where the time goes in v2:
time: 221 us; the launch traced here: 220 us
  waiting for transfers between devices  107 us (48%)
  Pallas kernels  53.6 us (24%)
  starting transfers between devices  42.4 us (19%)
  local copies, waits for them, and re-layouts  10 us (5%)
  other arithmetic  5.88 us (3%)
    ppermute x38, waiting for transfers between devices, flip_bit(): return lax.ppermute(v, axis, [(i, i ^ mask) for i in range(size)])  61.8 us
    pallas_call x19, Pallas kernels, call(): pl.pallas_call(body, out_shape=shapes, in_specs=[SM] * smem + [VM] * (len...  53.6 us
    ppermute x12, waiting for transfers between devices, shift_one(): return lax.ppermute(v, 'seq', [(i, (i + 2) % seqs) for i in range(seqs)])  45.2 us
    ppermute x38, starting transfers between devices, flip_bit(): return lax.ppermute(v, axis, [(i, i ^ mask) for i in range(size)])  33.3 us
    ppermute x12, starting transfers between devices, shift_one(): return lax.ppermute(v, 'seq', [(i, (i + 2) % seqs) for i in range(seqs)])  7.75 us
    unnamed x67, local copies, waits for them, and re-layouts  6.23 us
  transfers between devices with their start and end apart: 52, of which 27 were waited for; matrix products, arithmetic and copies ran while one was open for 3% of the time, Pallas kernels for 18%

profile of v2, /device:TPU:0, one launch (start us, length us, event | category | flops | bytes accessed | tf_op | source)
XLA Modules:
  0.0 220.1 jit_solution(14620009633537757561)
XLA Ops:
  8.5 3.0 %collective-permute-start.1 = (bf16[32,1920]{1,0:T(8,128)(2,1)S(1)}, bf16[32,1920]{1,0:T(8,128)(2,1)S(1)}, u32[]{:S(2)}, u32[]{:S(2)}) collective-permute-start(bf16[32,1920]{1,0:T(8,128)(2,1)S(1)} %get-tuple-element.167), channel_id=1, source_target_pairs={{0,2},{1,3},{2,0},{3,1},{4,6},{5,7},{6,4},{7,5},{8,10},{9,11},{10,... | collective-permute-start | bytes 368648 | tf_op jit(solution)/shard_map/ppermute | solution.py:463
  12.2 3.4 %collective-permute-done.1.c2 = bf16[32,1920]{1,0:T(8,128)(2,1)S(1)} collective-permute-done((bf16[32,1920]{1,0:T(8,128)(2,1)S(1)}, bf16[32,1920]{1,0:T(8,128)(2,1)S(1)}, u32[]{:S(2)}, u32[]{:S(2)}) %collective-permute-start.1) | collective-permute-done | bytes 122912 | tf_op jit(solution)/shard_map/ppermute | solution.py:463
  17.7 2.1 join.1
  24.6 7.0 %collective-permute-done.10.refs_2_ = bf16[128,1152]{1,0:T(8,128)(2,1)} collective-permute-done((bf16[128,1152]{1,0:T(8,128)(2,1)S(1)}, bf16[128,1152]{1,0:T(8,128)(2,1)}, u32[]{:S(2)}, u32[]{:S(2)}) %collective-permute-start.10) | collective-permute-done | bytes 294944 | tf_op jit(solution)/shard_map/ppermute | solution.py:479
  33.1 2.1 pick_cotangent.1
  38.1 4.3 %collective-permute-done.13.refs_4_ = bf16[128,1152]{1,0:T(8,128)(2,1)} collective-permute-done((bf16[128,1152]{1,0:T(8,128)(2,1)}, bf16[128,1152]{1,0:T(8,128)(2,1)}, u32[]{:S(2)}, u32[]{:S(2)}) %collective-permute-start.13) | collective-permute-done | bytes 294944 | tf_op jit(solution)/shard_map/ppermute | solution.py:479
  43.9 4.9 %collective-permute-done.12.refs_3_ = bf16[128,1152]{1,0:T(8,128)(2,1)} collective-permute-done((bf16[128,1152]{1,0:T(8,128)(2,1)}, bf16[128,1152]{1,0:T(8,128)(2,1)}, u32[]{:S(2)}, u32[]{:S(2)}) %collective-permute-start.12) | collective-permute-done | bytes 294944 | tf_op jit(solution)/shard_map/ppermute | solution.py:463
  50.2 4.3 %collective-permute-done.15.refs_6_ = bf16[128,1152]{1,0:T(8,128)(2,1)} collective-permute-done((bf16[128,1152]{1,0:T(8,128)(2,1)}, bf16[128,1152]{1,0:T(8,128)(2,1)}, u32[]{:S(2)}, u32[]{:S(2)}) %collective-permute-start.15) | collective-permute-done | bytes 294944 | tf_op jit(solution)/shard_map/ppermute | solution.py:479
  60.4 3.4 %collective-permute-done.7.refs_2_ = bf16[128,2048]{1,0:T(8,128)(2,1)} collective-permute-done((bf16[128,2048]{1,0:T(8,128)(2,1)}, bf16[128,2048]{1,0:T(8,128)(2,1)}, u32[]{:S(2)}, u32[]{:S(2)}) %collective-permute-start.7) | collective-permute-done | bytes 524320 | tf_op jit(solution)/shard_map/ppermute | solution.py:479
  65.3 8.2 %attn_fwd.1 = (bf16[512,1024]{1,0:T(8,128)(2,1)S(1)}, bf16[512,768]{1,0:T(8,128)(2,1)S(1)}, f32[8,256,256]{2,1,0:T(8,128)S(1)}, bf16[512,256]{1,0:T(8,128)(2,1)S...) custom-call(s32[8]{0:T(128)S(1)} %stack.83.idx, ...), custom_call_target="tpu_custom_call" | custom-call | flops 1073741824 | bytes 11309088 | tf_op jit(solution)/shard_map/attn_fwd/pallas_call | solution.py:49
  73.6 4.0 %collective-permute-done.22.refs_4_ = bf16[128,2048]{1,0:T(8,128)(2,1)S(1)} collective-permute-done((bf16[128,2048]{1,0:T(8,128)(2,1)}, bf16[128,2048]{1,0:T(8,128)(2,1)S(1)}, u32[]{:S(2)}, u32[]{:S(2)}) %collective-permute-start.22) | collective-permute-done | bytes 524320 | tf_op jit(solution)/shard_map/ppermute | solution.py:479
  81.3 9.1 %collective-permute-done.25.refs_6_ = bf16[128,2048]{1,0:T(8,128)(2,1)S(1)} collective-permute-done((bf16[128,2048]{1,0:T(8,128)(2,1)S(1)}, bf16[128,2048]{1,0:T(8,128)(2,1)S(1)}, u32[]{:S(2)}, u32[]{:S(2)}) %collective-permute-start.25) | collective-permute-done | bytes 524320 | tf_op jit(solution)/shard_map/ppermute | solution.py:479
  94.2 9.3 %collective-permute-done.26.refs_7_ = bf16[128,2048]{1,0:T(8,128)(2,1)S(1)} collective-permute-done((bf16[128,2048]{1,0:T(8,128)(2,1)S(1)}, bf16[128,2048]{1,0:T(8,128)(2,1)S(1)}, u32[]{:S(2)}, u32[]{:S(2)}) %collective-permute-start.26) | collective-permute-done | bytes 524320 | tf_op jit(solution)/shard_map/ppermute | solution.py:463
  104.5 8.8 %mlp.1 = (bf16[512,1024]{1,0:T(8,128)(2,1)S(1)}, bf16[512,1024]{1,0:T(8,128)(2,1)S(1)}, bf16[512,1024]{1,0:T(8,128)(2,1)S(1)}, bf16[1024,1024]{1,0:T(8,128)(2,1)...) custom-call(s32[8]{0:T(128)S(1)} %stack.83.idx, ...), custom_call_target="tpu_custom_call" | custom-call | flops 3221225472 | bytes 14942240 | tf_op jit(solution)/shard_map/mlp/pallas_call | solution.py:49
  115.4 2.0 collective-permute-start.30
  117.4 3.2 %early_grad.1 = (f32[1024,128]{1,0:T(8,128)S(1)}, bf16[1024,512]{1,0:T(8,128)(2,1)S(1)}, bf16[1024,512]{1,0:T(8,128)(2,1)S(1)}, bf16[128,2048]{1,0:T(8,128)(2,1)...) custom-call(s32[8]{0:T(128)S(1)} %stack.83.idx, ...), custom_call_target="tpu_custom_call" | custom-call | flops 1073741824 | bytes 11272224 | tf_op jit(solution)/shard_map/early_grad/pallas_call | solution.py:49
  121.7 5.8 %late_grad.1 = (bf16[256,1024]{1,0:T(8,128)(2,1)S(1)}, bf16[256,1024]{1,0:T(8,128)(2,1)S(1)}, f32[1024,128]{1,0:T(8,128)S(1)}, bf16[128,2048]{1,0:T(8,128)(2,1)S...) custom-call(s32[8]{0:T(128)S(1)} %stack.83.idx, ...), custom_call_target="tpu_custom_call" | custom-call | flops 2147483648 | bytes 17039392 | tf_op jit(solution)/shard_map/late_grad/pallas_call | solution.py:49
  127.5 2.1 collective-permute-done.30.du_ref
  132.1 2.9 %collective-permute-done.36 = bf16[128,2048]{1,0:T(8,128)(2,1)S(1)} collective-permute-done((bf16[128,2048]{1,0:T(8,128)(2,1)S(1)}, bf16[128,2048]{1,0:T(8,128)(2,1)S(1)}, u32[]{:S(2)}, u32[]{:S(2)}) %collective-permute-start.36) | collective-permute-done | bytes 524320 | tf_op jit(solution)/shard_map/ppermute | solution.py:463
  136.0 7.2 %attn_bwd.1 = (bf16[512,768]{1,0:T(8,128)(2,1)S(1)}, bf16[128,1152]{1,0:T(8,128)(2,1)S(1)}, bf16[128,1152]{1,0:T(8,128)(2,1)S(1)}, bf16[128,1152]{1,0:T(8,128)(2...) custom-call(s32[8]{0:T(128)S(1)} %stack.83.idx, ...), custom_call_target="tpu_custom_call" | custom-call | flops 1610612736 | bytes 11272224 | tf_op jit(solution)/shard_map/attn_bwd/pallas_call | solution.py:49
  147.7 1.9 collective-permute-done.40
  150.8 10.4 %collective-permute-done.42 = bf16[256,1152]{1,0:T(8,128)(2,1)S(1)} collective-permute-done((bf16[256,1152]{1,0:T(8,128)(2,1)S(1)}, bf16[256,1152]{1,0:T(8,128)(2,1)S(1)}, u32[]{:S(2)}, u32[]{:S(2)}) %collective-permute-start.42) | collective-permute-done | bytes 589856 | tf_op jit(solution)/shard_map/ppermute | solution.py:463
  163.3 7.4 %collective-permute-done.34.u_ref = bf16[256,1024]{1,0:T(8,128)(2,1)S(1)} collective-permute-done((bf16[256,1024]{1,0:T(8,128)(2,1)S(1)}, bf16[256,1024]{1,0:T(8,128)(2,1)S(1)}, u32[]{:S(2)}, u32[]{:S(2)}) %collective-permute-start.34) | collective-permute-done | bytes 524320 | tf_op jit(solution)/shard_map/ppermute | solution.py:463
  175.9 2.6 %place_mixed.1 = bf16[2,512,1024]{2,1,0:T(8,128)(2,1)} custom-call(s32[5]{0:T(128)S(1)} %stack.74.meta, s32[2,1,256]{2,1,0:T(1,128)S(1)} %broadcast_in_dim.14.pos_ref, bf16[2,512,1024]{2,1,0:T(8,128)(2,1)S(1)} %copy-done.4, bf16[256,1024]{1,0:T(8,128)(2,1)S(1)} %get-tuple-element.257.own_ref, bf16[256,1024]{1,0:T(8,128)(2,1)S(1)} %collective-permute-done.32.oth_ref), custom_call_target="tpu_custom_call" | custom-call | flops 536870912 | bytes 5244948 | tf_op jit(solution)/shard_map/place_mixed/pallas_call | solution.py:49
  178.4 4.7 %collective-permute-done.44 = bf16[128,1152]{1,0:T(8,128)(2,1)S(1)} collective-permute-done((bf16[128,1152]{1,0:T(8,128)(2,1)S(1)}, bf16[128,1152]{1,0:T(8,128)(2,1)S(1)}, u32[]{:S(2)}, u32[]{:S(2)}) %collective-permute-start.44) | collective-permute-done | bytes 294944 | tf_op jit(solution)/shard_map/ppermute | solution.py:479
  183.8 4.7 %collective-permute-done.46.a1 = bf16[256,1152]{1,0:T(8,128)(2,1)S(1)} collective-permute-done((bf16[256,1152]{1,0:T(8,128)(2,1)S(1)}, bf16[256,1152]{1,0:T(8,128)(2,1)S(1)}, u32[]{:S(2)}, u32[]{:S(2)}) %collective-permute-start.46) | collective-permute-done | bytes 589856 | tf_op jit(solution)/shard_map/ppermute | solution.py:463
  188.6 4.3 %collective-permute-start.47 = (bf16[128,1152]{1,0:T(8,128)(2,1)S(1)}, bf16[128,1152]{1,0:T(8,128)(2,1)S(1)}, u32[]{:S(2)}, u32[]{:S(2)}) collective-permute-start(bf16[128,1152]{1,0:T(8,128)(2,1)S(1)} %add_convert_fusion.9), channel_id=1, source_target_pairs={{0,8},{4,12},{8,16},{12,20},{16,24},{20,28},{24,0},{28,4},{1,9},{5... | collective-permute-start | bytes 884744 | tf_op jit(solution)/shard_map/ppermute | solution.py:479
  192.9 2.6 %place_input_grad.1 = bf16[2,512,1024]{2,1,0:T(8,128)(2,1)} custom-call(s32[5]{0:T(128)S(1)} %stack.74.meta, s32[2,1,256]{2,1,0:T(1,128)S(1)} %broadcast_in_dim.14.pos_ref, bf16[2,512,1024]{2,1,0:T(8,128)(2,1)S(1)} %copy-done.5, bf16[256,1024]{1,0:T(8,128)(2,1)S(1)} %input_grad.1.own_ref, bf16[256,1024]{1,0:T(8,128)(2,1)S(1)} %collective-permute-done.35.oth_ref), custom_call_target="tpu_custom_call" | custom-call | flops 536870912 | bytes 5244948 | tf_op jit(solution)/shard_map/place_input_grad/pallas_call | solution.py:49
  195.5 3.4 %collective-permute-done.38.m1 = bf16[128,2048]{1,0:T(8,128)(2,1)S(1)} collective-permute-done((bf16[128,2048]{1,0:T(8,128)(2,1)S(1)}, bf16[128,2048]{1,0:T(8,128)(2,1)S(1)}, u32[]{:S(2)}, u32[]{:S(2)}) %collective-permute-start.38) | collective-permute-done | bytes 524320 | tf_op jit(solution)/shard_map/ppermute | solution.py:463
  198.9 6.4 %collective-permute-done.47.a2 = bf16[128,1152]{1,0:T(8,128)(2,1)S(1)} collective-permute-done((bf16[128,1152]{1,0:T(8,128)(2,1)S(1)}, bf16[128,1152]{1,0:T(8,128)(2,1)S(1)}, u32[]{:S(2)}, u32[]{:S(2)}) %collective-permute-start.47) | collective-permute-done | bytes 294944 | tf_op jit(solution)/shard_map/ppermute | solution.py:479
  211.5 2.9 %collective-permute-done.49.c2 = bf16[32,1920]{1,0:T(8,128)(2,1)S(1)} collective-permute-done((bf16[32,1920]{1,0:T(8,128)(2,1)S(1)}, bf16[32,1920]{1,0:T(8,128)(2,1)S(1)}, u32[]{:S(2)}, u32[]{:S(2)}) %collective-permute-start.49) | collective-permute-done | bytes 122912 | tf_op jit(solution)/shard_map/ppermute | solution.py:463
  216.7 2.2 final.1
  (190 shorter events, 68.4 us)
Async XLA Ops:
  7.9 11.9 %collective-permute-start.4 = (bf16[256,1024]{1,0:T(8,128)(2,1)S(1)}, bf16[256,1024]{1,0:T(8,128)(2,1)S(1)}, u32[]{:S(2)}, u32[]{:S(2)}) collective-permute-start(bf16[256,1024]{1,0:T(8,128)(2,1)S(1)} %get-tuple-element.173), channel_id=1, source_target_pairs={{0,1},{1,0},{2,3},{3,2},{4,5},{5,4},{6,7},{7,6},{8,9},{9,8},{10,11... | collective-permute-start | bytes 1572872 | tf_op jit(solution)/shard_map/ppermute | solution.py:463
  21.6 14.9 %collective-permute-start.11 = (bf16[128,2048]{1,0:T(8,128)(2,1)}, bf16[128,2048]{1,0:T(8,128)(2,1)S(1)}, u32[]{:S(2)}, u32[]{:S(2)}) collective-permute-start(bf16[128,2048]{1,0:T(8,128)(2,1)} %get-tuple-element.175.refs_0_), channel_id=1, source_target_pairs={{0,4},{4,0},{8,12},{12,8},{16,20},{20,16},{24,28},{28,24},{1,5},{5... | collective-permute-start | bytes 1572872 | tf_op jit(solution)/shard_map/ppermute | solution.py:463
  23.2 19.5 %collective-permute-start.5 = (bf16[256,1024]{1,0:T(8,128)(2,1)S(1)}, bf16[256,1024]{1,0:T(8,128)(2,1)S(1)}, u32[]{:S(2)}, u32[]{:S(2)}) collective-permute-start(bf16[256,1024]{1,0:T(8,128)(2,1)S(1)} %add_convert_fusion.8), channel_id=1, source_target_pairs={{0,2},{1,3},{2,0},{3,1},{4,6},{5,7},{6,4},{7,5},{8,10},{9,11},{10,... | collective-permute-start | bytes 1572872 | tf_op jit(solution)/shard_map/ppermute | solution.py:463
  35.2 22.4 %collective-permute-start.8 = (bf16[256,1024]{1,0:T(8,128)(2,1)}, bf16[256,1024]{1,0:T(8,128)(2,1)}, u32[]{:S(2)}, u32[]{:S(2)}) collective-permute-start(bf16[256,1024]{1,0:T(8,128)(2,1)} %get-tuple-element.179), channel_id=1, source_target_pairs={{0,1},{1,0},{2,3},{3,2},{4,5},{5,4},{6,7},{7,6},{8,9},{9,8},{10,11... | collective-permute-start | bytes 1572872 | tf_op jit(solution)/shard_map/ppermute | solution.py:463
  36.6 12.3 %collective-permute-start.12 = (bf16[128,1152]{1,0:T(8,128)(2,1)}, bf16[128,1152]{1,0:T(8,128)(2,1)}, u32[]{:S(2)}, u32[]{:S(2)}) collective-permute-start(bf16[128,1152]{1,0:T(8,128)(2,1)} %collective-permute-done.10.refs_2_), channel_id=1, source_target_pairs={{0,4},{4,0},{8,12},{12,8},{16,20},{20,16},{24,28},{28,24},{1,5},{5... | collective-permute-start | bytes 884744 | tf_op jit(solution)/shard_map/ppermute | solution.py:463
  42.5 12.1 %collective-permute-start.15 = (bf16[128,1152]{1,0:T(8,128)(2,1)}, bf16[128,1152]{1,0:T(8,128)(2,1)}, u32[]{:S(2)}, u32[]{:S(2)}) collective-permute-start(bf16[128,1152]{1,0:T(8,128)(2,1)} %collective-permute-done.13.refs_4_), channel_id=1, source_target_pairs={{0,8},{4,12},{8,16},{12,20},{16,24},{20,28},{24,0},{28,4},{1,9},{5... | collective-permute-start | bytes 884744 | tf_op jit(solution)/shard_map/ppermute | solution.py:479
  42.7 21.0 %collective-permute-start.7 = (bf16[128,2048]{1,0:T(8,128)(2,1)}, bf16[128,2048]{1,0:T(8,128)(2,1)}, u32[]{:S(2)}, u32[]{:S(2)}) collective-permute-start(bf16[128,2048]{1,0:T(8,128)(2,1)} %get-tuple-element.175.refs_0_), channel_id=1, source_target_pairs={{0,8},{4,12},{8,16},{12,20},{16,24},{20,28},{24,0},{28,4},{1,9},{5... | collective-permute-start | bytes 1572872 | tf_op jit(solution)/shard_map/ppermute | solution.py:479
  43.0 22.3 %collective-permute-start.6 = (bf16[256,1024]{1,0:T(8,128)(2,1)S(1)}, bf16[256,1024]{1,0:T(8,128)(2,1)}, u32[]{:S(2)}, u32[]{:S(2)}) collective-permute-start(bf16[256,1024]{1,0:T(8,128)(2,1)S(1)} %add.96.xo_ref.x_ref), channel_id=1, source_target_pairs={{0,1},{1,0},{2,3},{3,2},{4,5},{5,4},{6,7},{7,6},{8,9},{9,8},{10,11... | collective-permute-start | bytes 1572872 | tf_op jit(solution)/shard_map/ppermute | solution.py:463
  48.8 14.9 %collective-permute-start.14 = (bf16[128,1152]{1,0:T(8,128)(2,1)}, bf16[128,1152]{1,0:T(8,128)(2,1)S(1)}, u32[]{:S(2)}, u32[]{:S(2)}) collective-permute-start(bf16[128,1152]{1,0:T(8,128)(2,1)} %collective-permute-done.13.refs_4_), channel_id=1, source_target_pairs={{0,4},{4,0},{8,12},{12,8},{16,20},{20,16},{24,28},{28,24},{1,5},{5... | collective-permute-start | bytes 884744 | tf_op jit(solution)/shard_map/ppermute | solution.py:463
  58.8 18.9 %collective-permute-start.20 = (bf16[256,1024]{1,0:T(8,128)(2,1)S(1)}, bf16[256,1024]{1,0:T(8,128)(2,1)S(1)}, u32[]{:S(2)}, u32[]{:S(2)}) collective-permute-start(bf16[256,1024]{1,0:T(8,128)(2,1)S(1)} %add_convert_fusion.7), channel_id=1, source_target_pairs={{0,2},{1,3},{2,0},{3,1},{4,6},{5,7},{6,4},{7,5},{8,10},{9,11},{10,... | collective-permute-start | bytes 1572872 | tf_op jit(solution)/shard_map/ppermute | solution.py:463
  63.7 13.9 %collective-permute-start.22 = (bf16[128,2048]{1,0:T(8,128)(2,1)}, bf16[128,2048]{1,0:T(8,128)(2,1)S(1)}, u32[]{:S(2)}, u32[]{:S(2)}) collective-permute-start(bf16[128,2048]{1,0:T(8,128)(2,1)} %collective-permute-done.7.refs_2_), channel_id=1, source_target_pairs={{0,8},{4,12},{8,16},{12,20},{16,24},{20,28},{24,0},{28,4},{1,9},{5... | collective-permute-start | bytes 1572872 | tf_op jit(solution)/shard_map/ppermute | solution.py:479
  63.8 15.7 %collective-permute-start.18 = (bf16[128,2048]{1,0:T(8,128)(2,1)}, bf16[128,2048]{1,0:T(8,128)(2,1)S(1)}, u32[]{:S(2)}, u32[]{:S(2)}) collective-permute-start(bf16[128,2048]{1,0:T(8,128)(2,1)} %collective-permute-done.7.refs_2_), channel_id=1, source_target_pairs={{0,4},{4,0},{8,12},{12,8},{16,20},{20,16},{24,28},{28,24},{1,5},{5... | collective-permute-start | bytes 1572872 | tf_op jit(solution)/shard_map/ppermute | solution.py:463
  77.6 12.8 %collective-permute-start.25 = (bf16[128,2048]{1,0:T(8,128)(2,1)S(1)}, bf16[128,2048]{1,0:T(8,128)(2,1)S(1)}, u32[]{:S(2)}, u32[]{:S(2)}) collective-permute-start(bf16[128,2048]{1,0:T(8,128)(2,1)S(1)} %collective-permute-done.22.refs_4_), channel_id=1, source_target_pairs={{0,8},{4,12},{8,16},{12,20},{16,24},{20,28},{24,0},{28,4},{1,9},{5... | collective-permute-start | bytes 1572872 | tf_op jit(solution)/shard_map/ppermute | solution.py:479
  77.9 14.0 %collective-permute-start.21 = (bf16[256,1024]{1,0:T(8,128)(2,1)S(1)}, bf16[256,1024]{1,0:T(8,128)(2,1)S(1)}, u32[]{:S(2)}, u32[]{:S(2)}) collective-permute-start(bf16[256,1024]{1,0:T(8,128)(2,1)S(1)} %add.99.co_ref.c_ref), channel_id=1, source_target_pairs={{0,1},{1,0},{2,3},{3,2},{4,5},{5,4},{6,7},{7,6},{8,9},{9,8},{10,11... | collective-permute-start | bytes 1572872 | tf_op jit(solution)/shard_map/ppermute | solution.py:463
  77.9 14.8 %collective-permute-start.23 = (bf16[128,2048]{1,0:T(8,128)(2,1)S(1)}, bf16[128,2048]{1,0:T(8,128)(2,1)S(1)}, u32[]{:S(2)}, u32[]{:S(2)}) collective-permute-start(bf16[128,2048]{1,0:T(8,128)(2,1)S(1)} %collective-permute-done.22.refs_4_), channel_id=1, source_target_pairs={{0,4},{4,0},{8,12},{12,8},{16,20},{20,16},{24,28},{28,24},{1,5},{5... | collective-permute-start | bytes 1572872 | tf_op jit(solution)/shard_map/ppermute | solution.py:463
  79.7 14.1 %collective-permute-start.19 = (bf16[256,1024]{1,0:T(8,128)(2,1)S(1)}, bf16[256,1024]{1,0:T(8,128)(2,1)S(1)}, u32[]{:S(2)}, u32[]{:S(2)}) collective-permute-start(bf16[256,1024]{1,0:T(8,128)(2,1)S(1)} %add_convert_fusion.6.t_ref.bt_ref.at_ref), channel_id=1, source_target_pairs={{0,2},{1,3},{2,0},{3,1},{4,6},{5,7},{6,4},{7,5},{8,10},{9,11},{10,... | collective-permute-start | bytes 1572872 | tf_op jit(solution)/shard_map/ppermute | solution.py:463
  90.4 13.1 %collective-permute-start.26 = (bf16[128,2048]{1,0:T(8,128)(2,1)S(1)}, bf16[128,2048]{1,0:T(8,128)(2,1)S(1)}, u32[]{:S(2)}, u32[]{:S(2)}) collective-permute-start(bf16[128,2048]{1,0:T(8,128)(2,1)S(1)} %collective-permute-done.25.refs_6_), channel_id=1, source_target_pairs={{0,4},{4,0},{8,12},{12,8},{16,20},{20,16},{24,28},{28,24},{1,5},{5... | collective-permute-start | bytes 1572872 | tf_op jit(solution)/shard_map/ppermute | solution.py:463
  115.4 14.2 %collective-permute-start.30 = (bf16[256,1024]{1,0:T(8,128)(2,1)S(1)}, bf16[256,1024]{1,0:T(8,128)(2,1)S(1)}, u32[]{:S(2)}, u32[]{:S(2)}) collective-permute-start(bf16[256,1024]{1,0:T(8,128)(2,1)S(1)} %add_convert_fusion.5.dt_ref), channel_id=1, source_target_pairs={{0,2},{1,3},{2,0},{3,1},{4,6},{5,7},{6,4},{7,5},{8,10},{9,11},{10,... | collective-permute-start | bytes 1572872 | tf_op jit(solution)/shard_map/ppermute | solution.py:463
  120.6 14.4 %collective-permute-start.36 = (bf16[128,2048]{1,0:T(8,128)(2,1)S(1)}, bf16[128,2048]{1,0:T(8,128)(2,1)S(1)}, u32[]{:S(2)}, u32[]{:S(2)}) collective-permute-start(bf16[128,2048]{1,0:T(8,128)(2,1)S(1)} %get-tuple-element.272), channel_id=1, source_target_pairs={{0,4},{4,0},{8,12},{12,8},{16,20},{20,16},{24,28},{28,24},{1,5},{5... | collective-permute-start | bytes 1572872 | tf_op jit(solution)/shard_map/ppermute | solution.py:463
  130.5 15.0 %collective-permute-start.39 = (bf16[128,2048]{1,0:T(8,128)(2,1)S(1)}, bf16[128,2048]{1,0:T(8,128)(2,1)S(1)}, u32[]{:S(2)}, u32[]{:S(2)}) collective-permute-start(bf16[128,2048]{1,0:T(8,128)(2,1)S(1)} %get-tuple-element.280), channel_id=1, source_target_pairs={{0,4},{4,0},{8,12},{12,8},{16,20},{20,16},{24,28},{28,24},{1,5},{5... | collective-permute-start | bytes 1572872 | tf_op jit(solution)/shard_map/ppermute | solution.py:463
  131.9 12.9 %collective-permute-start.28 = (bf16[256,1024]{1,0:T(8,128)(2,1)S(1)}, bf16[256,1024]{1,0:T(8,128)(2,1)S(1)}, u32[]{:S(2)}, u32[]{:S(2)}) collective-permute-start(bf16[256,1024]{1,0:T(8,128)(2,1)S(1)} %get-tuple-element.240), channel_id=1, source_target_pairs={{0,1},{1,0},{2,3},{3,2},{4,5},{5,4},{6,7},{7,6},{8,9},{9,8},{10,11... | collective-permute-start | bytes 1572872 | tf_op jit(solution)/shard_map/ppermute | solution.py:463
  135.1 14.5 %collective-permute-start.40 = (bf16[128,2048]{1,0:T(8,128)(2,1)S(1)}, bf16[128,2048]{1,0:T(8,128)(2,1)S(1)}, u32[]{:S(2)}, u32[]{:S(2)}) collective-permute-start(bf16[128,2048]{1,0:T(8,128)(2,1)S(1)} %add_convert_fusion.2), channel_id=1, source_target_pairs={{0,8},{4,12},{8,16},{12,20},{16,24},{20,28},{24,0},{28,4},{1,9},{5... | collective-permute-start | bytes 1572872 | tf_op jit(solution)/shard_map/ppermute | solution.py:479
  145.6 17.2 %collective-permute-start.29 = (bf16[256,1024]{1,0:T(8,128)(2,1)S(1)}, bf16[256,1024]{1,0:T(8,128)(2,1)S(1)}, u32[]{:S(2)}, u32[]{:S(2)}) collective-permute-start(bf16[256,1024]{1,0:T(8,128)(2,1)S(1)} %add_convert_fusion.4.mt_ref), channel_id=1, source_target_pairs={{0,2},{1,3},{2,0},{3,1},{4,6},{5,7},{6,4},{7,5},{8,10},{9,11},{10,... | collective-permute-start | bytes 1572872 | tf_op jit(solution)/shard_map/ppermute | solution.py:463
  146.6 14.6 %collective-permute-start.42 = (bf16[256,1152]{1,0:T(8,128)(2,1)S(1)}, bf16[256,1152]{1,0:T(8,128)(2,1)S(1)}, u32[]{:S(2)}, u32[]{:S(2)}) collective-permute-start(bf16[256,1152]{1,0:T(8,128)(2,1)S(1)} %get-tuple-element.288), channel_id=1, source_target_pairs={{0,4},{4,0},{8,12},{12,8},{16,20},{20,16},{24,28},{28,24},{1,5},{5... | collective-permute-start | bytes 1769480 | tf_op jit(solution)/shard_map/ppermute | solution.py:463
  149.9 13.4 %collective-permute-start.41 = (bf16[128,2048]{1,0:T(8,128)(2,1)S(1)}, bf16[128,2048]{1,0:T(8,128)(2,1)S(1)}, u32[]{:S(2)}, u32[]{:S(2)}) collective-permute-start(bf16[128,2048]{1,0:T(8,128)(2,1)S(1)} %add_convert_fusion.1), channel_id=1, source_target_pairs={{0,8},{4,12},{8,16},{12,20},{16,24},{20,28},{24,0},{28,4},{1,9},{5... | collective-permute-start | bytes 1572872 | tf_op jit(solution)/shard_map/ppermute | solution.py:479
  150.2 20.5 %collective-permute-start.34 = (bf16[256,1024]{1,0:T(8,128)(2,1)S(1)}, bf16[256,1024]{1,0:T(8,128)(2,1)S(1)}, u32[]{:S(2)}, u32[]{:S(2)}) collective-permute-start(bf16[256,1024]{1,0:T(8,128)(2,1)S(1)} %add_convert_fusion.3.t_ref), channel_id=1, source_target_pairs={{0,2},{1,3},{2,0},{3,1},{4,6},{5,7},{6,4},{7,5},{8,10},{9,11},{10,... | collective-permute-start | bytes 1572872 | tf_op jit(solution)/shard_map/ppermute | solution.py:463
  161.6 13.3 %collective-permute-start.37 = (bf16[128,2048]{1,0:T(8,128)(2,1)S(1)}, bf16[128,2048]{1,0:T(8,128)(2,1)S(1)}, u32[]{:S(2)}, u32[]{:S(2)}) collective-permute-start(bf16[128,2048]{1,0:T(8,128)(2,1)S(1)} %get-tuple-element.275), channel_id=1, source_target_pairs={{0,4},{4,0},{8,12},{12,8},{16,20},{20,16},{24,28},{28,24},{1,5},{5... | collective-permute-start | bytes 1572872 | tf_op jit(solution)/shard_map/ppermute | solution.py:463
  163.3 12.6 %collective-permute-start.32 = (bf16[256,1024]{1,0:T(8,128)(2,1)S(1)}, bf16[256,1024]{1,0:T(8,128)(2,1)S(1)}, u32[]{:S(2)}, u32[]{:S(2)}) collective-permute-start(bf16[256,1024]{1,0:T(8,128)(2,1)S(1)} %get-tuple-element.257.own_ref), channel_id=1, source_target_pairs={{0,1},{1,0},{2,3},{3,2},{4,5},{5,4},{6,7},{7,6},{8,9},{9,8},{10,11... | collective-permute-start | bytes 1572872 | tf_op jit(solution)/shard_map/ppermute | solution.py:463
  172.3 16.2 %collective-permute-start.46 = (bf16[256,1152]{1,0:T(8,128)(2,1)S(1)}, bf16[256,1152]{1,0:T(8,128)(2,1)S(1)}, u32[]{:S(2)}, u32[]{:S(2)}) collective-permute-start(bf16[256,1152]{1,0:T(8,128)(2,1)S(1)} %get-tuple-element.302), channel_id=1, source_target_pairs={{0,4},{4,0},{8,12},{12,8},{16,20},{20,16},{24,28},{28,24},{1,5},{5... | collective-permute-start | bytes 1769480 | tf_op jit(solution)/shard_map/ppermute | solution.py:463
  174.9 24.0 %collective-permute-start.38 = (bf16[128,2048]{1,0:T(8,128)(2,1)S(1)}, bf16[128,2048]{1,0:T(8,128)(2,1)S(1)}, u32[]{:S(2)}, u32[]{:S(2)}) collective-permute-start(bf16[128,2048]{1,0:T(8,128)(2,1)S(1)} %get-tuple-element.278), channel_id=1, source_target_pairs={{0,4},{4,0},{8,12},{12,8},{16,20},{20,16},{24,28},{28,24},{1,5},{5... | collective-permute-start | bytes 1572872 | tf_op jit(solution)/shard_map/ppermute | solution.py:463
  183.4 21.9 %collective-permute-start.45 = (bf16[128,2048]{1,0:T(8,128)(2,1)S(1)}, bf16[128,2048]{1,0:T(8,128)(2,1)S(1)}, u32[]{:S(2)}, u32[]{:S(2)}) collective-permute-start(bf16[128,2048]{1,0:T(8,128)(2,1)S(1)} %add_convert_fusion), channel_id=1, source_target_pairs={{0,8},{4,12},{8,16},{12,20},{16,24},{20,28},{24,0},{28,4},{1,9},{5... | collective-permute-start | bytes 1572872 | tf_op jit(solution)/shard_map/ppermute | solution.py:479
  188.6 16.7 %collective-permute-start.47 = (bf16[128,1152]{1,0:T(8,128)(2,1)S(1)}, bf16[128,1152]{1,0:T(8,128)(2,1)S(1)}, u32[]{:S(2)}, u32[]{:S(2)}) collective-permute-start(bf16[128,1152]{1,0:T(8,128)(2,1)S(1)} %add_convert_fusion.9), channel_id=1, source_target_pairs={{0,8},{4,12},{8,16},{12,20},{16,24},{20,28},{24,0},{28,4},{1,9},{5... | collective-permute-start | bytes 884744 | tf_op jit(solution)/shard_map/ppermute | solution.py:479
  (53 other events, 468.6 us)

commit v3 on v2

--- a/solution.py
+++ b/solution.py
@@ -665,7 +665,6 @@
         v.tc = add(c_mine, swap_core(c_send))
         v.yc = swap_pair(v.tc)
         v.sync("x", "xo", "m1")
-        v.sync("tc", "xo")
         attn_names = [n + str(k) for k in range(4) for n in ("a", "xa")]
         attn_packs = [v[n] for n in attn_names]
 
@@ -874,6 +873,8 @@
                 v.sync("ym", "tm", "a2")
                 v.e, dr = give()
                 v.eo = swap_core(v.e)
+            if (n, k) == ("a", 3):
+                v.sync("yx2", "tx2", "eo", "e", "a3")
             if (n, k) == ("m", 3):
                 v.dx = take(dr)
                 v.dxo = swap_core(v.dx)

time: 221 us -> 216 us (0.977)
  waiting for transfers between devices: 107 us -> 98.5 us
  starting transfers between devices: 42.4 us -> 46.4 us
    ppermute x12, waiting for transfers between devices: 45.2 us -> 39.4 us  [shift_one(): return lax.ppermute(v, 'seq', [(i, (i + 2) % seqs) for i in range(seqs)])]
    ppermute x12, starting transfers between devices: 7.75 us -> 10.4 us  [shift_one(): return lax.ppermute(v, 'seq', [(i, (i + 2) % seqs) for i in range(seqs)])]
    ppermute x38, waiting for transfers between devices: 61.8 us -> 59.1 us  [flip_bit(): return lax.ppermute(v, axis, [(i, i ^ mask) for i in range(size)])]
  transfers between devices with their start and end apart: 52 -> 52, of which waited for: 27 -> 23; matrix products, arithmetic and copies ran while one was open for 3% -> 3% of each run, Pallas kernels for 18% -> 19%
where the time goes in v3:
time: 216 us
  waiting for transfers between devices  98.5 us (46%)
  Pallas kernels  53.6 us (25%)
  starting transfers between devices  46.4 us (21%)
  local copies, waits for them, and re-layouts  10 us (5%)
  other arithmetic  5.88 us (3%)
    ppermute x38, waiting for transfers between devices, flip_bit(): return lax.ppermute(v, axis, [(i, i ^ mask) for i in range(size)])  59.1 us
    pallas_call x19, Pallas kernels, call(): pl.pallas_call(body, out_shape=shapes, in_specs=[SM] * smem + [VM] * (len...  53.6 us
    ppermute x12, waiting for transfers between devices, shift_one(): return lax.ppermute(v, 'seq', [(i, (i + 2) % seqs) for i in range(seqs)])  39.4 us
    ppermute x38, starting transfers between devices, flip_bit(): return lax.ppermute(v, axis, [(i, i ^ mask) for i in range(size)])  34.7 us
    ppermute x12, starting transfers between devices, shift_one(): return lax.ppermute(v, 'seq', [(i, (i + 2) % seqs) for i in range(seqs)])  10.4 us
    unnamed x67, local copies, waits for them, and re-layouts  6.23 us
  transfers between devices with their start and end apart: 52, of which 23 were waited for; matrix products, arithmetic and copies ran while one was open for 3% of the time, Pallas kernels for 19%

profile of v3, /device:TPU:0, one launch (start us, length us, event | category | flops | bytes accessed | tf_op | source)
XLA Modules:
  0.0 215.7 jit_solution(8433548352695384213)
XLA Ops:
  8.5 3.0 %collective-permute-start.1 = (bf16[32,1920]{1,0:T(8,128)(2,1)S(1)}, bf16[32,1920]{1,0:T(8,128)(2,1)S(1)}, u32[]{:S(2)}, u32[]{:S(2)}) collective-permute-start(bf16[32,1920]{1,0:T(8,128)(2,1)S(1)} %get-tuple-element.170), channel_id=1, source_target_pairs={{0,2},{1,3},{2,0},{3,1},{4,6},{5,7},{6,4},{7,5},{8,10},{9,11},{10,... | collective-permute-start | bytes 368648 | tf_op jit(solution)/shard_map/ppermute | solution.py:463
  12.2 3.4 %collective-permute-done.1.c2 = bf16[32,1920]{1,0:T(8,128)(2,1)S(1)} collective-permute-done((bf16[32,1920]{1,0:T(8,128)(2,1)S(1)}, bf16[32,1920]{1,0:T(8,128)(2,1)S(1)}, u32[]{:S(2)}, u32[]{:S(2)}) %collective-permute-start.1) | collective-permute-done | bytes 122912 | tf_op jit(solution)/shard_map/ppermute | solution.py:463
  17.7 2.1 join.1
  24.6 7.0 %collective-permute-done.9.refs_2_ = bf16[128,1152]{1,0:T(8,128)(2,1)} collective-permute-done((bf16[128,1152]{1,0:T(8,128)(2,1)S(1)}, bf16[128,1152]{1,0:T(8,128)(2,1)}, u32[]{:S(2)}, u32[]{:S(2)}) %collective-permute-start.9) | collective-permute-done | bytes 294944 | tf_op jit(solution)/shard_map/ppermute | solution.py:479
  33.1 2.1 pick_cotangent.1
  38.1 4.3 %collective-permute-done.12.refs_4_ = bf16[128,1152]{1,0:T(8,128)(2,1)} collective-permute-done((bf16[128,1152]{1,0:T(8,128)(2,1)}, bf16[128,1152]{1,0:T(8,128)(2,1)}, u32[]{:S(2)}, u32[]{:S(2)}) %collective-permute-start.12) | collective-permute-done | bytes 294944 | tf_op jit(solution)/shard_map/ppermute | solution.py:479
  43.9 4.9 %collective-permute-done.11.refs_3_ = bf16[128,1152]{1,0:T(8,128)(2,1)} collective-permute-done((bf16[128,1152]{1,0:T(8,128)(2,1)}, bf16[128,1152]{1,0:T(8,128)(2,1)}, u32[]{:S(2)}, u32[]{:S(2)}) %collective-permute-start.11) | collective-permute-done | bytes 294944 | tf_op jit(solution)/shard_map/ppermute | solution.py:463
  50.2 4.3 %collective-permute-done.14.refs_6_ = bf16[128,1152]{1,0:T(8,128)(2,1)} collective-permute-done((bf16[128,1152]{1,0:T(8,128)(2,1)}, bf16[128,1152]{1,0:T(8,128)(2,1)}, u32[]{:S(2)}, u32[]{:S(2)}) %collective-permute-start.14) | collective-permute-done | bytes 294944 | tf_op jit(solution)/shard_map/ppermute | solution.py:479
  60.4 3.4 %collective-permute-done.7.refs_2_ = bf16[128,2048]{1,0:T(8,128)(2,1)} collective-permute-done((bf16[128,2048]{1,0:T(8,128)(2,1)}, bf16[128,2048]{1,0:T(8,128)(2,1)}, u32[]{:S(2)}, u32[]{:S(2)}) %collective-permute-start.7) | collective-permute-done | bytes 524320 | tf_op jit(solution)/shard_map/ppermute | solution.py:479
  65.3 8.3 %attn_fwd.1 = (bf16[512,1024]{1,0:T(8,128)(2,1)S(1)}, bf16[512,768]{1,0:T(8,128)(2,1)S(1)}, f32[8,256,256]{2,1,0:T(8,128)S(1)}, bf16[512,256]{1,0:T(8,128)(2,1)S...) custom-call(s32[8]{0:T(128)S(1)} %stack.83.idx, ...), custom_call_target="tpu_custom_call" | custom-call | flops 1073741824 | bytes 11309088 | tf_op jit(solution)/shard_map/attn_fwd/pallas_call | solution.py:49
  74.4 3.2 %collective-permute-done.22.refs_4_ = bf16[128,2048]{1,0:T(8,128)(2,1)S(1)} collective-permute-done((bf16[128,2048]{1,0:T(8,128)(2,1)}, bf16[128,2048]{1,0:T(8,128)(2,1)S(1)}, u32[]{:S(2)}, u32[]{:S(2)}) %collective-permute-start.22) | collective-permute-done | bytes 524320 | tf_op jit(solution)/shard_map/ppermute | solution.py:479
  80.9 9.6 %collective-permute-done.25.refs_6_ = bf16[128,2048]{1,0:T(8,128)(2,1)S(1)} collective-permute-done((bf16[128,2048]{1,0:T(8,128)(2,1)S(1)}, bf16[128,2048]{1,0:T(8,128)(2,1)S(1)}, u32[]{:S(2)}, u32[]{:S(2)}) %collective-permute-start.25) | collective-permute-done | bytes 524320 | tf_op jit(solution)/shard_map/ppermute | solution.py:479
  92.3 8.8 %collective-permute-done.26.refs_7_ = bf16[128,2048]{1,0:T(8,128)(2,1)S(1)} collective-permute-done((bf16[128,2048]{1,0:T(8,128)(2,1)S(1)}, bf16[128,2048]{1,0:T(8,128)(2,1)S(1)}, u32[]{:S(2)}, u32[]{:S(2)}) %collective-permute-start.26) | collective-permute-done | bytes 524320 | tf_op jit(solution)/shard_map/ppermute | solution.py:463
  102.1 8.8 %mlp.1 = (bf16[512,1024]{1,0:T(8,128)(2,1)S(1)}, bf16[512,1024]{1,0:T(8,128)(2,1)S(1)}, bf16[512,1024]{1,0:T(8,128)(2,1)S(1)}, bf16[1024,1024]{1,0:T(8,128)(2,1)...) custom-call(s32[8]{0:T(128)S(1)} %stack.83.idx, ...), custom_call_target="tpu_custom_call" | custom-call | flops 3221225472 | bytes 14942240 | tf_op jit(solution)/shard_map/mlp/pallas_call | solution.py:49
  110.9 1.9 collective-permute-done.27
  114.6 3.2 %early_grad.1 = (f32[1024,128]{1,0:T(8,128)S(1)}, bf16[1024,512]{1,0:T(8,128)(2,1)S(1)}, bf16[1024,512]{1,0:T(8,128)(2,1)S(1)}, bf16[128,2048]{1,0:T(8,128)(2,1)...) custom-call(s32[8]{0:T(128)S(1)} %stack.83.idx, ...), custom_call_target="tpu_custom_call" | custom-call | flops 1073741824 | bytes 11272224 | tf_op jit(solution)/shard_map/early_grad/pallas_call | solution.py:49
  119.3 5.8 %late_grad.1 = (bf16[256,1024]{1,0:T(8,128)(2,1)S(1)}, bf16[256,1024]{1,0:T(8,128)(2,1)S(1)}, f32[1024,128]{1,0:T(8,128)S(1)}, bf16[128,2048]{1,0:T(8,128)(2,1)S...) custom-call(s32[8]{0:T(128)S(1)} %stack.83.idx, ...), custom_call_target="tpu_custom_call" | custom-call | flops 2147483648 | bytes 17039392 | tf_op jit(solution)/shard_map/late_grad/pallas_call | solution.py:49
  128.0 4.7 %collective-permute-done.36 = bf16[128,2048]{1,0:T(8,128)(2,1)S(1)} collective-permute-done((bf16[128,2048]{1,0:T(8,128)(2,1)S(1)}, bf16[128,2048]{1,0:T(8,128)(2,1)S(1)}, u32[]{:S(2)}, u32[]{:S(2)}) %collective-permute-start.36) | collective-permute-done | bytes 524320 | tf_op jit(solution)/shard_map/ppermute | solution.py:463
  132.8 1.8 collective-permute-start.40
  136.1 7.2 %attn_bwd.1 = (bf16[512,768]{1,0:T(8,128)(2,1)S(1)}, bf16[128,1152]{1,0:T(8,128)(2,1)S(1)}, bf16[128,1152]{1,0:T(8,128)(2,1)S(1)}, bf16[128,1152]{1,0:T(8,128)(2...) custom-call(s32[8]{0:T(128)S(1)} %stack.83.idx, ...), custom_call_target="tpu_custom_call" | custom-call | flops 1610612736 | bytes 11272224 | tf_op jit(solution)/shard_map/attn_bwd/pallas_call | solution.py:49
  151.3 9.3 %collective-permute-done.42 = bf16[256,1152]{1,0:T(8,128)(2,1)S(1)} collective-permute-done((bf16[256,1152]{1,0:T(8,128)(2,1)S(1)}, bf16[256,1152]{1,0:T(8,128)(2,1)S(1)}, u32[]{:S(2)}, u32[]{:S(2)}) %collective-permute-start.42) | collective-permute-done | bytes 589856 | tf_op jit(solution)/shard_map/ppermute | solution.py:463
  160.8 2.4 %collective-permute-start.43 = (bf16[128,1152]{1,0:T(8,128)(2,1)S(1)}, bf16[128,1152]{1,0:T(8,128)(2,1)S(1)}, u32[]{:S(2)}, u32[]{:S(2)}) collective-permute-start(bf16[128,1152]{1,0:T(8,128)(2,1)S(1)} %add_convert_fusion.11), channel_id=1, source_target_pairs={{0,8},{4,12},{8,16},{12,20},{16,24},{20,28},{24,0},{28,4},{1,9},{5... | collective-permute-start | bytes 884744 | tf_op jit(solution)/shard_map/ppermute | solution.py:479
  165.4 5.8 %collective-permute-done.43 = bf16[128,1152]{1,0:T(8,128)(2,1)S(1)} collective-permute-done((bf16[128,1152]{1,0:T(8,128)(2,1)S(1)}, bf16[128,1152]{1,0:T(8,128)(2,1)S(1)}, u32[]{:S(2)}, u32[]{:S(2)}) %collective-permute-start.43) | collective-permute-done | bytes 294944 | tf_op jit(solution)/shard_map/ppermute | solution.py:479
  173.3 4.7 %collective-permute-done.37 = bf16[128,2048]{1,0:T(8,128)(2,1)S(1)} collective-permute-done((bf16[128,2048]{1,0:T(8,128)(2,1)S(1)}, bf16[128,2048]{1,0:T(8,128)(2,1)S(1)}, u32[]{:S(2)}, u32[]{:S(2)}) %collective-permute-start.37) | collective-permute-done | bytes 524320 | tf_op jit(solution)/shard_map/ppermute | solution.py:463
  179.4 2.6 %place_mixed.1 = bf16[2,512,1024]{2,1,0:T(8,128)(2,1)} custom-call(s32[5]{0:T(128)S(1)} %stack.74.meta, s32[2,1,256]{2,1,0:T(1,128)S(1)} %broadcast_in_dim.14.pos_ref, bf16[2,512,1024]{2,1,0:T(8,128)(2,1)S(1)} %copy-done.4, bf16[256,1024]{1,0:T(8,128)(2,1)S(1)} %get-tuple-element.265.own_ref, bf16[256,1024]{1,0:T(8,128)(2,1)S(1)} %collective-permute-done.34.oth_ref), custom_call_target="tpu_custom_call" | custom-call | flops 536870912 | bytes 5244948 | tf_op jit(solution)/shard_map/place_mixed/pallas_call | solution.py:49
  183.2 7.4 %collective-permute-done.46.a1 = bf16[256,1152]{1,0:T(8,128)(2,1)S(1)} collective-permute-done((bf16[256,1152]{1,0:T(8,128)(2,1)S(1)}, bf16[256,1152]{1,0:T(8,128)(2,1)S(1)}, u32[]{:S(2)}, u32[]{:S(2)}) %collective-permute-start.46) | collective-permute-done | bytes 589856 | tf_op jit(solution)/shard_map/ppermute | solution.py:463
  192.4 2.6 %place_input_grad.1 = bf16[2,512,1024]{2,1,0:T(8,128)(2,1)} custom-call(s32[5]{0:T(128)S(1)} %stack.74.meta, s32[2,1,256]{2,1,0:T(1,128)S(1)} %broadcast_in_dim.14.pos_ref, bf16[2,512,1024]{2,1,0:T(8,128)(2,1)S(1)} %copy-done.5, bf16[256,1024]{1,0:T(8,128)(2,1)S(1)} %input_grad.1.own_ref, bf16[256,1024]{1,0:T(8,128)(2,1)S(1)} %collective-permute-done.35.oth_ref), custom_call_target="tpu_custom_call" | custom-call | flops 536870912 | bytes 5244948 | tf_op jit(solution)/shard_map/place_input_grad/pallas_call | solution.py:49
  195.0 5.2 %collective-permute-done.38.m1 = bf16[128,2048]{1,0:T(8,128)(2,1)S(1)} collective-permute-done((bf16[128,2048]{1,0:T(8,128)(2,1)S(1)}, bf16[128,2048]{1,0:T(8,128)(2,1)S(1)}, u32[]{:S(2)}, u32[]{:S(2)}) %collective-permute-start.38) | collective-permute-done | bytes 524320 | tf_op jit(solution)/shard_map/ppermute | solution.py:463
  201.8 1.9 split.1
  207.1 2.9 %collective-permute-done.49.c2 = bf16[32,1920]{1,0:T(8,128)(2,1)S(1)} collective-permute-done((bf16[32,1920]{1,0:T(8,128)(2,1)S(1)}, bf16[32,1920]{1,0:T(8,128)(2,1)S(1)}, u32[]{:S(2)}, u32[]{:S(2)}) %collective-permute-start.49) | collective-permute-done | bytes 122912 | tf_op jit(solution)/shard_map/ppermute | solution.py:463
  209.9 1.7 collective-permute-done.50.c3
  212.3 2.2 %final.1 = (f32[32,3072]{1,0:T(8,128)}, f32[32,4096]{1,0:T(8,128)}, f32[8,128]{1,0:T(8,128)S(1)}) custom-call(s32[5]{0:T(128)S(1)} %stack.74.meta, f32[32,1920]{1,0:T(8,128)S(1)} %get-tuple-element.312.c0, bf16[32,1920]{1,0:T(8,128)(2,1)} %copy-done.18, bf16[32,1920]{1,0:T(8,128)(2,1)} %copy-done.19, bf16[32,1920]{1,0:T(8,128)(2,1)} %copy-done.20), custom_call_target="tpu_custom_call" | custom-call | bytes 1536020 | tf_op jit(solution)/shard_map/final/pallas_call | solution.py:49
  (190 shorter events, 68.2 us)
Async XLA Ops:
  7.9 11.9 %collective-permute-start.4 = (bf16[256,1024]{1,0:T(8,128)(2,1)S(1)}, bf16[256,1024]{1,0:T(8,128)(2,1)S(1)}, u32[]{:S(2)}, u32[]{:S(2)}) collective-permute-start(bf16[256,1024]{1,0:T(8,128)(2,1)S(1)} %get-tuple-element.176), channel_id=1, source_target_pairs={{0,1},{1,0},{2,3},{3,2},{4,5},{5,4},{6,7},{7,6},{8,9},{9,8},{10,11... | collective-permute-start | bytes 1572872 | tf_op jit(solution)/shard_map/ppermute | solution.py:463
  20.0 11.6 %collective-permute-start.9 = (bf16[128,1152]{1,0:T(8,128)(2,1)S(1)}, bf16[128,1152]{1,0:T(8,128)(2,1)}, u32[]{:S(2)}, u32[]{:S(2)}) collective-permute-start(bf16[128,1152]{1,0:T(8,128)(2,1)S(1)} %get-tuple-element.182.refs_0_), channel_id=1, source_target_pairs={{0,8},{4,12},{8,16},{12,20},{16,24},{20,28},{24,0},{28,4},{1,9},{5... | collective-permute-start | bytes 884744 | tf_op jit(solution)/shard_map/ppermute | solution.py:479
  21.6 14.9 %collective-permute-start.10 = (bf16[128,2048]{1,0:T(8,128)(2,1)}, bf16[128,2048]{1,0:T(8,128)(2,1)S(1)}, u32[]{:S(2)}, u32[]{:S(2)}) collective-permute-start(bf16[128,2048]{1,0:T(8,128)(2,1)} %get-tuple-element.178.refs_0_), channel_id=1, source_target_pairs={{0,4},{4,0},{8,12},{12,8},{16,20},{20,16},{24,28},{28,24},{1,5},{5... | collective-permute-start | bytes 1572872 | tf_op jit(solution)/shard_map/ppermute | solution.py:463
  23.2 19.5 %collective-permute-start.5 = (bf16[256,1024]{1,0:T(8,128)(2,1)S(1)}, bf16[256,1024]{1,0:T(8,128)(2,1)S(1)}, u32[]{:S(2)}, u32[]{:S(2)}) collective-permute-start(bf16[256,1024]{1,0:T(8,128)(2,1)S(1)} %add_convert_fusion.8), channel_id=1, source_target_pairs={{0,2},{1,3},{2,0},{3,1},{4,6},{5,7},{6,4},{7,5},{8,10},{9,11},{10,... | collective-permute-start | bytes 1572872 | tf_op jit(solution)/shard_map/ppermute | solution.py:463
  31.6 11.4 %collective-permute-start.8 = (bf16[128,1152]{1,0:T(8,128)(2,1)S(1)}, bf16[128,1152]{1,0:T(8,128)(2,1)S(1)}, u32[]{:S(2)}, u32[]{:S(2)}) collective-permute-start(bf16[128,1152]{1,0:T(8,128)(2,1)S(1)} %get-tuple-element.182.refs_0_), channel_id=1, source_target_pairs={{0,4},{4,0},{8,12},{12,8},{16,20},{20,16},{24,28},{28,24},{1,5},{5... | collective-permute-start | bytes 884744 | tf_op jit(solution)/shard_map/ppermute | solution.py:463
  35.2 22.4 %collective-permute-start.19 = (bf16[256,1024]{1,0:T(8,128)(2,1)}, bf16[256,1024]{1,0:T(8,128)(2,1)}, u32[]{:S(2)}, u32[]{:S(2)}) collective-permute-start(bf16[256,1024]{1,0:T(8,128)(2,1)} %get-tuple-element.212), channel_id=1, source_target_pairs={{0,1},{1,0},{2,3},{3,2},{4,5},{5,4},{6,7},{7,6},{8,9},{9,8},{10,11... | collective-permute-start | bytes 1572872 | tf_op jit(solution)/shard_map/ppermute | solution.py:463
  36.6 12.3 %collective-permute-start.11 = (bf16[128,1152]{1,0:T(8,128)(2,1)}, bf16[128,1152]{1,0:T(8,128)(2,1)}, u32[]{:S(2)}, u32[]{:S(2)}) collective-permute-start(bf16[128,1152]{1,0:T(8,128)(2,1)} %collective-permute-done.9.refs_2_), channel_id=1, source_target_pairs={{0,4},{4,0},{8,12},{12,8},{16,20},{20,16},{24,28},{28,24},{1,5},{5... | collective-permute-start | bytes 884744 | tf_op jit(solution)/shard_map/ppermute | solution.py:463
  42.5 12.1 %collective-permute-start.14 = (bf16[128,1152]{1,0:T(8,128)(2,1)}, bf16[128,1152]{1,0:T(8,128)(2,1)}, u32[]{:S(2)}, u32[]{:S(2)}) collective-permute-start(bf16[128,1152]{1,0:T(8,128)(2,1)} %collective-permute-done.12.refs_4_), channel_id=1, source_target_pairs={{0,8},{4,12},{8,16},{12,20},{16,24},{20,28},{24,0},{28,4},{1,9},{5... | collective-permute-start | bytes 884744 | tf_op jit(solution)/shard_map/ppermute | solution.py:479
  42.7 21.0 %collective-permute-start.7 = (bf16[128,2048]{1,0:T(8,128)(2,1)}, bf16[128,2048]{1,0:T(8,128)(2,1)}, u32[]{:S(2)}, u32[]{:S(2)}) collective-permute-start(bf16[128,2048]{1,0:T(8,128)(2,1)} %get-tuple-element.178.refs_0_), channel_id=1, source_target_pairs={{0,8},{4,12},{8,16},{12,20},{16,24},{20,28},{24,0},{28,4},{1,9},{5... | collective-permute-start | bytes 1572872 | tf_op jit(solution)/shard_map/ppermute | solution.py:479
  43.0 22.3 %collective-permute-start.6 = (bf16[256,1024]{1,0:T(8,128)(2,1)S(1)}, bf16[256,1024]{1,0:T(8,128)(2,1)}, u32[]{:S(2)}, u32[]{:S(2)}) collective-permute-start(bf16[256,1024]{1,0:T(8,128)(2,1)S(1)} %add.96.xo_ref.x_ref), channel_id=1, source_target_pairs={{0,1},{1,0},{2,3},{3,2},{4,5},{5,4},{6,7},{7,6},{8,9},{9,8},{10,11... | collective-permute-start | bytes 1572872 | tf_op jit(solution)/shard_map/ppermute | solution.py:463
  48.8 14.9 %collective-permute-start.13 = (bf16[128,1152]{1,0:T(8,128)(2,1)}, bf16[128,1152]{1,0:T(8,128)(2,1)S(1)}, u32[]{:S(2)}, u32[]{:S(2)}) collective-permute-start(bf16[128,1152]{1,0:T(8,128)(2,1)} %collective-permute-done.12.refs_4_), channel_id=1, source_target_pairs={{0,4},{4,0},{8,12},{12,8},{16,20},{20,16},{24,28},{28,24},{1,5},{5... | collective-permute-start | bytes 884744 | tf_op jit(solution)/shard_map/ppermute | solution.py:463
  58.8 14.9 %collective-permute-start.20 = (bf16[256,1024]{1,0:T(8,128)(2,1)S(1)}, bf16[256,1024]{1,0:T(8,128)(2,1)S(1)}, u32[]{:S(2)}, u32[]{:S(2)}) collective-permute-start(bf16[256,1024]{1,0:T(8,128)(2,1)S(1)} %add_convert_fusion.6), channel_id=1, source_target_pairs={{0,2},{1,3},{2,0},{3,1},{4,6},{5,7},{6,4},{7,5},{8,10},{9,11},{10,... | collective-permute-start | bytes 1572872 | tf_op jit(solution)/shard_map/ppermute | solution.py:463
  63.7 13.9 %collective-permute-start.22 = (bf16[128,2048]{1,0:T(8,128)(2,1)}, bf16[128,2048]{1,0:T(8,128)(2,1)S(1)}, u32[]{:S(2)}, u32[]{:S(2)}) collective-permute-start(bf16[128,2048]{1,0:T(8,128)(2,1)} %collective-permute-done.7.refs_2_), channel_id=1, source_target_pairs={{0,8},{4,12},{8,16},{12,20},{16,24},{20,28},{24,0},{28,4},{1,9},{5... | collective-permute-start | bytes 1572872 | tf_op jit(solution)/shard_map/ppermute | solution.py:479
  63.8 15.4 %collective-permute-start.17 = (bf16[128,2048]{1,0:T(8,128)(2,1)}, bf16[128,2048]{1,0:T(8,128)(2,1)S(1)}, u32[]{:S(2)}, u32[]{:S(2)}) collective-permute-start(bf16[128,2048]{1,0:T(8,128)(2,1)} %collective-permute-done.7.refs_2_), channel_id=1, source_target_pairs={{0,4},{4,0},{8,12},{12,8},{16,20},{20,16},{24,28},{28,24},{1,5},{5... | collective-permute-start | bytes 1572872 | tf_op jit(solution)/shard_map/ppermute | solution.py:463
  73.9 18.0 %collective-permute-start.21 = (bf16[256,1024]{1,0:T(8,128)(2,1)S(1)}, bf16[256,1024]{1,0:T(8,128)(2,1)S(1)}, u32[]{:S(2)}, u32[]{:S(2)}) collective-permute-start(bf16[256,1024]{1,0:T(8,128)(2,1)S(1)} %add.99.co_ref.c_ref), channel_id=1, source_target_pairs={{0,1},{1,0},{2,3},{3,2},{4,5},{5,4},{6,7},{7,6},{8,9},{9,8},{10,11... | collective-permute-start | bytes 1572872 | tf_op jit(solution)/shard_map/ppermute | solution.py:463
  77.6 12.9 %collective-permute-start.25 = (bf16[128,2048]{1,0:T(8,128)(2,1)S(1)}, bf16[128,2048]{1,0:T(8,128)(2,1)S(1)}, u32[]{:S(2)}, u32[]{:S(2)}) collective-permute-start(bf16[128,2048]{1,0:T(8,128)(2,1)S(1)} %collective-permute-done.22.refs_4_), channel_id=1, source_target_pairs={{0,8},{4,12},{8,16},{12,20},{16,24},{20,28},{24,0},{28,4},{1,9},{5... | collective-permute-start | bytes 1572872 | tf_op jit(solution)/shard_map/ppermute | solution.py:479
  77.6 14.2 %collective-permute-start.23 = (bf16[128,2048]{1,0:T(8,128)(2,1)S(1)}, bf16[128,2048]{1,0:T(8,128)(2,1)S(1)}, u32[]{:S(2)}, u32[]{:S(2)}) collective-permute-start(bf16[128,2048]{1,0:T(8,128)(2,1)S(1)} %collective-permute-done.22.refs_4_), channel_id=1, source_target_pairs={{0,4},{4,0},{8,12},{12,8},{16,20},{20,16},{24,28},{28,24},{1,5},{5... | collective-permute-start | bytes 1572872 | tf_op jit(solution)/shard_map/ppermute | solution.py:463
  79.3 12.6 %collective-permute-start.18 = (bf16[256,1024]{1,0:T(8,128)(2,1)S(1)}, bf16[256,1024]{1,0:T(8,128)(2,1)S(1)}, u32[]{:S(2)}, u32[]{:S(2)}) collective-permute-start(bf16[256,1024]{1,0:T(8,128)(2,1)S(1)} %add_convert_fusion.7.t_ref.bt_ref.at_ref), channel_id=1, source_target_pairs={{0,2},{1,3},{2,0},{3,1},{4,6},{5,7},{6,4},{7,5},{8,10},{9,11},{10,... | collective-permute-start | bytes 1572872 | tf_op jit(solution)/shard_map/ppermute | solution.py:463
  113.0 14.0 %collective-permute-start.28 = (bf16[256,1024]{1,0:T(8,128)(2,1)S(1)}, bf16[256,1024]{1,0:T(8,128)(2,1)S(1)}, u32[]{:S(2)}, u32[]{:S(2)}) collective-permute-start(bf16[256,1024]{1,0:T(8,128)(2,1)S(1)} %add_convert_fusion.5.dt_ref), channel_id=1, source_target_pairs={{0,2},{1,3},{2,0},{3,1},{4,6},{5,7},{6,4},{7,5},{8,10},{9,11},{10,... | collective-permute-start | bytes 1572872 | tf_op jit(solution)/shard_map/ppermute | solution.py:463
  117.8 14.9 %collective-permute-start.36 = (bf16[128,2048]{1,0:T(8,128)(2,1)S(1)}, bf16[128,2048]{1,0:T(8,128)(2,1)S(1)}, u32[]{:S(2)}, u32[]{:S(2)}) collective-permute-start(bf16[128,2048]{1,0:T(8,128)(2,1)S(1)} %get-tuple-element.278), channel_id=1, source_target_pairs={{0,4},{4,0},{8,12},{12,8},{16,20},{20,16},{24,28},{28,24},{1,5},{5... | collective-permute-start | bytes 1572872 | tf_op jit(solution)/shard_map/ppermute | solution.py:463
  125.2 19.8 %collective-permute-start.39 = (bf16[128,2048]{1,0:T(8,128)(2,1)S(1)}, bf16[128,2048]{1,0:T(8,128)(2,1)S(1)}, u32[]{:S(2)}, u32[]{:S(2)}) collective-permute-start(bf16[128,2048]{1,0:T(8,128)(2,1)S(1)} %get-tuple-element.286), channel_id=1, source_target_pairs={{0,4},{4,0},{8,12},{12,8},{16,20},{20,16},{24,28},{28,24},{1,5},{5... | collective-permute-start | bytes 1572872 | tf_op jit(solution)/shard_map/ppermute | solution.py:463
  132.8 14.7 %collective-permute-start.40 = (bf16[128,2048]{1,0:T(8,128)(2,1)S(1)}, bf16[128,2048]{1,0:T(8,128)(2,1)S(1)}, u32[]{:S(2)}, u32[]{:S(2)}) collective-permute-start(bf16[128,2048]{1,0:T(8,128)(2,1)S(1)} %add_convert_fusion.2), channel_id=1, source_target_pairs={{0,8},{4,12},{8,16},{12,20},{16,24},{20,28},{24,0},{28,4},{1,9},{5... | collective-permute-start | bytes 1572872 | tf_op jit(solution)/shard_map/ppermute | solution.py:479
  134.9 12.6 %collective-permute-start.33 = (bf16[256,1024]{1,0:T(8,128)(2,1)S(1)}, bf16[256,1024]{1,0:T(8,128)(2,1)S(1)}, u32[]{:S(2)}, u32[]{:S(2)}) collective-permute-start(bf16[256,1024]{1,0:T(8,128)(2,1)S(1)} %add_convert_fusion.3.mt_ref), channel_id=1, source_target_pairs={{0,2},{1,3},{2,0},{3,1},{4,6},{5,7},{6,4},{7,5},{8,10},{9,11},{10,... | collective-permute-start | bytes 1572872 | tf_op jit(solution)/shard_map/ppermute | solution.py:463
  144.9 15.7 %collective-permute-start.42 = (bf16[256,1152]{1,0:T(8,128)(2,1)S(1)}, bf16[256,1152]{1,0:T(8,128)(2,1)S(1)}, u32[]{:S(2)}, u32[]{:S(2)}) collective-permute-start(bf16[256,1152]{1,0:T(8,128)(2,1)S(1)} %get-tuple-element.294), channel_id=1, source_target_pairs={{0,4},{4,0},{8,12},{12,8},{16,20},{20,16},{24,28},{28,24},{1,5},{5... | collective-permute-start | bytes 1769480 | tf_op jit(solution)/shard_map/ppermute | solution.py:463
  147.7 16.9 %collective-permute-start.41 = (bf16[128,2048]{1,0:T(8,128)(2,1)S(1)}, bf16[128,2048]{1,0:T(8,128)(2,1)S(1)}, u32[]{:S(2)}, u32[]{:S(2)}) collective-permute-start(bf16[128,2048]{1,0:T(8,128)(2,1)S(1)} %add_convert_fusion.1), channel_id=1, source_target_pairs={{0,8},{4,12},{8,16},{12,20},{16,24},{20,28},{24,0},{28,4},{1,9},{5... | collective-permute-start | bytes 1572872 | tf_op jit(solution)/shard_map/ppermute | solution.py:479
  149.5 15.0 %collective-permute-start.34 = (bf16[256,1024]{1,0:T(8,128)(2,1)S(1)}, bf16[256,1024]{1,0:T(8,128)(2,1)S(1)}, u32[]{:S(2)}, u32[]{:S(2)}) collective-permute-start(bf16[256,1024]{1,0:T(8,128)(2,1)S(1)} %get-tuple-element.265.own_ref), channel_id=1, source_target_pairs={{0,1},{1,0},{2,3},{3,2},{4,5},{5,4},{6,7},{7,6},{8,9},{9,8},{10,11... | collective-permute-start | bytes 1572872 | tf_op jit(solution)/shard_map/ppermute | solution.py:463
  149.8 14.8 %collective-permute-start.31 = (bf16[256,1024]{1,0:T(8,128)(2,1)S(1)}, bf16[256,1024]{1,0:T(8,128)(2,1)S(1)}, u32[]{:S(2)}, u32[]{:S(2)}) collective-permute-start(bf16[256,1024]{1,0:T(8,128)(2,1)S(1)} %add_convert_fusion.4.t_ref), channel_id=1, source_target_pairs={{0,2},{1,3},{2,0},{3,1},{4,6},{5,7},{6,4},{7,5},{8,10},{9,11},{10,... | collective-permute-start | bytes 1572872 | tf_op jit(solution)/shard_map/ppermute | solution.py:463
  163.1 14.9 %collective-permute-start.37 = (bf16[128,2048]{1,0:T(8,128)(2,1)S(1)}, bf16[128,2048]{1,0:T(8,128)(2,1)S(1)}, u32[]{:S(2)}, u32[]{:S(2)}) collective-permute-start(bf16[128,2048]{1,0:T(8,128)(2,1)S(1)} %get-tuple-element.281), channel_id=1, source_target_pairs={{0,4},{4,0},{8,12},{12,8},{16,20},{20,16},{24,28},{28,24},{1,5},{5... | collective-permute-start | bytes 1572872 | tf_op jit(solution)/shard_map/ppermute | solution.py:463
  165.3 16.7 %collective-permute-start.35 = (bf16[256,1024]{1,0:T(8,128)(2,1)S(1)}, bf16[256,1024]{1,0:T(8,128)(2,1)S(1)}, u32[]{:S(2)}, u32[]{:S(2)}) collective-permute-start(bf16[256,1024]{1,0:T(8,128)(2,1)S(1)} %input_grad.1.own_ref), channel_id=1, source_target_pairs={{0,1},{1,0},{2,3},{3,2},{4,5},{5,4},{6,7},{7,6},{8,9},{9,8},{10,11... | collective-permute-start | bytes 1572872 | tf_op jit(solution)/shard_map/ppermute | solution.py:463
  171.9 18.8 %collective-permute-start.46 = (bf16[256,1152]{1,0:T(8,128)(2,1)S(1)}, bf16[256,1152]{1,0:T(8,128)(2,1)S(1)}, u32[]{:S(2)}, u32[]{:S(2)}) collective-permute-start(bf16[256,1152]{1,0:T(8,128)(2,1)S(1)} %get-tuple-element.308), channel_id=1, source_target_pairs={{0,4},{4,0},{8,12},{12,8},{16,20},{20,16},{24,28},{28,24},{1,5},{5... | collective-permute-start | bytes 1769480 | tf_op jit(solution)/shard_map/ppermute | solution.py:463
  178.0 22.2 %collective-permute-start.38 = (bf16[128,2048]{1,0:T(8,128)(2,1)S(1)}, bf16[128,2048]{1,0:T(8,128)(2,1)S(1)}, u32[]{:S(2)}, u32[]{:S(2)}) collective-permute-start(bf16[128,2048]{1,0:T(8,128)(2,1)S(1)} %get-tuple-element.284), channel_id=1, source_target_pairs={{0,4},{4,0},{8,12},{12,8},{16,20},{20,16},{24,28},{28,24},{1,5},{5... | collective-permute-start | bytes 1572872 | tf_op jit(solution)/shard_map/ppermute | solution.py:463
  182.3 18.6 %collective-permute-start.45 = (bf16[128,2048]{1,0:T(8,128)(2,1)S(1)}, bf16[128,2048]{1,0:T(8,128)(2,1)S(1)}, u32[]{:S(2)}, u32[]{:S(2)}) collective-permute-start(bf16[128,2048]{1,0:T(8,128)(2,1)S(1)} %add_convert_fusion), channel_id=1, source_target_pairs={{0,8},{4,12},{8,16},{12,20},{16,24},{20,28},{24,0},{28,4},{1,9},{5... | collective-permute-start | bytes 1572872 | tf_op jit(solution)/shard_map/ppermute | solution.py:479
  (53 other events, 463.3 us)

commit v4 on v3

--- a/solution.py
+++ b/solution.py
@@ -723,7 +723,8 @@
         smem=1,
         flops=6 * both * width * ff,
         name="mlp",
-        cold=(2, 3, 4, *range(6, 14)),
+        cold=(2, 3, 4, *range(6, 13)),
+        free=(13,),
     )
 
     v.du = du
@@ -768,7 +769,7 @@
     v.__dict__.update({n + str(k): None for n in ("xm", "xa") for k in range(4)})
     if not native:
         for n, k in (('m', 1), ('m', 2)):
-            side("x%s%d" % (n, k), parts[n][2 * k + 1], 2)
+            side("x%s%d" % (n, k), parts[n][2 * k + 1], 4)
     v.sync("yd", "td", "bm")
     da_own, dh = call(
         hidden_grad_body,
@@ -851,8 +852,8 @@
         for k in range(4):
             v["m%d" % k], v["a%d" % k] = mlp_grads[2 * k], attn_grads[k]
         v.ym = swap_pair(v.tm)
-        for n, k in (('m', 3), ('a', 4), ('m', 0), ('a', 5)):
-            side("x%s%d" % (n, k), parts[n][2 * k + 1 if n == "m" else k], 2)
+        for n, k in (('a', 4), ('m', 3), ('a', 5), ('m', 0)):
+            side("x%s%d" % (n, k), parts[n][2 * k + 1 if n == "m" else k], 4)
         blk = width // BLOCKS
         v.tx2 = add(v.dxm, swap_core(v.dxs))
 

time: 216 us -> 216 us (level)
    ppermute x12, waiting for transfers between devices: 39.4 us -> 43.7 us  [shift_one(): return lax.ppermute(v, 'seq', [(i, (i + 2) % seqs) for i in range(seqs)])]
    ppermute x38, waiting for transfers between devices: 59.1 us -> 56.5 us  [flip_bit(): return lax.ppermute(v, axis, [(i, i ^ mask) for i in range(size)])]
    unnamed x67 -> x65, local copies, waits for them, and re-layouts: 6.23 us -> 6.06 us
where the time goes in v4:
time: 216 us; the launch traced here: 215 us
  waiting for transfers between devices  100 us (46%)
  Pallas kernels  53.4 us (25%)
  starting transfers between devices  44.7 us (21%)
  local copies, waits for them, and re-layouts  9.86 us (5%)
  other arithmetic  5.88 us (3%)
    ppermute x38, waiting for transfers between devices, flip_bit(): return lax.ppermute(v, axis, [(i, i ^ mask) for i in range(size)])  56.5 us
    pallas_call x19, Pallas kernels, call(): pl.pallas_call(body, out_shape=shapes, in_specs=[SM] * smem + [VM] * (len...  53.4 us
    ppermute x12, waiting for transfers between devices, shift_one(): return lax.ppermute(v, 'seq', [(i, (i + 2) % seqs) for i in range(seqs)])  43.7 us
    ppermute x38, starting transfers between devices, flip_bit(): return lax.ppermute(v, axis, [(i, i ^ mask) for i in range(size)])  33.8 us
    ppermute x12, starting transfers between devices, shift_one(): return lax.ppermute(v, 'seq', [(i, (i + 2) % seqs) for i in range(seqs)])  9.56 us
    unnamed x65, local copies, waits for them, and re-layouts  6.06 us
  transfers between devices with their start and end apart: 52, of which 23 were waited for; matrix products, arithmetic and copies ran while one was open for 3% of the time, Pallas kernels for 19%

profile of v4, /device:TPU:0, one launch (start us, length us, event | category | flops | bytes accessed | tf_op | source)
XLA Modules:
  0.0 215.4 jit_solution(14951866706722811794)
XLA Ops:
  8.5 3.0 %collective-permute-start.1 = (bf16[32,1920]{1,0:T(8,128)(2,1)S(1)}, bf16[32,1920]{1,0:T(8,128)(2,1)S(1)}, u32[]{:S(2)}, u32[]{:S(2)}) collective-permute-start(bf16[32,1920]{1,0:T(8,128)(2,1)S(1)} %get-tuple-element.164), channel_id=1, source_target_pairs={{0,2},{1,3},{2,0},{3,1},{4,6},{5,7},{6,4},{7,5},{8,10},{9,11},{10,... | collective-permute-start | bytes 368648 | tf_op jit(solution)/shard_map/ppermute | solution.py:463
  12.2 3.4 %collective-permute-done.1.c2 = bf16[32,1920]{1,0:T(8,128)(2,1)S(1)} collective-permute-done((bf16[32,1920]{1,0:T(8,128)(2,1)S(1)}, bf16[32,1920]{1,0:T(8,128)(2,1)S(1)}, u32[]{:S(2)}, u32[]{:S(2)}) %collective-permute-start.1) | collective-permute-done | bytes 122912 | tf_op jit(solution)/shard_map/ppermute | solution.py:463
  17.7 2.1 join.1
  24.6 7.0 %collective-permute-done.9.refs_2_ = bf16[128,1152]{1,0:T(8,128)(2,1)} collective-permute-done((bf16[128,1152]{1,0:T(8,128)(2,1)S(1)}, bf16[128,1152]{1,0:T(8,128)(2,1)}, u32[]{:S(2)}, u32[]{:S(2)}) %collective-permute-start.9) | collective-permute-done | bytes 294944 | tf_op jit(solution)/shard_map/ppermute | solution.py:479
  33.1 2.1 pick_cotangent.1
  38.1 4.3 %collective-permute-done.12.refs_4_ = bf16[128,1152]{1,0:T(8,128)(2,1)} collective-permute-done((bf16[128,1152]{1,0:T(8,128)(2,1)}, bf16[128,1152]{1,0:T(8,128)(2,1)}, u32[]{:S(2)}, u32[]{:S(2)}) %collective-permute-start.12) | collective-permute-done | bytes 294944 | tf_op jit(solution)/shard_map/ppermute | solution.py:479
  43.9 4.9 %collective-permute-done.11.refs_3_ = bf16[128,1152]{1,0:T(8,128)(2,1)} collective-permute-done((bf16[128,1152]{1,0:T(8,128)(2,1)}, bf16[128,1152]{1,0:T(8,128)(2,1)}, u32[]{:S(2)}, u32[]{:S(2)}) %collective-permute-start.11) | collective-permute-done | bytes 294944 | tf_op jit(solution)/shard_map/ppermute | solution.py:463
  50.2 4.3 %collective-permute-done.14.refs_6_ = bf16[128,1152]{1,0:T(8,128)(2,1)} collective-permute-done((bf16[128,1152]{1,0:T(8,128)(2,1)}, bf16[128,1152]{1,0:T(8,128)(2,1)}, u32[]{:S(2)}, u32[]{:S(2)}) %collective-permute-start.14) | collective-permute-done | bytes 294944 | tf_op jit(solution)/shard_map/ppermute | solution.py:479
  60.4 3.4 %collective-permute-done.7.refs_2_ = bf16[128,2048]{1,0:T(8,128)(2,1)} collective-permute-done((bf16[128,2048]{1,0:T(8,128)(2,1)}, bf16[128,2048]{1,0:T(8,128)(2,1)}, u32[]{:S(2)}, u32[]{:S(2)}) %collective-permute-start.7) | collective-permute-done | bytes 524320 | tf_op jit(solution)/shard_map/ppermute | solution.py:479
  65.3 8.3 %attn_fwd.1 = (bf16[512,1024]{1,0:T(8,128)(2,1)S(1)}, bf16[512,768]{1,0:T(8,128)(2,1)S(1)}, f32[8,256,256]{2,1,0:T(8,128)S(1)}, bf16[512,256]{1,0:T(8,128)(2,1)S...) custom-call(s32[8]{0:T(128)S(1)} %stack.83.idx, ...), custom_call_target="tpu_custom_call" | custom-call | flops 1073741824 | bytes 11309088 | tf_op jit(solution)/shard_map/attn_fwd/pallas_call | solution.py:49
  74.4 3.2 %collective-permute-done.22.refs_4_ = bf16[128,2048]{1,0:T(8,128)(2,1)S(1)} collective-permute-done((bf16[128,2048]{1,0:T(8,128)(2,1)}, bf16[128,2048]{1,0:T(8,128)(2,1)S(1)}, u32[]{:S(2)}, u32[]{:S(2)}) %collective-permute-start.22) | collective-permute-done | bytes 524320 | tf_op jit(solution)/shard_map/ppermute | solution.py:479
  80.9 9.6 %collective-permute-done.25.refs_6_ = bf16[128,2048]{1,0:T(8,128)(2,1)S(1)} collective-permute-done((bf16[128,2048]{1,0:T(8,128)(2,1)S(1)}, bf16[128,2048]{1,0:T(8,128)(2,1)S(1)}, u32[]{:S(2)}, u32[]{:S(2)}) %collective-permute-start.25) | collective-permute-done | bytes 524320 | tf_op jit(solution)/shard_map/ppermute | solution.py:479
  92.3 8.8 %collective-permute-done.26.refs_7_ = bf16[128,2048]{1,0:T(8,128)(2,1)S(1)} collective-permute-done((bf16[128,2048]{1,0:T(8,128)(2,1)S(1)}, bf16[128,2048]{1,0:T(8,128)(2,1)S(1)}, u32[]{:S(2)}, u32[]{:S(2)}) %collective-permute-start.26) | collective-permute-done | bytes 524320 | tf_op jit(solution)/shard_map/ppermute | solution.py:463
  101.9 8.6 %mlp.1 = (bf16[512,1024]{1,0:T(8,128)(2,1)S(1)}, bf16[512,1024]{1,0:T(8,128)(2,1)S(1)}, bf16[512,1024]{1,0:T(8,128)(2,1)S(1)}, bf16[1024,1024]{1,0:T(8,128)(2,1)...) custom-call(s32[8]{0:T(128)S(1)} %stack.83.idx, ...), custom_call_target="tpu_custom_call" | custom-call | flops 3221225472 | bytes 14942240 | tf_op jit(solution)/shard_map/mlp/pallas_call | solution.py:49
  110.6 1.9 collective-permute-done.27
  114.3 3.2 %early_grad.1 = (f32[1024,128]{1,0:T(8,128)S(1)}, bf16[1024,512]{1,0:T(8,128)(2,1)S(1)}, bf16[1024,512]{1,0:T(8,128)(2,1)S(1)}, bf16[128,2048]{1,0:T(8,128)(2,1)...) custom-call(s32[8]{0:T(128)S(1)} %stack.83.idx, ...), custom_call_target="tpu_custom_call" | custom-call | flops 1073741824 | bytes 11272224 | tf_op jit(solution)/shard_map/early_grad/pallas_call | solution.py:49
  119.0 5.8 %late_grad.1 = (bf16[256,1024]{1,0:T(8,128)(2,1)S(1)}, bf16[256,1024]{1,0:T(8,128)(2,1)S(1)}, f32[1024,128]{1,0:T(8,128)S(1)}, bf16[128,2048]{1,0:T(8,128)(2,1)S...) custom-call(s32[8]{0:T(128)S(1)} %stack.83.idx, ...), custom_call_target="tpu_custom_call" | custom-call | flops 2147483648 | bytes 17039392 | tf_op jit(solution)/shard_map/late_grad/pallas_call | solution.py:49
  127.7 4.7 %collective-permute-done.38 = bf16[128,2048]{1,0:T(8,128)(2,1)S(1)} collective-permute-done((bf16[128,2048]{1,0:T(8,128)(2,1)S(1)}, bf16[128,2048]{1,0:T(8,128)(2,1)S(1)}, u32[]{:S(2)}, u32[]{:S(2)}) %collective-permute-start.38) | collective-permute-done | bytes 524320 | tf_op jit(solution)/shard_map/ppermute | solution.py:463
  132.5 1.8 collective-permute-start.39
  135.7 7.2 %attn_bwd.1 = (bf16[512,768]{1,0:T(8,128)(2,1)S(1)}, bf16[128,1152]{1,0:T(8,128)(2,1)S(1)}, bf16[128,1152]{1,0:T(8,128)(2,1)S(1)}, bf16[128,1152]{1,0:T(8,128)(2...) custom-call(s32[8]{0:T(128)S(1)} %stack.83.idx, ...), custom_call_target="tpu_custom_call" | custom-call | flops 1610612736 | bytes 11272224 | tf_op jit(solution)/shard_map/attn_bwd/pallas_call | solution.py:49
  151.0 9.3 %collective-permute-done.41 = bf16[256,1152]{1,0:T(8,128)(2,1)S(1)} collective-permute-done((bf16[256,1152]{1,0:T(8,128)(2,1)S(1)}, bf16[256,1152]{1,0:T(8,128)(2,1)S(1)}, u32[]{:S(2)}, u32[]{:S(2)}) %collective-permute-start.41) | collective-permute-done | bytes 589856 | tf_op jit(solution)/shard_map/ppermute | solution.py:463
  160.4 2.4 %collective-permute-start.42 = (bf16[128,1152]{1,0:T(8,128)(2,1)S(1)}, bf16[128,1152]{1,0:T(8,128)(2,1)S(1)}, u32[]{:S(2)}, u32[]{:S(2)}) collective-permute-start(bf16[128,1152]{1,0:T(8,128)(2,1)S(1)} %add_convert_fusion.11), channel_id=1, source_target_pairs={{0,8},{4,12},{8,16},{12,20},{16,24},{20,28},{24,0},{28,4},{1,9},{5... | collective-permute-start | bytes 884744 | tf_op jit(solution)/shard_map/ppermute | solution.py:479
  165.1 5.8 %collective-permute-done.42 = bf16[128,1152]{1,0:T(8,128)(2,1)S(1)} collective-permute-done((bf16[128,1152]{1,0:T(8,128)(2,1)S(1)}, bf16[128,1152]{1,0:T(8,128)(2,1)S(1)}, u32[]{:S(2)}, u32[]{:S(2)}) %collective-permute-start.42) | collective-permute-done | bytes 294944 | tf_op jit(solution)/shard_map/ppermute | solution.py:479
  173.6 2.6 %place_mixed.1 = bf16[2,512,1024]{2,1,0:T(8,128)(2,1)} custom-call(s32[5]{0:T(128)S(1)} %stack.74.meta, s32[2,1,256]{2,1,0:T(1,128)S(1)} %broadcast_in_dim.14.pos_ref, bf16[2,512,1024]{2,1,0:T(8,128)(2,1)S(1)} %copy-done.4, bf16[256,1024]{1,0:T(8,128)(2,1)S(1)} %get-tuple-element.259.own_ref, bf16[256,1024]{1,0:T(8,128)(2,1)S(1)} %collective-permute-done.34.oth_ref), custom_call_target="tpu_custom_call" | custom-call | flops 536870912 | bytes 5244948 | tf_op jit(solution)/shard_map/place_mixed/pallas_call | solution.py:49
  176.2 4.3 %collective-permute-done.43 = bf16[128,1152]{1,0:T(8,128)(2,1)S(1)} collective-permute-done((bf16[128,1152]{1,0:T(8,128)(2,1)S(1)}, bf16[128,1152]{1,0:T(8,128)(2,1)S(1)}, u32[]{:S(2)}, u32[]{:S(2)}) %collective-permute-start.43) | collective-permute-done | bytes 294944 | tf_op jit(solution)/shard_map/ppermute | solution.py:479
  180.8 9.5 %collective-permute-done.46.a1 = bf16[256,1152]{1,0:T(8,128)(2,1)S(1)} collective-permute-done((bf16[256,1152]{1,0:T(8,128)(2,1)S(1)}, bf16[256,1152]{1,0:T(8,128)(2,1)S(1)}, u32[]{:S(2)}, u32[]{:S(2)}) %collective-permute-start.46) | collective-permute-done | bytes 589856 | tf_op jit(solution)/shard_map/ppermute | solution.py:463
  192.1 2.6 %place_input_grad.1 = bf16[2,512,1024]{2,1,0:T(8,128)(2,1)} custom-call(s32[5]{0:T(128)S(1)} %stack.74.meta, s32[2,1,256]{2,1,0:T(1,128)S(1)} %broadcast_in_dim.14.pos_ref, bf16[2,512,1024]{2,1,0:T(8,128)(2,1)S(1)} %copy-done.5, bf16[256,1024]{1,0:T(8,128)(2,1)S(1)} %input_grad.1.own_ref, bf16[256,1024]{1,0:T(8,128)(2,1)S(1)} %collective-permute-done.35.oth_ref), custom_call_target="tpu_custom_call" | custom-call | flops 536870912 | bytes 5244948 | tf_op jit(solution)/shard_map/place_input_grad/pallas_call | solution.py:49
  194.7 5.2 %collective-permute-done.37.m1 = bf16[128,2048]{1,0:T(8,128)(2,1)S(1)} collective-permute-done((bf16[128,2048]{1,0:T(8,128)(2,1)S(1)}, bf16[128,2048]{1,0:T(8,128)(2,1)S(1)}, u32[]{:S(2)}, u32[]{:S(2)}) %collective-permute-start.37) | collective-permute-done | bytes 524320 | tf_op jit(solution)/shard_map/ppermute | solution.py:463
  201.5 1.9 split.1
  206.8 2.9 %collective-permute-done.49.c2 = bf16[32,1920]{1,0:T(8,128)(2,1)S(1)} collective-permute-done((bf16[32,1920]{1,0:T(8,128)(2,1)S(1)}, bf16[32,1920]{1,0:T(8,128)(2,1)S(1)}, u32[]{:S(2)}, u32[]{:S(2)}) %collective-permute-start.49) | collective-permute-done | bytes 122912 | tf_op jit(solution)/shard_map/ppermute | solution.py:463
  209.6 1.7 collective-permute-done.50.c3
  212.0 2.2 %final.1 = (f32[32,3072]{1,0:T(8,128)}, f32[32,4096]{1,0:T(8,128)}, f32[8,128]{1,0:T(8,128)S(1)}) custom-call(s32[5]{0:T(128)S(1)} %stack.74.meta, f32[32,1920]{1,0:T(8,128)S(1)} %get-tuple-element.300.c0, bf16[32,1920]{1,0:T(8,128)(2,1)} %copy-done.18, bf16[32,1920]{1,0:T(8,128)(2,1)} %copy-done.19, bf16[32,1920]{1,0:T(8,128)(2,1)} %copy-done.20), custom_call_target="tpu_custom_call" | custom-call | bytes 1536020 | tf_op jit(solution)/shard_map/final/pallas_call | solution.py:49
  (188 shorter events, 66.3 us)
Async XLA Ops:
  7.9 11.9 %collective-permute-start.4 = (bf16[256,1024]{1,0:T(8,128)(2,1)S(1)}, bf16[256,1024]{1,0:T(8,128)(2,1)S(1)}, u32[]{:S(2)}, u32[]{:S(2)}) collective-permute-start(bf16[256,1024]{1,0:T(8,128)(2,1)S(1)} %get-tuple-element.170), channel_id=1, source_target_pairs={{0,1},{1,0},{2,3},{3,2},{4,5},{5,4},{6,7},{7,6},{8,9},{9,8},{10,11... | collective-permute-start | bytes 1572872 | tf_op jit(solution)/shard_map/ppermute | solution.py:463
  20.0 11.6 %collective-permute-start.9 = (bf16[128,1152]{1,0:T(8,128)(2,1)S(1)}, bf16[128,1152]{1,0:T(8,128)(2,1)}, u32[]{:S(2)}, u32[]{:S(2)}) collective-permute-start(bf16[128,1152]{1,0:T(8,128)(2,1)S(1)} %get-tuple-element.176.refs_0_), channel_id=1, source_target_pairs={{0,8},{4,12},{8,16},{12,20},{16,24},{20,28},{24,0},{28,4},{1,9},{5... | collective-permute-start | bytes 884744 | tf_op jit(solution)/shard_map/ppermute | solution.py:479
  21.6 14.9 %collective-permute-start.10 = (bf16[128,2048]{1,0:T(8,128)(2,1)}, bf16[128,2048]{1,0:T(8,128)(2,1)S(1)}, u32[]{:S(2)}, u32[]{:S(2)}) collective-permute-start(bf16[128,2048]{1,0:T(8,128)(2,1)} %get-tuple-element.172.refs_0_), channel_id=1, source_target_pairs={{0,4},{4,0},{8,12},{12,8},{16,20},{20,16},{24,28},{28,24},{1,5},{5... | collective-permute-start | bytes 1572872 | tf_op jit(solution)/shard_map/ppermute | solution.py:463
  23.2 19.5 %collective-permute-start.5 = (bf16[256,1024]{1,0:T(8,128)(2,1)S(1)}, bf16[256,1024]{1,0:T(8,128)(2,1)S(1)}, u32[]{:S(2)}, u32[]{:S(2)}) collective-permute-start(bf16[256,1024]{1,0:T(8,128)(2,1)S(1)} %add_convert_fusion.8), channel_id=1, source_target_pairs={{0,2},{1,3},{2,0},{3,1},{4,6},{5,7},{6,4},{7,5},{8,10},{9,11},{10,... | collective-permute-start | bytes 1572872 | tf_op jit(solution)/shard_map/ppermute | solution.py:463
  31.6 11.4 %collective-permute-start.8 = (bf16[128,1152]{1,0:T(8,128)(2,1)S(1)}, bf16[128,1152]{1,0:T(8,128)(2,1)S(1)}, u32[]{:S(2)}, u32[]{:S(2)}) collective-permute-start(bf16[128,1152]{1,0:T(8,128)(2,1)S(1)} %get-tuple-element.176.refs_0_), channel_id=1, source_target_pairs={{0,4},{4,0},{8,12},{12,8},{16,20},{20,16},{24,28},{28,24},{1,5},{5... | collective-permute-start | bytes 884744 | tf_op jit(solution)/shard_map/ppermute | solution.py:463
  35.2 22.4 %collective-permute-start.19 = (bf16[256,1024]{1,0:T(8,128)(2,1)}, bf16[256,1024]{1,0:T(8,128)(2,1)}, u32[]{:S(2)}, u32[]{:S(2)}) collective-permute-start(bf16[256,1024]{1,0:T(8,128)(2,1)} %get-tuple-element.206), channel_id=1, source_target_pairs={{0,1},{1,0},{2,3},{3,2},{4,5},{5,4},{6,7},{7,6},{8,9},{9,8},{10,11... | collective-permute-start | bytes 1572872 | tf_op jit(solution)/shard_map/ppermute | solution.py:463
  36.6 12.3 %collective-permute-start.11 = (bf16[128,1152]{1,0:T(8,128)(2,1)}, bf16[128,1152]{1,0:T(8,128)(2,1)}, u32[]{:S(2)}, u32[]{:S(2)}) collective-permute-start(bf16[128,1152]{1,0:T(8,128)(2,1)} %collective-permute-done.9.refs_2_), channel_id=1, source_target_pairs={{0,4},{4,0},{8,12},{12,8},{16,20},{20,16},{24,28},{28,24},{1,5},{5... | collective-permute-start | bytes 884744 | tf_op jit(solution)/shard_map/ppermute | solution.py:463
  42.5 12.1 %collective-permute-start.14 = (bf16[128,1152]{1,0:T(8,128)(2,1)}, bf16[128,1152]{1,0:T(8,128)(2,1)}, u32[]{:S(2)}, u32[]{:S(2)}) collective-permute-start(bf16[128,1152]{1,0:T(8,128)(2,1)} %collective-permute-done.12.refs_4_), channel_id=1, source_target_pairs={{0,8},{4,12},{8,16},{12,20},{16,24},{20,28},{24,0},{28,4},{1,9},{5... | collective-permute-start | bytes 884744 | tf_op jit(solution)/shard_map/ppermute | solution.py:479
  42.7 21.0 %collective-permute-start.7 = (bf16[128,2048]{1,0:T(8,128)(2,1)}, bf16[128,2048]{1,0:T(8,128)(2,1)}, u32[]{:S(2)}, u32[]{:S(2)}) collective-permute-start(bf16[128,2048]{1,0:T(8,128)(2,1)} %get-tuple-element.172.refs_0_), channel_id=1, source_target_pairs={{0,8},{4,12},{8,16},{12,20},{16,24},{20,28},{24,0},{28,4},{1,9},{5... | collective-permute-start | bytes 1572872 | tf_op jit(solution)/shard_map/ppermute | solution.py:479
  43.0 22.3 %collective-permute-start.6 = (bf16[256,1024]{1,0:T(8,128)(2,1)S(1)}, bf16[256,1024]{1,0:T(8,128)(2,1)}, u32[]{:S(2)}, u32[]{:S(2)}) collective-permute-start(bf16[256,1024]{1,0:T(8,128)(2,1)S(1)} %add.96.xo_ref.x_ref), channel_id=1, source_target_pairs={{0,1},{1,0},{2,3},{3,2},{4,5},{5,4},{6,7},{7,6},{8,9},{9,8},{10,11... | collective-permute-start | bytes 1572872 | tf_op jit(solution)/shard_map/ppermute | solution.py:463
  48.8 14.9 %collective-permute-start.13 = (bf16[128,1152]{1,0:T(8,128)(2,1)}, bf16[128,1152]{1,0:T(8,128)(2,1)S(1)}, u32[]{:S(2)}, u32[]{:S(2)}) collective-permute-start(bf16[128,1152]{1,0:T(8,128)(2,1)} %collective-permute-done.12.refs_4_), channel_id=1, source_target_pairs={{0,4},{4,0},{8,12},{12,8},{16,20},{20,16},{24,28},{28,24},{1,5},{5... | collective-permute-start | bytes 884744 | tf_op jit(solution)/shard_map/ppermute | solution.py:463
  58.8 14.8 %collective-permute-start.20 = (bf16[256,1024]{1,0:T(8,128)(2,1)S(1)}, bf16[256,1024]{1,0:T(8,128)(2,1)S(1)}, u32[]{:S(2)}, u32[]{:S(2)}) collective-permute-start(bf16[256,1024]{1,0:T(8,128)(2,1)S(1)} %add_convert_fusion.6), channel_id=1, source_target_pairs={{0,2},{1,3},{2,0},{3,1},{4,6},{5,7},{6,4},{7,5},{8,10},{9,11},{10,... | collective-permute-start | bytes 1572872 | tf_op jit(solution)/shard_map/ppermute | solution.py:463
  63.7 13.9 %collective-permute-start.22 = (bf16[128,2048]{1,0:T(8,128)(2,1)}, bf16[128,2048]{1,0:T(8,128)(2,1)S(1)}, u32[]{:S(2)}, u32[]{:S(2)}) collective-permute-start(bf16[128,2048]{1,0:T(8,128)(2,1)} %collective-permute-done.7.refs_2_), channel_id=1, source_target_pairs={{0,8},{4,12},{8,16},{12,20},{16,24},{20,28},{24,0},{28,4},{1,9},{5... | collective-permute-start | bytes 1572872 | tf_op jit(solution)/shard_map/ppermute | solution.py:479
  63.8 15.4 %collective-permute-start.17 = (bf16[128,2048]{1,0:T(8,128)(2,1)}, bf16[128,2048]{1,0:T(8,128)(2,1)S(1)}, u32[]{:S(2)}, u32[]{:S(2)}) collective-permute-start(bf16[128,2048]{1,0:T(8,128)(2,1)} %collective-permute-done.7.refs_2_), channel_id=1, source_target_pairs={{0,4},{4,0},{8,12},{12,8},{16,20},{20,16},{24,28},{28,24},{1,5},{5... | collective-permute-start | bytes 1572872 | tf_op jit(solution)/shard_map/ppermute | solution.py:463
  73.9 18.0 %collective-permute-start.21 = (bf16[256,1024]{1,0:T(8,128)(2,1)S(1)}, bf16[256,1024]{1,0:T(8,128)(2,1)S(1)}, u32[]{:S(2)}, u32[]{:S(2)}) collective-permute-start(bf16[256,1024]{1,0:T(8,128)(2,1)S(1)} %add.99.co_ref.c_ref), channel_id=1, source_target_pairs={{0,1},{1,0},{2,3},{3,2},{4,5},{5,4},{6,7},{7,6},{8,9},{9,8},{10,11... | collective-permute-start | bytes 1572872 | tf_op jit(solution)/shard_map/ppermute | solution.py:463
  77.6 12.9 %collective-permute-start.25 = (bf16[128,2048]{1,0:T(8,128)(2,1)S(1)}, bf16[128,2048]{1,0:T(8,128)(2,1)S(1)}, u32[]{:S(2)}, u32[]{:S(2)}) collective-permute-start(bf16[128,2048]{1,0:T(8,128)(2,1)S(1)} %collective-permute-done.22.refs_4_), channel_id=1, source_target_pairs={{0,8},{4,12},{8,16},{12,20},{16,24},{20,28},{24,0},{28,4},{1,9},{5... | collective-permute-start | bytes 1572872 | tf_op jit(solution)/shard_map/ppermute | solution.py:479
  77.6 14.2 %collective-permute-start.23 = (bf16[128,2048]{1,0:T(8,128)(2,1)S(1)}, bf16[128,2048]{1,0:T(8,128)(2,1)S(1)}, u32[]{:S(2)}, u32[]{:S(2)}) collective-permute-start(bf16[128,2048]{1,0:T(8,128)(2,1)S(1)} %collective-permute-done.22.refs_4_), channel_id=1, source_target_pairs={{0,4},{4,0},{8,12},{12,8},{16,20},{20,16},{24,28},{28,24},{1,5},{5... | collective-permute-start | bytes 1572872 | tf_op jit(solution)/shard_map/ppermute | solution.py:463
  79.3 12.6 %collective-permute-start.18 = (bf16[256,1024]{1,0:T(8,128)(2,1)S(1)}, bf16[256,1024]{1,0:T(8,128)(2,1)S(1)}, u32[]{:S(2)}, u32[]{:S(2)}) collective-permute-start(bf16[256,1024]{1,0:T(8,128)(2,1)S(1)} %add_convert_fusion.7.t_ref.bt_ref.at_ref), channel_id=1, source_target_pairs={{0,2},{1,3},{2,0},{3,1},{4,6},{5,7},{6,4},{7,5},{8,10},{9,11},{10,... | collective-permute-start | bytes 1572872 | tf_op jit(solution)/shard_map/ppermute | solution.py:463
  112.7 14.0 %collective-permute-start.28 = (bf16[256,1024]{1,0:T(8,128)(2,1)S(1)}, bf16[256,1024]{1,0:T(8,128)(2,1)S(1)}, u32[]{:S(2)}, u32[]{:S(2)}) collective-permute-start(bf16[256,1024]{1,0:T(8,128)(2,1)S(1)} %add_convert_fusion.5.dt_ref), channel_id=1, source_target_pairs={{0,2},{1,3},{2,0},{3,1},{4,6},{5,7},{6,4},{7,5},{8,10},{9,11},{10,... | collective-permute-start | bytes 1572872 | tf_op jit(solution)/shard_map/ppermute | solution.py:463
  117.5 14.9 %collective-permute-start.38 = (bf16[128,2048]{1,0:T(8,128)(2,1)S(1)}, bf16[128,2048]{1,0:T(8,128)(2,1)S(1)}, u32[]{:S(2)}, u32[]{:S(2)}) collective-permute-start(bf16[128,2048]{1,0:T(8,128)(2,1)S(1)} %get-tuple-element.279), channel_id=1, source_target_pairs={{0,4},{4,0},{8,12},{12,8},{16,20},{20,16},{24,28},{28,24},{1,5},{5... | collective-permute-start | bytes 1572872 | tf_op jit(solution)/shard_map/ppermute | solution.py:463
  124.9 19.7 %collective-permute-start.36 = (bf16[128,2048]{1,0:T(8,128)(2,1)S(1)}, bf16[128,2048]{1,0:T(8,128)(2,1)S(1)}, u32[]{:S(2)}, u32[]{:S(2)}) collective-permute-start(bf16[128,2048]{1,0:T(8,128)(2,1)S(1)} %get-tuple-element.272), channel_id=1, source_target_pairs={{0,4},{4,0},{8,12},{12,8},{16,20},{20,16},{24,28},{28,24},{1,5},{5... | collective-permute-start | bytes 1572872 | tf_op jit(solution)/shard_map/ppermute | solution.py:463
  132.5 14.7 %collective-permute-start.39 = (bf16[128,2048]{1,0:T(8,128)(2,1)S(1)}, bf16[128,2048]{1,0:T(8,128)(2,1)S(1)}, u32[]{:S(2)}, u32[]{:S(2)}) collective-permute-start(bf16[128,2048]{1,0:T(8,128)(2,1)S(1)} %add_convert_fusion.2), channel_id=1, source_target_pairs={{0,8},{4,12},{8,16},{12,20},{16,24},{20,28},{24,0},{28,4},{1,9},{5... | collective-permute-start | bytes 1572872 | tf_op jit(solution)/shard_map/ppermute | solution.py:479
  134.5 12.6 %collective-permute-start.33 = (bf16[256,1024]{1,0:T(8,128)(2,1)S(1)}, bf16[256,1024]{1,0:T(8,128)(2,1)S(1)}, u32[]{:S(2)}, u32[]{:S(2)}) collective-permute-start(bf16[256,1024]{1,0:T(8,128)(2,1)S(1)} %add_convert_fusion.3.mt_ref), channel_id=1, source_target_pairs={{0,2},{1,3},{2,0},{3,1},{4,6},{5,7},{6,4},{7,5},{8,10},{9,11},{10,... | collective-permute-start | bytes 1572872 | tf_op jit(solution)/shard_map/ppermute | solution.py:463
  144.6 15.7 %collective-permute-start.41 = (bf16[256,1152]{1,0:T(8,128)(2,1)S(1)}, bf16[256,1152]{1,0:T(8,128)(2,1)S(1)}, u32[]{:S(2)}, u32[]{:S(2)}) collective-permute-start(bf16[256,1152]{1,0:T(8,128)(2,1)S(1)} %get-tuple-element.283), channel_id=1, source_target_pairs={{0,4},{4,0},{8,12},{12,8},{16,20},{20,16},{24,28},{28,24},{1,5},{5... | collective-permute-start | bytes 1769480 | tf_op jit(solution)/shard_map/ppermute | solution.py:463
  147.4 16.9 %collective-permute-start.40 = (bf16[128,2048]{1,0:T(8,128)(2,1)S(1)}, bf16[128,2048]{1,0:T(8,128)(2,1)S(1)}, u32[]{:S(2)}, u32[]{:S(2)}) collective-permute-start(bf16[128,2048]{1,0:T(8,128)(2,1)S(1)} %add_convert_fusion.1), channel_id=1, source_target_pairs={{0,8},{4,12},{8,16},{12,20},{16,24},{20,28},{24,0},{28,4},{1,9},{5... | collective-permute-start | bytes 1572872 | tf_op jit(solution)/shard_map/ppermute | solution.py:479
  149.2 15.0 %collective-permute-start.34 = (bf16[256,1024]{1,0:T(8,128)(2,1)S(1)}, bf16[256,1024]{1,0:T(8,128)(2,1)S(1)}, u32[]{:S(2)}, u32[]{:S(2)}) collective-permute-start(bf16[256,1024]{1,0:T(8,128)(2,1)S(1)} %get-tuple-element.259.own_ref), channel_id=1, source_target_pairs={{0,1},{1,0},{2,3},{3,2},{4,5},{5,4},{6,7},{7,6},{8,9},{9,8},{10,11... | collective-permute-start | bytes 1572872 | tf_op jit(solution)/shard_map/ppermute | solution.py:463
  149.5 14.8 %collective-permute-start.31 = (bf16[256,1024]{1,0:T(8,128)(2,1)S(1)}, bf16[256,1024]{1,0:T(8,128)(2,1)S(1)}, u32[]{:S(2)}, u32[]{:S(2)}) collective-permute-start(bf16[256,1024]{1,0:T(8,128)(2,1)S(1)} %add_convert_fusion.4.t_ref), channel_id=1, source_target_pairs={{0,2},{1,3},{2,0},{3,1},{4,6},{5,7},{6,4},{7,5},{8,10},{9,11},{10,... | collective-permute-start | bytes 1572872 | tf_op jit(solution)/shard_map/ppermute | solution.py:463
  162.8 17.7 %collective-permute-start.44 = (bf16[128,2048]{1,0:T(8,128)(2,1)S(1)}, bf16[128,2048]{1,0:T(8,128)(2,1)S(1)}, u32[]{:S(2)}, u32[]{:S(2)}) collective-permute-start(bf16[128,2048]{1,0:T(8,128)(2,1)S(1)} %get-tuple-element.290), channel_id=1, source_target_pairs={{0,4},{4,0},{8,12},{12,8},{16,20},{20,16},{24,28},{28,24},{1,5},{5... | collective-permute-start | bytes 1572872 | tf_op jit(solution)/shard_map/ppermute | solution.py:463
  165.0 15.5 %collective-permute-start.35 = (bf16[256,1024]{1,0:T(8,128)(2,1)S(1)}, bf16[256,1024]{1,0:T(8,128)(2,1)S(1)}, u32[]{:S(2)}, u32[]{:S(2)}) collective-permute-start(bf16[256,1024]{1,0:T(8,128)(2,1)S(1)} %input_grad.1.own_ref), channel_id=1, source_target_pairs={{0,1},{1,0},{2,3},{3,2},{4,5},{5,4},{6,7},{7,6},{8,9},{9,8},{10,11... | collective-permute-start | bytes 1572872 | tf_op jit(solution)/shard_map/ppermute | solution.py:463
  171.5 18.8 %collective-permute-start.46 = (bf16[256,1152]{1,0:T(8,128)(2,1)S(1)}, bf16[256,1152]{1,0:T(8,128)(2,1)S(1)}, u32[]{:S(2)}, u32[]{:S(2)}) collective-permute-start(bf16[256,1152]{1,0:T(8,128)(2,1)S(1)} %get-tuple-element.296), channel_id=1, source_target_pairs={{0,4},{4,0},{8,12},{12,8},{16,20},{20,16},{24,28},{28,24},{1,5},{5... | collective-permute-start | bytes 1769480 | tf_op jit(solution)/shard_map/ppermute | solution.py:463
  173.0 26.9 %collective-permute-start.37 = (bf16[128,2048]{1,0:T(8,128)(2,1)S(1)}, bf16[128,2048]{1,0:T(8,128)(2,1)S(1)}, u32[]{:S(2)}, u32[]{:S(2)}) collective-permute-start(bf16[128,2048]{1,0:T(8,128)(2,1)S(1)} %get-tuple-element.275), channel_id=1, source_target_pairs={{0,4},{4,0},{8,12},{12,8},{16,20},{20,16},{24,28},{28,24},{1,5},{5... | collective-permute-start | bytes 1572872 | tf_op jit(solution)/shard_map/ppermute | solution.py:463
  180.8 19.8 %collective-permute-start.45 = (bf16[128,2048]{1,0:T(8,128)(2,1)S(1)}, bf16[128,2048]{1,0:T(8,128)(2,1)S(1)}, u32[]{:S(2)}, u32[]{:S(2)}) collective-permute-start(bf16[128,2048]{1,0:T(8,128)(2,1)S(1)} %add_convert_fusion), channel_id=1, source_target_pairs={{0,8},{4,12},{8,16},{12,20},{16,24},{20,28},{24,0},{28,4},{1,9},{5... | collective-permute-start | bytes 1572872 | tf_op jit(solution)/shard_map/ppermute | solution.py:479
  (52 other events, 455.5 us)

commit v5 on v3

--- a/solution.py
+++ b/solution.py
@@ -593,7 +593,8 @@
     def pick(source, name):
         return call(
             pick_body, (meta, pos_col, source), (half, half), smem=1,
-            flops=4 * rows * span * width, name=name, keep=False, limit=24,
+            flops=4 * rows * span * width, name=name, keep_out=False, cold=(2,), free=(1,),
+            limit=24,
         )
 
     gains = jnp.stack([attn_gain, mlp_gain, router_weight], axis=1)
@@ -687,7 +688,8 @@
         smem=1,
         flops=2 * both * width * width,
         name="attn_fwd",
-        cold=range(1, 13),
+        cold=range(1, 12),
+        free=(12,),
     )
     v.a, v.mix = a, mix
     v.tb = add(ba_o, swap_core(ba_t))
@@ -723,7 +725,8 @@
         smem=1,
         flops=6 * both * width * ff,
         name="mlp",
-        cold=(2, 3, 4, *range(6, 14)),
+        cold=(2, 3, 4, *range(6, 13)),
+        free=(13,),
     )
 
     v.du = du
@@ -767,7 +770,7 @@
     chain.clear()
     v.__dict__.update({n + str(k): None for n in ("xm", "xa") for k in range(4)})
     if not native:
-        for n, k in (('m', 1), ('m', 2)):
+        for n, k in (('m', 1),):
             side("x%s%d" % (n, k), parts[n][2 * k + 1], 2)
     v.sync("yd", "td", "bm")
     da_own, dh = call(
@@ -851,7 +854,7 @@
         for k in range(4):
             v["m%d" % k], v["a%d" % k] = mlp_grads[2 * k], attn_grads[k]
         v.ym = swap_pair(v.tm)
-        for n, k in (('m', 3), ('a', 4), ('m', 0), ('a', 5)):
+        for n, k in (('m', 2), ('m', 3), ('a', 4), ('m', 0), ('a', 5)):
             side("x%s%d" % (n, k), parts[n][2 * k + 1 if n == "m" else k], 2)
         blk = width // BLOCKS
         v.tx2 = add(v.dxm, swap_core(v.dxs))
@@ -889,7 +892,7 @@
             (meta, v.m0, v.xm0, v.zm3, v.a0, v.xa5, v.za3),
             (*piece, out((4 * mine, width), f32), out((mine, width), f32)),
             scratch=[pltpu.VMEM((4 * mine, ff), f32), pltpu.VMEM((4 * mine, head), f32)], smem=1,
-            name="split", cold=(2, 3, 5, 6),
+            name="split", cold=(2, 3), free=(5, 6),
         )
         cut = [cut[0]] + [flip_bit(cut[k], "grp", 4, k) for k in range(1, 4)]
         out_moved = lax.ppermute(og, ("seq", "grp"), swaps)

time: 216 us -> 215 us (level)
    ppermute x12, waiting for transfers between devices: 39.4 us -> 42.7 us  [shift_one(): return lax.ppermute(v, 'seq', [(i, (i + 2) % seqs) for i in range(seqs)])]
    unnamed x67 -> x61, local copies, waits for them, and re-layouts: 6.23 us -> 5.19 us
  transfers between devices with their start and end apart: 52 -> 52, of which waited for: 23 -> 23; matrix products, arithmetic and copies ran while one was open for 3% -> 2% of each run, Pallas kernels for 19% -> 19%
where the time goes in v5:
time: 215 us; the launch traced here: 214 us
  waiting for transfers between devices  100 us (47%)
  Pallas kernels  53.6 us (25%)
  starting transfers between devices  45.1 us (21%)
  local copies, waits for them, and re-layouts  8.96 us (4%)
  other arithmetic  4.84 us (2%)
    ppermute x38, waiting for transfers between devices, flip_bit(): return lax.ppermute(v, axis, [(i, i ^ mask) for i in range(size)])  57.7 us
    pallas_call x19, Pallas kernels, call(): pl.pallas_call(body, out_shape=shapes, in_specs=[SM] * smem + [VM] * (len...  53.6 us
    ppermute x12, waiting for transfers between devices, shift_one(): return lax.ppermute(v, 'seq', [(i, (i + 2) % seqs) for i in range(seqs)])  42.7 us
    ppermute x38, starting transfers between devices, flip_bit(): return lax.ppermute(v, axis, [(i, i ^ mask) for i in range(size)])  33.3 us
    ppermute x12, starting transfers between devices, shift_one(): return lax.ppermute(v, 'seq', [(i, (i + 2) % seqs) for i in range(seqs)])  10.6 us
    unnamed x61, local copies, waits for them, and re-layouts  5.19 us
  transfers between devices with their start and end apart: 52, of which 23 were waited for; matrix products, arithmetic and copies ran while one was open for 2% of the time, Pallas kernels for 19%

profile of v5, /device:TPU:0, one launch (start us, length us, event | category | flops | bytes accessed | tf_op | source)
XLA Modules:
  0.0 214.3 jit_solution(16537739336683817498)
XLA Ops:
  5.0 2.4 %pick_tokens.1 = (bf16[256,1024]{1,0:T(8,128)(2,1)S(1)}, bf16[256,1024]{1,0:T(8,128)(2,1)S(1)}) custom-call(s32[5]{0:T(128)S(1)} %stack.74.meta, s32[2,256,1]{2,1,0:T(8,128)S(1)} %copy.33.pos_ref, bf16[2,512,1024]{2,1,0:T(8,128)(2,1)} %base_ref.2), custom_call_target="tpu_custom_call" | custom-call | flops 536870912 | bytes 3147796 | tf_op jit(solution)/shard_map/pick_tokens/pallas_call | solution.py:49
  7.9 3.0 %collective-permute-start.1 = (bf16[32,1920]{1,0:T(8,128)(2,1)S(1)}, bf16[32,1920]{1,0:T(8,128)(2,1)S(1)}, u32[]{:S(2)}, u32[]{:S(2)}) collective-permute-start(bf16[32,1920]{1,0:T(8,128)(2,1)S(1)} %get-tuple-element.170), channel_id=1, source_target_pairs={{0,2},{1,3},{2,0},{3,1},{4,6},{5,7},{6,4},{7,5},{8,10},{9,11},{10,... | collective-permute-start | bytes 368648 | tf_op jit(solution)/shard_map/ppermute | solution.py:463
  11.6 3.4 %collective-permute-done.1.c2 = bf16[32,1920]{1,0:T(8,128)(2,1)S(1)} collective-permute-done((bf16[32,1920]{1,0:T(8,128)(2,1)S(1)}, bf16[32,1920]{1,0:T(8,128)(2,1)S(1)}, u32[]{:S(2)}, u32[]{:S(2)}) %collective-permute-start.1) | collective-permute-done | bytes 122912 | tf_op jit(solution)/shard_map/ppermute | solution.py:463
  23.3 7.0 %collective-permute-done.9.refs_2_ = bf16[128,1152]{1,0:T(8,128)(2,1)} collective-permute-done((bf16[128,1152]{1,0:T(8,128)(2,1)S(1)}, bf16[128,1152]{1,0:T(8,128)(2,1)}, u32[]{:S(2)}, u32[]{:S(2)}) %collective-permute-start.9) | collective-permute-done | bytes 294944 | tf_op jit(solution)/shard_map/ppermute | solution.py:479
  31.8 2.4 %pick_cotangent.1 = (bf16[256,1024]{1,0:T(8,128)(2,1)S(1)}, bf16[256,1024]{1,0:T(8,128)(2,1)S(1)}) custom-call(s32[5]{0:T(128)S(1)} %stack.74.meta, s32[2,256,1]{2,1,0:T(8,128)S(1)} %copy.33.pos_ref, bf16[2,512,1024]{2,1,0:T(8,128)(2,1)} %base_ref.3), custom_call_target="tpu_custom_call" | custom-call | flops 536870912 | bytes 3147796 | tf_op jit(solution)/shard_map/pick_cotangent/pallas_call | solution.py:49
  36.7 4.6 %collective-permute-done.12.refs_4_ = bf16[128,1152]{1,0:T(8,128)(2,1)} collective-permute-done((bf16[128,1152]{1,0:T(8,128)(2,1)}, bf16[128,1152]{1,0:T(8,128)(2,1)}, u32[]{:S(2)}, u32[]{:S(2)}) %collective-permute-start.12) | collective-permute-done | bytes 294944 | tf_op jit(solution)/shard_map/ppermute | solution.py:479
  42.7 4.7 %collective-permute-done.11.refs_3_ = bf16[128,1152]{1,0:T(8,128)(2,1)} collective-permute-done((bf16[128,1152]{1,0:T(8,128)(2,1)}, bf16[128,1152]{1,0:T(8,128)(2,1)}, u32[]{:S(2)}, u32[]{:S(2)}) %collective-permute-start.11) | collective-permute-done | bytes 294944 | tf_op jit(solution)/shard_map/ppermute | solution.py:463
  48.8 4.5 %collective-permute-done.14.refs_6_ = bf16[128,1152]{1,0:T(8,128)(2,1)} collective-permute-done((bf16[128,1152]{1,0:T(8,128)(2,1)}, bf16[128,1152]{1,0:T(8,128)(2,1)}, u32[]{:S(2)}, u32[]{:S(2)}) %collective-permute-start.14) | collective-permute-done | bytes 294944 | tf_op jit(solution)/shard_map/ppermute | solution.py:479
  58.0 4.4 %collective-permute-done.7.refs_2_ = bf16[128,2048]{1,0:T(8,128)(2,1)} collective-permute-done((bf16[128,2048]{1,0:T(8,128)(2,1)S(1)}, bf16[128,2048]{1,0:T(8,128)(2,1)}, u32[]{:S(2)}, u32[]{:S(2)}) %collective-permute-start.7) | collective-permute-done | bytes 524320 | tf_op jit(solution)/shard_map/ppermute | solution.py:479
  64.5 8.2 %attn_fwd.1 = (bf16[512,1024]{1,0:T(8,128)(2,1)S(1)}, bf16[512,768]{1,0:T(8,128)(2,1)S(1)}, f32[8,256,256]{2,1,0:T(8,128)S(1)}, bf16[512,256]{1,0:T(8,128)(2,1)S...) custom-call(s32[8]{0:T(128)S(1)} %stack.83.idx, ...), custom_call_target="tpu_custom_call" | custom-call | flops 1073741824 | bytes 11309088 | tf_op jit(solution)/shard_map/attn_fwd/pallas_call | solution.py:49
  73.5 2.8 %collective-permute-done.22.refs_4_ = bf16[128,2048]{1,0:T(8,128)(2,1)S(1)} collective-permute-done((bf16[128,2048]{1,0:T(8,128)(2,1)}, bf16[128,2048]{1,0:T(8,128)(2,1)S(1)}, u32[]{:S(2)}, u32[]{:S(2)}) %collective-permute-start.22) | collective-permute-done | bytes 524320 | tf_op jit(solution)/shard_map/ppermute | solution.py:479
  79.6 10.1 %collective-permute-done.25.refs_6_ = bf16[128,2048]{1,0:T(8,128)(2,1)S(1)} collective-permute-done((bf16[128,2048]{1,0:T(8,128)(2,1)S(1)}, bf16[128,2048]{1,0:T(8,128)(2,1)S(1)}, u32[]{:S(2)}, u32[]{:S(2)}) %collective-permute-start.25) | collective-permute-done | bytes 524320 | tf_op jit(solution)/shard_map/ppermute | solution.py:479
  91.0 9.4 %collective-permute-done.26.refs_7_ = bf16[128,2048]{1,0:T(8,128)(2,1)S(1)} collective-permute-done((bf16[128,2048]{1,0:T(8,128)(2,1)S(1)}, bf16[128,2048]{1,0:T(8,128)(2,1)S(1)}, u32[]{:S(2)}, u32[]{:S(2)}) %collective-permute-start.26) | collective-permute-done | bytes 524320 | tf_op jit(solution)/shard_map/ppermute | solution.py:463
  101.1 8.6 %mlp.1 = (bf16[512,1024]{1,0:T(8,128)(2,1)S(1)}, bf16[512,1024]{1,0:T(8,128)(2,1)S(1)}, bf16[512,1024]{1,0:T(8,128)(2,1)S(1)}, bf16[1024,1024]{1,0:T(8,128)(2,1)...) custom-call(s32[8]{0:T(128)S(1)} %stack.83.idx, ...), custom_call_target="tpu_custom_call" | custom-call | flops 3221225472 | bytes 14942240 | tf_op jit(solution)/shard_map/mlp/pallas_call | solution.py:49
  113.6 3.2 %early_grad.1 = (f32[1024,128]{1,0:T(8,128)S(1)}, bf16[1024,512]{1,0:T(8,128)(2,1)S(1)}, bf16[1024,512]{1,0:T(8,128)(2,1)S(1)}, bf16[128,2048]{1,0:T(8,128)(2,1)...) custom-call(s32[8]{0:T(128)S(1)} %stack.83.idx, ...), custom_call_target="tpu_custom_call" | custom-call | flops 1073741824 | bytes 11272224 | tf_op jit(solution)/shard_map/early_grad/pallas_call | solution.py:49
  117.4 5.8 %late_grad.1 = (bf16[256,1024]{1,0:T(8,128)(2,1)S(1)}, bf16[256,1024]{1,0:T(8,128)(2,1)S(1)}, f32[1024,128]{1,0:T(8,128)S(1)}, bf16[128,2048]{1,0:T(8,128)(2,1)S...) custom-call(s32[8]{0:T(128)S(1)} %stack.83.idx, ...), custom_call_target="tpu_custom_call" | custom-call | flops 2147483648 | bytes 17039392 | tf_op jit(solution)/shard_map/late_grad/pallas_call | solution.py:49
  126.9 4.7 %collective-permute-done.36 = bf16[128,2048]{1,0:T(8,128)(2,1)S(1)} collective-permute-done((bf16[128,2048]{1,0:T(8,128)(2,1)S(1)}, bf16[128,2048]{1,0:T(8,128)(2,1)S(1)}, u32[]{:S(2)}, u32[]{:S(2)}) %collective-permute-start.36) | collective-permute-done | bytes 524320 | tf_op jit(solution)/shard_map/ppermute | solution.py:463
  134.1 7.2 %attn_bwd.1 = (bf16[512,768]{1,0:T(8,128)(2,1)S(1)}, bf16[128,1152]{1,0:T(8,128)(2,1)S(1)}, bf16[128,1152]{1,0:T(8,128)(2,1)S(1)}, bf16[128,1152]{1,0:T(8,128)(2...) custom-call(s32[8]{0:T(128)S(1)} %stack.83.idx, ...), custom_call_target="tpu_custom_call" | custom-call | flops 1610612736 | bytes 11272224 | tf_op jit(solution)/shard_map/attn_bwd/pallas_call | solution.py:49
  144.4 2.1 collective-permute-done.40
  149.3 9.3 %collective-permute-done.42 = bf16[256,1152]{1,0:T(8,128)(2,1)S(1)} collective-permute-done((bf16[256,1152]{1,0:T(8,128)(2,1)S(1)}, bf16[256,1152]{1,0:T(8,128)(2,1)S(1)}, u32[]{:S(2)}, u32[]{:S(2)}) %collective-permute-start.42) | collective-permute-done | bytes 589856 | tf_op jit(solution)/shard_map/ppermute | solution.py:463
  158.8 2.6 %collective-permute-start.43 = (bf16[128,1152]{1,0:T(8,128)(2,1)S(1)}, bf16[128,1152]{1,0:T(8,128)(2,1)S(1)}, u32[]{:S(2)}, u32[]{:S(2)}) collective-permute-start(bf16[128,1152]{1,0:T(8,128)(2,1)S(1)} %add_convert_fusion.11), channel_id=1, source_target_pairs={{0,8},{4,12},{8,16},{12,20},{16,24},{20,28},{24,0},{28,4},{1,9},{5... | collective-permute-start | bytes 884744 | tf_op jit(solution)/shard_map/ppermute | solution.py:479
  163.4 6.0 %collective-permute-done.43 = bf16[128,1152]{1,0:T(8,128)(2,1)S(1)} collective-permute-done((bf16[128,1152]{1,0:T(8,128)(2,1)S(1)}, bf16[128,1152]{1,0:T(8,128)(2,1)S(1)}, u32[]{:S(2)}, u32[]{:S(2)}) %collective-permute-start.43) | collective-permute-done | bytes 294944 | tf_op jit(solution)/shard_map/ppermute | solution.py:479
  171.3 4.9 %collective-permute-done.37 = bf16[128,2048]{1,0:T(8,128)(2,1)S(1)} collective-permute-done((bf16[128,2048]{1,0:T(8,128)(2,1)S(1)}, bf16[128,2048]{1,0:T(8,128)(2,1)S(1)}, u32[]{:S(2)}, u32[]{:S(2)}) %collective-permute-start.37) | collective-permute-done | bytes 524320 | tf_op jit(solution)/shard_map/ppermute | solution.py:463
  177.4 2.6 %place_mixed.1 = bf16[2,512,1024]{2,1,0:T(8,128)(2,1)} custom-call(s32[5]{0:T(128)S(1)} %stack.74.meta, s32[2,1,256]{2,1,0:T(1,128)S(1)} %broadcast_in_dim.14.pos_ref, bf16[2,512,1024]{2,1,0:T(8,128)(2,1)S(1)} %copy-done.3, bf16[256,1024]{1,0:T(8,128)(2,1)S(1)} %get-tuple-element.265.own_ref, bf16[256,1024]{1,0:T(8,128)(2,1)S(1)} %collective-permute-done.34.oth_ref), custom_call_target="tpu_custom_call" | custom-call | flops 536870912 | bytes 5244948 | tf_op jit(solution)/shard_map/place_mixed/pallas_call | solution.py:49
  182.2 6.6 %collective-permute-done.46.a1 = bf16[256,1152]{1,0:T(8,128)(2,1)S(1)} collective-permute-done((bf16[256,1152]{1,0:T(8,128)(2,1)S(1)}, bf16[256,1152]{1,0:T(8,128)(2,1)S(1)}, u32[]{:S(2)}, u32[]{:S(2)}) %collective-permute-start.46) | collective-permute-done | bytes 589856 | tf_op jit(solution)/shard_map/ppermute | solution.py:463
  188.9 2.4 %collective-permute-start.47 = (bf16[128,1152]{1,0:T(8,128)(2,1)S(1)}, bf16[128,1152]{1,0:T(8,128)(2,1)S(1)}, u32[]{:S(2)}, u32[]{:S(2)}) collective-permute-start(bf16[128,1152]{1,0:T(8,128)(2,1)S(1)} %add_convert_fusion.9), channel_id=1, source_target_pairs={{0,8},{4,12},{8,16},{12,20},{16,24},{20,28},{24,0},{28,4},{1,9},{5... | collective-permute-start | bytes 884744 | tf_op jit(solution)/shard_map/ppermute | solution.py:479
  191.3 2.6 %place_input_grad.1 = bf16[2,512,1024]{2,1,0:T(8,128)(2,1)} custom-call(s32[5]{0:T(128)S(1)} %stack.74.meta, s32[2,1,256]{2,1,0:T(1,128)S(1)} %broadcast_in_dim.14.pos_ref, bf16[2,512,1024]{2,1,0:T(8,128)(2,1)S(1)} %copy-done.4, bf16[256,1024]{1,0:T(8,128)(2,1)S(1)} %input_grad.1.own_ref, bf16[256,1024]{1,0:T(8,128)(2,1)S(1)} %collective-permute-done.35.oth_ref), custom_call_target="tpu_custom_call" | custom-call | flops 536870912 | bytes 5244948 | tf_op jit(solution)/shard_map/place_input_grad/pallas_call | solution.py:49
  193.9 4.5 %collective-permute-done.38.m1 = bf16[128,2048]{1,0:T(8,128)(2,1)S(1)} collective-permute-done((bf16[128,2048]{1,0:T(8,128)(2,1)S(1)}, bf16[128,2048]{1,0:T(8,128)(2,1)S(1)}, u32[]{:S(2)}, u32[]{:S(2)}) %collective-permute-start.38) | collective-permute-done | bytes 524320 | tf_op jit(solution)/shard_map/ppermute | solution.py:463
  202.0 2.0 collective-permute-start.49
  205.5 2.7 %collective-permute-done.49.c2 = bf16[32,1920]{1,0:T(8,128)(2,1)S(1)} collective-permute-done((bf16[32,1920]{1,0:T(8,128)(2,1)S(1)}, bf16[32,1920]{1,0:T(8,128)(2,1)S(1)}, u32[]{:S(2)}, u32[]{:S(2)}) %collective-permute-start.49) | collective-permute-done | bytes 122912 | tf_op jit(solution)/shard_map/ppermute | solution.py:463
  208.2 2.1 collective-permute-done.50.c3
  210.9 2.2 %final.1 = (f32[32,3072]{1,0:T(8,128)}, f32[32,4096]{1,0:T(8,128)}, f32[8,128]{1,0:T(8,128)S(1)}) custom-call(s32[5]{0:T(128)S(1)} %stack.74.meta, f32[32,1920]{1,0:T(8,128)S(1)} %get-tuple-element.312.c0, bf16[32,1920]{1,0:T(8,128)(2,1)} %copy-done.17, bf16[32,1920]{1,0:T(8,128)(2,1)} %copy-done.18, bf16[32,1920]{1,0:T(8,128)(2,1)} %copy-done.19), custom_call_target="tpu_custom_call" | custom-call | bytes 1536020 | tf_op jit(solution)/shard_map/final/pallas_call | solution.py:49
  (184 shorter events, 64.3 us)
Async XLA Ops:
  7.4 11.1 %collective-permute-start.4 = (bf16[256,1024]{1,0:T(8,128)(2,1)S(1)}, bf16[256,1024]{1,0:T(8,128)(2,1)S(1)}, u32[]{:S(2)}, u32[]{:S(2)}) collective-permute-start(bf16[256,1024]{1,0:T(8,128)(2,1)S(1)} %get-tuple-element.176), channel_id=1, source_target_pairs={{0,1},{1,0},{2,3},{3,2},{4,5},{5,4},{6,7},{7,6},{8,9},{9,8},{10,11... | collective-permute-start | bytes 1572872 | tf_op jit(solution)/shard_map/ppermute | solution.py:463
  18.7 11.6 %collective-permute-start.9 = (bf16[128,1152]{1,0:T(8,128)(2,1)S(1)}, bf16[128,1152]{1,0:T(8,128)(2,1)}, u32[]{:S(2)}, u32[]{:S(2)}) collective-permute-start(bf16[128,1152]{1,0:T(8,128)(2,1)S(1)} %get-tuple-element.182.refs_0_), channel_id=1, source_target_pairs={{0,8},{4,12},{8,16},{12,20},{16,24},{20,28},{24,0},{28,4},{1,9},{5... | collective-permute-start | bytes 884744 | tf_op jit(solution)/shard_map/ppermute | solution.py:479
  20.3 14.7 %collective-permute-start.10 = (bf16[128,2048]{1,0:T(8,128)(2,1)S(1)}, bf16[128,2048]{1,0:T(8,128)(2,1)S(1)}, u32[]{:S(2)}, u32[]{:S(2)}) collective-permute-start(bf16[128,2048]{1,0:T(8,128)(2,1)S(1)} %get-tuple-element.178.refs_0_), channel_id=1, source_target_pairs={{0,4},{4,0},{8,12},{12,8},{16,20},{20,16},{24,28},{28,24},{1,5},{5... | collective-permute-start | bytes 1572872 | tf_op jit(solution)/shard_map/ppermute | solution.py:463
  21.9 19.5 %collective-permute-start.5 = (bf16[256,1024]{1,0:T(8,128)(2,1)S(1)}, bf16[256,1024]{1,0:T(8,128)(2,1)S(1)}, u32[]{:S(2)}, u32[]{:S(2)}) collective-permute-start(bf16[256,1024]{1,0:T(8,128)(2,1)S(1)} %add_convert_fusion.8), channel_id=1, source_target_pairs={{0,2},{1,3},{2,0},{3,1},{4,6},{5,7},{6,4},{7,5},{8,10},{9,11},{10,... | collective-permute-start | bytes 1572872 | tf_op jit(solution)/shard_map/ppermute | solution.py:463
  30.3 11.4 %collective-permute-start.8 = (bf16[128,1152]{1,0:T(8,128)(2,1)S(1)}, bf16[128,1152]{1,0:T(8,128)(2,1)S(1)}, u32[]{:S(2)}, u32[]{:S(2)}) collective-permute-start(bf16[128,1152]{1,0:T(8,128)(2,1)S(1)} %get-tuple-element.182.refs_0_), channel_id=1, source_target_pairs={{0,4},{4,0},{8,12},{12,8},{16,20},{20,16},{24,28},{28,24},{1,5},{5... | collective-permute-start | bytes 884744 | tf_op jit(solution)/shard_map/ppermute | solution.py:463
  34.1 22.0 %collective-permute-start.19 = (bf16[256,1024]{1,0:T(8,128)(2,1)S(1)}, bf16[256,1024]{1,0:T(8,128)(2,1)S(1)}, u32[]{:S(2)}, u32[]{:S(2)}) collective-permute-start(bf16[256,1024]{1,0:T(8,128)(2,1)S(1)} %get-tuple-element.212), channel_id=1, source_target_pairs={{0,1},{1,0},{2,3},{3,2},{4,5},{5,4},{6,7},{7,6},{8,9},{9,8},{10,11... | collective-permute-start | bytes 1572872 | tf_op jit(solution)/shard_map/ppermute | solution.py:463
  35.1 12.3 %collective-permute-start.11 = (bf16[128,1152]{1,0:T(8,128)(2,1)}, bf16[128,1152]{1,0:T(8,128)(2,1)}, u32[]{:S(2)}, u32[]{:S(2)}) collective-permute-start(bf16[128,1152]{1,0:T(8,128)(2,1)} %collective-permute-done.9.refs_2_), channel_id=1, source_target_pairs={{0,4},{4,0},{8,12},{12,8},{16,20},{20,16},{24,28},{28,24},{1,5},{5... | collective-permute-start | bytes 884744 | tf_op jit(solution)/shard_map/ppermute | solution.py:463
  41.2 12.1 %collective-permute-start.14 = (bf16[128,1152]{1,0:T(8,128)(2,1)}, bf16[128,1152]{1,0:T(8,128)(2,1)}, u32[]{:S(2)}, u32[]{:S(2)}) collective-permute-start(bf16[128,1152]{1,0:T(8,128)(2,1)} %collective-permute-done.12.refs_4_), channel_id=1, source_target_pairs={{0,8},{4,12},{8,16},{12,20},{16,24},{20,28},{24,0},{28,4},{1,9},{5... | collective-permute-start | bytes 884744 | tf_op jit(solution)/shard_map/ppermute | solution.py:479
  41.4 21.1 %collective-permute-start.7 = (bf16[128,2048]{1,0:T(8,128)(2,1)S(1)}, bf16[128,2048]{1,0:T(8,128)(2,1)}, u32[]{:S(2)}, u32[]{:S(2)}) collective-permute-start(bf16[128,2048]{1,0:T(8,128)(2,1)S(1)} %get-tuple-element.178.refs_0_), channel_id=1, source_target_pairs={{0,8},{4,12},{8,16},{12,20},{16,24},{20,28},{24,0},{28,4},{1,9},{5... | collective-permute-start | bytes 1572872 | tf_op jit(solution)/shard_map/ppermute | solution.py:479
  41.8 22.0 %collective-permute-start.6 = (bf16[256,1024]{1,0:T(8,128)(2,1)S(1)}, bf16[256,1024]{1,0:T(8,128)(2,1)S(1)}, u32[]{:S(2)}, u32[]{:S(2)}) collective-permute-start(bf16[256,1024]{1,0:T(8,128)(2,1)S(1)} %add.96.xo_ref.x_ref), channel_id=1, source_target_pairs={{0,1},{1,0},{2,3},{3,2},{4,5},{5,4},{6,7},{7,6},{8,9},{9,8},{10,11... | collective-permute-start | bytes 1572872 | tf_op jit(solution)/shard_map/ppermute | solution.py:463
  47.3 15.1 %collective-permute-start.13 = (bf16[128,1152]{1,0:T(8,128)(2,1)}, bf16[128,1152]{1,0:T(8,128)(2,1)}, u32[]{:S(2)}, u32[]{:S(2)}) collective-permute-start(bf16[128,1152]{1,0:T(8,128)(2,1)} %collective-permute-done.12.refs_4_), channel_id=1, source_target_pairs={{0,4},{4,0},{8,12},{12,8},{16,20},{20,16},{24,28},{28,24},{1,5},{5... | collective-permute-start | bytes 884744 | tf_op jit(solution)/shard_map/ppermute | solution.py:463
  56.4 16.4 %collective-permute-start.20 = (bf16[256,1024]{1,0:T(8,128)(2,1)S(1)}, bf16[256,1024]{1,0:T(8,128)(2,1)S(1)}, u32[]{:S(2)}, u32[]{:S(2)}) collective-permute-start(bf16[256,1024]{1,0:T(8,128)(2,1)S(1)} %add_convert_fusion.6), channel_id=1, source_target_pairs={{0,2},{1,3},{2,0},{3,1},{4,6},{5,7},{6,4},{7,5},{8,10},{9,11},{10,... | collective-permute-start | bytes 1572872 | tf_op jit(solution)/shard_map/ppermute | solution.py:463
  62.5 13.9 %collective-permute-start.22 = (bf16[128,2048]{1,0:T(8,128)(2,1)}, bf16[128,2048]{1,0:T(8,128)(2,1)S(1)}, u32[]{:S(2)}, u32[]{:S(2)}) collective-permute-start(bf16[128,2048]{1,0:T(8,128)(2,1)} %collective-permute-done.7.refs_2_), channel_id=1, source_target_pairs={{0,8},{4,12},{8,16},{12,20},{16,24},{20,28},{24,0},{28,4},{1,9},{5... | collective-permute-start | bytes 1572872 | tf_op jit(solution)/shard_map/ppermute | solution.py:479
  62.5 15.0 %collective-permute-start.17 = (bf16[128,2048]{1,0:T(8,128)(2,1)}, bf16[128,2048]{1,0:T(8,128)(2,1)S(1)}, u32[]{:S(2)}, u32[]{:S(2)}) collective-permute-start(bf16[128,2048]{1,0:T(8,128)(2,1)} %collective-permute-done.7.refs_2_), channel_id=1, source_target_pairs={{0,4},{4,0},{8,12},{12,8},{16,20},{20,16},{24,28},{28,24},{1,5},{5... | collective-permute-start | bytes 1572872 | tf_op jit(solution)/shard_map/ppermute | solution.py:463
  73.0 17.5 %collective-permute-start.21 = (bf16[256,1024]{1,0:T(8,128)(2,1)S(1)}, bf16[256,1024]{1,0:T(8,128)(2,1)S(1)}, u32[]{:S(2)}, u32[]{:S(2)}) collective-permute-start(bf16[256,1024]{1,0:T(8,128)(2,1)S(1)} %add.99.co_ref.c_ref), channel_id=1, source_target_pairs={{0,1},{1,0},{2,3},{3,2},{4,5},{5,4},{6,7},{7,6},{8,9},{9,8},{10,11... | collective-permute-start | bytes 1572872 | tf_op jit(solution)/shard_map/ppermute | solution.py:463
  76.4 13.3 %collective-permute-start.25 = (bf16[128,2048]{1,0:T(8,128)(2,1)S(1)}, bf16[128,2048]{1,0:T(8,128)(2,1)S(1)}, u32[]{:S(2)}, u32[]{:S(2)}) collective-permute-start(bf16[128,2048]{1,0:T(8,128)(2,1)S(1)} %collective-permute-done.22.refs_4_), channel_id=1, source_target_pairs={{0,8},{4,12},{8,16},{12,20},{16,24},{20,28},{24,0},{28,4},{1,9},{5... | collective-permute-start | bytes 1572872 | tf_op jit(solution)/shard_map/ppermute | solution.py:479
  76.4 14.1 %collective-permute-start.23 = (bf16[128,2048]{1,0:T(8,128)(2,1)S(1)}, bf16[128,2048]{1,0:T(8,128)(2,1)S(1)}, u32[]{:S(2)}, u32[]{:S(2)}) collective-permute-start(bf16[128,2048]{1,0:T(8,128)(2,1)S(1)} %collective-permute-done.22.refs_4_), channel_id=1, source_target_pairs={{0,4},{4,0},{8,12},{12,8},{16,20},{20,16},{24,28},{28,24},{1,5},{5... | collective-permute-start | bytes 1572872 | tf_op jit(solution)/shard_map/ppermute | solution.py:463
  77.7 12.8 %collective-permute-start.18 = (bf16[256,1024]{1,0:T(8,128)(2,1)S(1)}, bf16[256,1024]{1,0:T(8,128)(2,1)S(1)}, u32[]{:S(2)}, u32[]{:S(2)}) collective-permute-start(bf16[256,1024]{1,0:T(8,128)(2,1)S(1)} %add_convert_fusion.7.t_ref.bt_ref.at_ref), channel_id=1, source_target_pairs={{0,2},{1,3},{2,0},{3,1},{4,6},{5,7},{6,4},{7,5},{8,10},{9,11},{10,... | collective-permute-start | bytes 1572872 | tf_op jit(solution)/shard_map/ppermute | solution.py:463
  111.9 14.0 %collective-permute-start.28 = (bf16[256,1024]{1,0:T(8,128)(2,1)S(1)}, bf16[256,1024]{1,0:T(8,128)(2,1)S(1)}, u32[]{:S(2)}, u32[]{:S(2)}) collective-permute-start(bf16[256,1024]{1,0:T(8,128)(2,1)S(1)} %add_convert_fusion.5.dt_ref), channel_id=1, source_target_pairs={{0,2},{1,3},{2,0},{3,1},{4,6},{5,7},{6,4},{7,5},{8,10},{9,11},{10,... | collective-permute-start | bytes 1572872 | tf_op jit(solution)/shard_map/ppermute | solution.py:463
  116.8 14.9 %collective-permute-start.36 = (bf16[128,2048]{1,0:T(8,128)(2,1)S(1)}, bf16[128,2048]{1,0:T(8,128)(2,1)S(1)}, u32[]{:S(2)}, u32[]{:S(2)}) collective-permute-start(bf16[128,2048]{1,0:T(8,128)(2,1)S(1)} %get-tuple-element.278), channel_id=1, source_target_pairs={{0,4},{4,0},{8,12},{12,8},{16,20},{20,16},{24,28},{28,24},{1,5},{5... | collective-permute-start | bytes 1572872 | tf_op jit(solution)/shard_map/ppermute | solution.py:463
  123.2 19.7 %collective-permute-start.39 = (bf16[128,2048]{1,0:T(8,128)(2,1)S(1)}, bf16[128,2048]{1,0:T(8,128)(2,1)S(1)}, u32[]{:S(2)}, u32[]{:S(2)}) collective-permute-start(bf16[128,2048]{1,0:T(8,128)(2,1)S(1)} %get-tuple-element.286), channel_id=1, source_target_pairs={{0,4},{4,0},{8,12},{12,8},{16,20},{20,16},{24,28},{28,24},{1,5},{5... | collective-permute-start | bytes 1572872 | tf_op jit(solution)/shard_map/ppermute | solution.py:463
  131.8 14.8 %collective-permute-start.40 = (bf16[128,2048]{1,0:T(8,128)(2,1)S(1)}, bf16[128,2048]{1,0:T(8,128)(2,1)S(1)}, u32[]{:S(2)}, u32[]{:S(2)}) collective-permute-start(bf16[128,2048]{1,0:T(8,128)(2,1)S(1)} %add_convert_fusion.2), channel_id=1, source_target_pairs={{0,8},{4,12},{8,16},{12,20},{16,24},{20,28},{24,0},{28,4},{1,9},{5... | collective-permute-start | bytes 1572872 | tf_op jit(solution)/shard_map/ppermute | solution.py:479
  132.8 13.7 %collective-permute-start.33 = (bf16[256,1024]{1,0:T(8,128)(2,1)S(1)}, bf16[256,1024]{1,0:T(8,128)(2,1)S(1)}, u32[]{:S(2)}, u32[]{:S(2)}) collective-permute-start(bf16[256,1024]{1,0:T(8,128)(2,1)S(1)} %add_convert_fusion.3.mt_ref), channel_id=1, source_target_pairs={{0,2},{1,3},{2,0},{3,1},{4,6},{5,7},{6,4},{7,5},{8,10},{9,11},{10,... | collective-permute-start | bytes 1572872 | tf_op jit(solution)/shard_map/ppermute | solution.py:463
  142.9 15.7 %collective-permute-start.42 = (bf16[256,1152]{1,0:T(8,128)(2,1)S(1)}, bf16[256,1152]{1,0:T(8,128)(2,1)S(1)}, u32[]{:S(2)}, u32[]{:S(2)}) collective-permute-start(bf16[256,1152]{1,0:T(8,128)(2,1)S(1)} %get-tuple-element.294), channel_id=1, source_target_pairs={{0,4},{4,0},{8,12},{12,8},{16,20},{20,16},{24,28},{28,24},{1,5},{5... | collective-permute-start | bytes 1769480 | tf_op jit(solution)/shard_map/ppermute | solution.py:463
  146.8 15.8 %collective-permute-start.41 = (bf16[128,2048]{1,0:T(8,128)(2,1)S(1)}, bf16[128,2048]{1,0:T(8,128)(2,1)S(1)}, u32[]{:S(2)}, u32[]{:S(2)}) collective-permute-start(bf16[128,2048]{1,0:T(8,128)(2,1)S(1)} %add_convert_fusion.1), channel_id=1, source_target_pairs={{0,8},{4,12},{8,16},{12,20},{16,24},{20,28},{24,0},{28,4},{1,9},{5... | collective-permute-start | bytes 1572872 | tf_op jit(solution)/shard_map/ppermute | solution.py:479
  147.8 14.7 %collective-permute-start.34 = (bf16[256,1024]{1,0:T(8,128)(2,1)S(1)}, bf16[256,1024]{1,0:T(8,128)(2,1)S(1)}, u32[]{:S(2)}, u32[]{:S(2)}) collective-permute-start(bf16[256,1024]{1,0:T(8,128)(2,1)S(1)} %get-tuple-element.265.own_ref), channel_id=1, source_target_pairs={{0,1},{1,0},{2,3},{3,2},{4,5},{5,4},{6,7},{7,6},{8,9},{9,8},{10,11... | collective-permute-start | bytes 1572872 | tf_op jit(solution)/shard_map/ppermute | solution.py:463
  148.1 14.5 %collective-permute-start.31 = (bf16[256,1024]{1,0:T(8,128)(2,1)S(1)}, bf16[256,1024]{1,0:T(8,128)(2,1)S(1)}, u32[]{:S(2)}, u32[]{:S(2)}) collective-permute-start(bf16[256,1024]{1,0:T(8,128)(2,1)S(1)} %add_convert_fusion.4.t_ref), channel_id=1, source_target_pairs={{0,2},{1,3},{2,0},{3,1},{4,6},{5,7},{6,4},{7,5},{8,10},{9,11},{10,... | collective-permute-start | bytes 1572872 | tf_op jit(solution)/shard_map/ppermute | solution.py:463
  161.3 14.9 %collective-permute-start.37 = (bf16[128,2048]{1,0:T(8,128)(2,1)S(1)}, bf16[128,2048]{1,0:T(8,128)(2,1)S(1)}, u32[]{:S(2)}, u32[]{:S(2)}) collective-permute-start(bf16[128,2048]{1,0:T(8,128)(2,1)S(1)} %get-tuple-element.281), channel_id=1, source_target_pairs={{0,4},{4,0},{8,12},{12,8},{16,20},{20,16},{24,28},{28,24},{1,5},{5... | collective-permute-start | bytes 1572872 | tf_op jit(solution)/shard_map/ppermute | solution.py:463
  163.3 16.7 %collective-permute-start.35 = (bf16[256,1024]{1,0:T(8,128)(2,1)S(1)}, bf16[256,1024]{1,0:T(8,128)(2,1)S(1)}, u32[]{:S(2)}, u32[]{:S(2)}) collective-permute-start(bf16[256,1024]{1,0:T(8,128)(2,1)S(1)} %input_grad.1.own_ref), channel_id=1, source_target_pairs={{0,1},{1,0},{2,3},{3,2},{4,5},{5,4},{6,7},{7,6},{8,9},{9,8},{10,11... | collective-permute-start | bytes 1572872 | tf_op jit(solution)/shard_map/ppermute | solution.py:463
  170.0 18.8 %collective-permute-start.46 = (bf16[256,1152]{1,0:T(8,128)(2,1)S(1)}, bf16[256,1152]{1,0:T(8,128)(2,1)S(1)}, u32[]{:S(2)}, u32[]{:S(2)}) collective-permute-start(bf16[256,1152]{1,0:T(8,128)(2,1)S(1)} %get-tuple-element.308), channel_id=1, source_target_pairs={{0,4},{4,0},{8,12},{12,8},{16,20},{20,16},{24,28},{28,24},{1,5},{5... | collective-permute-start | bytes 1769480 | tf_op jit(solution)/shard_map/ppermute | solution.py:463
  176.2 22.2 %collective-permute-start.38 = (bf16[128,2048]{1,0:T(8,128)(2,1)S(1)}, bf16[128,2048]{1,0:T(8,128)(2,1)S(1)}, u32[]{:S(2)}, u32[]{:S(2)}) collective-permute-start(bf16[128,2048]{1,0:T(8,128)(2,1)S(1)} %get-tuple-element.284), channel_id=1, source_target_pairs={{0,4},{4,0},{8,12},{12,8},{16,20},{20,16},{24,28},{28,24},{1,5},{5... | collective-permute-start | bytes 1572872 | tf_op jit(solution)/shard_map/ppermute | solution.py:463
  180.3 19.2 %collective-permute-start.45 = (bf16[128,2048]{1,0:T(8,128)(2,1)S(1)}, bf16[128,2048]{1,0:T(8,128)(2,1)S(1)}, u32[]{:S(2)}, u32[]{:S(2)}) collective-permute-start(bf16[128,2048]{1,0:T(8,128)(2,1)S(1)} %add_convert_fusion), channel_id=1, source_target_pairs={{0,8},{4,12},{8,16},{12,20},{16,24},{20,28},{24,0},{28,4},{1,9},{5... | collective-permute-start | bytes 1572872 | tf_op jit(solution)/shard_map/ppermute | solution.py:479
  (50 other events, 466.3 us)
